TPU v7x, 32 devices: a whole 2x2x4 slice. The times are simulated.
32 devices in a mesh: groups: 2 (over y), slab: 4 (over z), pair: 4 (over x, core).
Axes of the slice: x: 2, y: 2, z: 4, core: 2. Of those that a mesh axis runs over, the one named last changes fastest.
Arguments:
- occupancy: float32 [8, 128, 256, 128], P(('groups', 'pair'), 'slab'), parts along dimension 0, may hold values from 0 to 1
- classes: int32 [8, 128, 256, 128], P(('groups', 'pair'), 'slab'), parts along dimension 0, may hold values from 0 to 7
- conductance: float32 [8], replicated, may hold values from 0.1 to 1
- damping: float32 [8], P('groups'), parts along dimension 0, may hold values from 1 to 8
- matches: int32 [8], P('groups'), parts along dimension 0, may hold values from 0 to 3, each once
Outputs:
- correlation: float32 [8, 128, 256, 128], P(('groups', 'pair'), 'slab'), parts along dimension 0
There are 2 independent parts, one for each index of `groups`. A program takes and returns all parts, laid end to end along the dimension named above; an argument that names none is the same for every part. Nothing has to cross between parts.
Inputs may be any that keep to these rules, and one draw needn't show every extreme that they name: A permutation of the 4 submaps; submap s is registered against submap matches[s]. `classes`: a row of the conductance table.
All inputs are finite; a program needn't handle non-finite values.
Results may differ from a plain program's by a relative error of at most 0.0003.
Values sent between devices are 32-bit elements; how exact they have to be, the bound alone decides.
No kernel may reach another device: no remote copies, remote signals or barrier semaphores. Data moves between devices by JAX's collectives and lax.ppermute only.
A program may use at most 128 MiB of HBM per device.

v0:
```python
import math

import jax
import jax.numpy as jnp
from jax import lax
from jax.sharding import PartitionSpec as P

X = 256
STEPS = 4


STEP_SIZE = 1.0 / 6.0
FLOOR_VALUE = 0.01
FORMS = {1: "bjxy,jk->bkxy", 2: "bzjy,jk->bzky", 3: "bzxj,jk->bzxk"}


def with_halo(shard, sides, width):
    for axis, dim in sides:
        size, length = (lax.axis_size(axis), shard.shape[dim])
        up = [(i, (i + 1) % size) for i in range(size - 1)]
        down = [(j, i) for i, j in up]
        last = lax.slice_in_dim(shard, length - width, length, axis=dim)
        leading = lax.slice_in_dim(shard, 0, width, axis=dim)
        before = lax.ppermute(last, axis, up)
        after = lax.ppermute(leading, axis, down)
        shard = jnp.concatenate([before, shard, after], axis=dim)
    return shard


def tables(length):
    counter = jnp.arange(length, dtype=jnp.int32)
    product = counter[:, None] * counter[None, :] % length
    angles = product.astype(jnp.float32) * (2.0 * math.pi / length)
    factor = 1.0 / math.sqrt(length)
    return (jnp.cos(angles) * factor, jnp.sin(angles) * factor)


def multiply_along(values, matrix, axis_dim):
    return jnp.einsum(FORMS[axis_dim], values, matrix, precision=lax.Precision.HIGHEST)


def forward_real(values, axis_dim):
    cosine, sine_table = tables(values.shape[axis_dim])
    return (multiply_along(values, cosine, axis_dim), -multiply_along(values, sine_table, axis_dim))


def forward_complex(real_part, imag_part, axis_dim):
    cosine, sine_table = tables(real_part.shape[axis_dim])
    return (
        multiply_along(real_part, cosine, axis_dim)
        + multiply_along(imag_part, sine_table, axis_dim),
        multiply_along(imag_part, cosine, axis_dim)
        - multiply_along(real_part, sine_table, axis_dim),
    )


def inverse_complex(real_part, imag_part, axis_dim):
    cosine, sine_table = tables(real_part.shape[axis_dim])
    return (
        multiply_along(real_part, cosine, axis_dim)
        - multiply_along(imag_part, sine_table, axis_dim),
        multiply_along(imag_part, cosine, axis_dim)
        + multiply_along(real_part, sine_table, axis_dim),
    )


def inverse_real(real_part, imag_part, axis_dim):
    cosine, sine_table = tables(real_part.shape[axis_dim])
    return multiply_along(real_part, cosine, axis_dim) - multiply_along(
        imag_part, sine_table, axis_dim
    )


def local_neighbours(padded):
    widened = jnp.pad(padded, ((0, 0), (0, 0), (1, 1), (1, 1)))
    return [
        widened[:, 2:, 1:-1, 1:-1],
        widened[:, :-2, 1:-1, 1:-1],
        widened[:, 1:-1, 2:, 1:-1],
        widened[:, 1:-1, :-2, 1:-1],
        widened[:, 1:-1, 1:-1, 2:],
        widened[:, 1:-1, 1:-1, :-2],
    ]


def signed_frequency(counter, length):
    return jnp.where(counter < length // 2, counter, counter - length).astype(jnp.float32) / length


def cross_power(own_real, own_imag, far_real, far_imag, decay_rate, offset):
    depth_count = own_real.shape[1]
    row_count = own_real.shape[2]
    width_count = own_real.shape[3]
    along_depth = signed_frequency(jnp.arange(depth_count, dtype=jnp.int32), depth_count)
    along_rows = signed_frequency(offset + jnp.arange(row_count, dtype=jnp.int32), X)
    along_width = signed_frequency(jnp.arange(width_count, dtype=jnp.int32), width_count)
    radius = (
        along_depth[:, None, None] ** 2
        + along_rows[None, :, None] ** 2
        + along_width[None, None, :] ** 2
    )
    cross_real = own_real * far_real + own_imag * far_imag
    cross_imag = own_imag * far_real - own_real * far_imag
    magnitude = jnp.sqrt((own_real**2 + own_imag**2) * (far_real**2 + far_imag**2) + FLOOR_VALUE**2)
    weight = jnp.exp(-decay_rate[:, None, None, None] * radius[None]) / magnitude
    return (cross_real * weight, cross_imag * weight)


def local(occupancy, classes, conductance, damping, matches):
    conduct = jnp.zeros(occupancy.shape, jnp.float32)
    for class_id in range(conductance.shape[0]):
        conduct = jnp.where(classes == class_id, conductance[class_id], conduct)
    outer_rims = local_neighbours(with_halo(conduct, (("slab", 1),), 1))
    volume = occupancy
    for sweep_index in range(STEPS):
        beside_all = local_neighbours(with_halo(volume, (("slab", 1),), 1))
        change = jnp.zeros_like(volume)
        for other_field, other_conduct in zip(beside_all, outer_rims):
            change = change + 0.5 * (conduct + other_conduct) * (other_field - volume)
        volume = volume + STEP_SIZE * change
    real_part, imag_part = forward_real(volume, 3)
    real_part, imag_part = forward_complex(real_part, imag_part, 2)
    real_part, imag_part = (
        lax.all_to_all(
            lax.all_to_all(real_part, "pair", split_axis=2, concat_axis=0, tiled=True),
            "slab",
            split_axis=2,
            concat_axis=1,
            tiled=True,
        ),
        lax.all_to_all(
            lax.all_to_all(imag_part, "pair", split_axis=2, concat_axis=0, tiled=True),
            "slab",
            split_axis=2,
            concat_axis=1,
            tiled=True,
        ),
    )
    real_part, imag_part = forward_complex(real_part, imag_part, 1)
    far_real = jnp.take(real_part, matches, axis=0)
    far_imag = jnp.take(imag_part, matches, axis=0)
    offset = (
        lax.axis_index("pair") * lax.axis_size("slab") + lax.axis_index("slab")
    ) * real_part.shape[2]
    cross_real, cross_imag = cross_power(real_part, imag_part, far_real, far_imag, damping, offset)
    cross_real, cross_imag = inverse_complex(cross_real, cross_imag, 1)
    back_real, back_imag = (
        lax.all_to_all(
            lax.all_to_all(cross_real, "slab", split_axis=1, concat_axis=2, tiled=True),
            "pair",
            split_axis=0,
            concat_axis=2,
            tiled=True,
        ),
        lax.all_to_all(
            lax.all_to_all(cross_imag, "slab", split_axis=1, concat_axis=2, tiled=True),
            "pair",
            split_axis=0,
            concat_axis=2,
            tiled=True,
        ),
    )
    back_real, back_imag = inverse_complex(back_real, back_imag, 2)
    return inverse_real(back_real, back_imag, 3)


def solution(mesh):
    in_specs = (
        P(("groups", "pair"), "slab", None, None),
        P(("groups", "pair"), "slab", None, None),
        P(),
        P("groups"),
        P("groups"),
    )
    out_specs = P(("groups", "pair"), "slab", None, None)
    return jax.shard_map(local, mesh=mesh, in_specs=in_specs, out_specs=out_specs, check_vma=False)
```

profile of v0, /device:TPU:11, one launch (start us, length us, event | category | flops | bytes accessed | tf_op | source)
XLA Modules:
  0.0 884.1 jit_solution(9573891897190911826)
XLA Ops:
  1.6 9.0 %select_select_fusion = f32[1,32,256,128]{3,2,1,0:T(8,128)S(1)} fusion(s32[1,32,256,128]{3,2,1,0:T(8,128)} %param.8, f32[]{:T(128)} %bitcast.10, f32[]{:T(128)} %bitcast.9, f32[]{:T(128)} %bitcast.8, f32[]{:T(128)} %bitcast.7, f32[]{:T(128)} %bitcast.6, f32[]{:T(128)} %bitcast.5, f32[]{:T(128)} %bitcast.4, f32[]{:T(128)} %bitcast.3), kind=kLoop, calls=%fused_computation.138 | loop fusion | flops 16777216 | bytes 8388640 | tf_op jit(solution)/shard_map/jit(_where)/select_n | solution.py:112
  25.7 6.3 select_maximum_fusion.6
  32.1 25.3 %fusion.52 = f32[1,32,256,128]{3,2,1,0:T(8,128)} fusion(f32[1,32,256,128]{3,2,1,0:T(8,128)} %param.7, f32[1,34,258,130]{3,2,1,0:T(8,128)} %select_maximum_fusion.6, f32[1,1,256,128]{3,2,1,0:T(8,128)S(1)} %collective-permute-done.3, f32[1,1,256,128]{3,2,1,0:T(8,128)S(1)} %collective-permute-done.1, f32[1,32,256,128]{3,2,1,0:T(8,128)} %copy-done, ...), kind=kLoop, calls=%fused_computation.87 | loop fusion | flops 36700160 | bytes 46661632 | tf_op jit(solution)/shard_map/add | solution.py:120
  66.5 8.3 select_maximum_fusion.4
  74.8 25.2 %fusion.37 = f32[1,32,256,128]{3,2,1,0:T(8,128)} fusion(f32[1,32,256,128]{3,2,1,0:T(8,128)} %fusion.52, f32[1,34,258,130]{3,2,1,0:T(8,128)} %select_maximum_fusion.4, f32[1,1,256,128]{3,2,1,0:T(8,128)S(1)} %collective-permute-done.5, f32[1,1,256,128]{3,2,1,0:T(8,128)S(1)} %collective-permute-done.4, f32[1,32,256,128]{3,2,1,0:T(8,128)} %copy-done, ...), kind=kLoop, calls=%fused_computation.66 | loop fusion | flops 36700160 | bytes 46661632 | tf_op jit(solution)/shard_map/add | solution.py:120
  108.7 8.3 select_maximum_fusion.2
  117.0 25.5 %fusion.22 = f32[1,32,256,128]{3,2,1,0:T(8,128)} fusion(f32[1,32,256,128]{3,2,1,0:T(8,128)} %fusion.37, f32[1,34,258,130]{3,2,1,0:T(8,128)} %select_maximum_fusion.2, f32[1,1,256,128]{3,2,1,0:T(8,128)S(1)} %collective-permute-done.7, f32[1,1,256,128]{3,2,1,0:T(8,128)S(1)} %collective-permute-done.6, f32[1,32,256,128]{3,2,1,0:T(8,128)} %copy-done, ...), kind=kLoop, calls=%fused_computation.45 | loop fusion | flops 36700160 | bytes 46661632 | tf_op jit(solution)/shard_map/add | solution.py:120
  151.1 8.3 select_maximum_fusion
  159.4 25.2 %fusion.7 = f32[32,256,128]{2,1,0:T(8,128)} fusion(f32[1,32,256,128]{3,2,1,0:T(8,128)} %fusion.22, f32[1,34,258,130]{3,2,1,0:T(8,128)} %select_maximum_fusion, f32[1,1,256,128]{3,2,1,0:T(8,128)S(1)} %collective-permute-done.9, f32[1,1,256,128]{3,2,1,0:T(8,128)S(1)} %collective-permute-done.8, f32[1,32,256,128]{3,2,1,0:T(8,128)} %copy-done, ...), kind=kLoop, calls=%fused_computation.24 | loop fusion | flops 36700160 | bytes 46661632 | tf_op jit(solution)/shard_map/reshape.1
  184.7 6.3 fusion.136
  194.7 4.8 fusion.104
  199.5 4.9 add_bitcast_fusion.2
  204.4 4.5 copy.48
  208.9 9.8 %all-to-all-start = ((f32[1,32,256,128]{3,1,0,2:T(8,128)}), f32[1,32,256,128]{3,1,0,2:T(8,128)}, u32[]{:S(2)}, u32[]{:S(2)}) async-start(f32[1,32,256,128]{3,1,0,2:T(8,128)} %copy.48), calls=%async_computation | async-start | bytes 8388608 | tf_op jit(solution)/shard_map/all_to_all | solution.py:125
  218.6 7.5 fusion.96
  226.2 4.7 subtract_bitcast_fusion.3
  235.3 29.7 %all-to-all-done = f32[1,32,256,128]{3,1,0,2:T(8,128)} async-done(((f32[1,32,256,128]{3,1,0,2:T(8,128)}), f32[1,32,256,128]{3,1,0,2:T(8,128)}, u32[]{:S(2)}, u32[]{:S(2)}) %all-to-all-start) | async-done | bytes 4194336 | tf_op jit(solution)/shard_map/all_to_all | solution.py:125
  265.0 6.9 all-to-all-start.2
  271.9 8.2 copy.91
  280.1 38.2 %all-to-all-done.2 = f32[1,32,256,128]{3,1,0,2:T(8,128)} async-done(((f32[1,32,256,128]{3,1,0,2:T(8,128)}), f32[1,32,256,128]{3,1,0,2:T(8,128)}, u32[]{:S(2)}, u32[]{:S(2)}) %all-to-all-start.2) | async-done | bytes 4194336 | tf_op jit(solution)/shard_map/all_to_all | solution.py:132
  318.3 5.6 all-to-all-start.1
  323.9 8.1 copy.90
  332.0 81.2 %all-to-all-done.1 = f32[4,32,64,128]{3,0,1,2:T(4,128)} async-done(((f32[4,32,64,128]{3,0,1,2:T(4,128)}), f32[4,32,64,128]{3,0,1,2:T(4,128)}, u32[]{:S(2)}, u32[]{:S(2)}) %all-to-all-start.1) | async-done | bytes 4194336 | tf_op jit(solution)/shard_map/all_to_all | solution.py:124
  413.3 8.6 all-to-all-start.3
  427.1 5.7 fusion.142
  432.8 77.5 %all-to-all-done.3 = f32[4,32,64,128]{3,0,1,2:T(4,128)} async-done(((f32[4,32,64,128]{3,0,1,2:T(4,128)}), f32[4,32,64,128]{3,0,1,2:T(4,128)}, u32[]{:S(2)}, u32[]{:S(2)}) %all-to-all-start.3) | async-done | bytes 4194336 | tf_op jit(solution)/shard_map/all_to_all | solution.py:131
  517.2 5.7 add_bitcast_fusion.1
  523.0 5.8 subtract_bitcast_fusion.2
  528.8 5.1 gather_fusion
  533.8 5.0 gather_fusion.1
  538.8 7.5 fusion.78
  554.6 4.5 copy.60
  559.1 9.5 %all-to-all-start.4 = ((f32[4,128,16,128]{3,2,0,1:T(8,128)}), f32[4,128,16,128]{3,2,0,1:T(8,128)}, u32[]{:S(2)}, u32[]{:S(2)}) async-start(f32[4,128,16,128]{3,2,0,1:T(8,128)} %copy.60), calls=%async_computation.4 | async-start | bytes 8388608 | tf_op jit(solution)/shard_map/all_to_all | solution.py:149
  568.6 6.1 fusion.138
  583.2 74.2 %all-to-all-done.4 = f32[4,128,16,128]{3,2,0,1:T(8,128)} async-done(((f32[4,128,16,128]{3,2,0,1:T(8,128)}), f32[4,128,16,128]{3,2,0,1:T(8,128)}, u32[]{:S(2)}, u32[]{:S(2)}) %all-to-all-start.4) | async-done | bytes 4194336 | tf_op jit(solution)/shard_map/all_to_all | solution.py:149
  657.4 8.8 all-to-all-start.6
  666.2 4.9 copy.62
  671.1 84.0 %all-to-all-done.6 = f32[4,128,16,128]{3,2,0,1:T(8,128)} async-done(((f32[4,128,16,128]{3,2,0,1:T(8,128)}), f32[4,128,16,128]{3,2,0,1:T(8,128)}, u32[]{:S(2)}, u32[]{:S(2)}) %all-to-all-start.6) | async-done | bytes 4194336 | tf_op jit(solution)/shard_map/all_to_all | solution.py:156
  755.0 8.0 all-to-all-start.5
  763.0 4.8 copy.68
  767.9 41.5 %all-to-all-done.5 = f32[4,32,64,128]{3,2,1,0:T(8,128)} async-done(((f32[4,32,64,128]{3,2,1,0:T(8,128)}), f32[4,32,64,128]{3,2,1,0:T(8,128)}, u32[]{:S(2)}, u32[]{:S(2)}) %all-to-all-start.5) | async-done | bytes 4194336 | tf_op jit(solution)/shard_map/all_to_all | solution.py:148
  809.4 6.7 all-to-all-start.7
  818.6 7.1 fusion.92
  825.7 7.3 fusion.101
  833.0 29.4 %all-to-all-done.7 = f32[4,32,64,128]{3,2,1,0:T(8,128)} async-done(((f32[4,32,64,128]{3,2,1,0:T(8,128)}), f32[4,32,64,128]{3,2,1,0:T(8,128)}, u32[]{:S(2)}, u32[]{:S(2)}) %all-to-all-start.7) | async-done | bytes 4194336 | tf_op jit(solution)/shard_map/all_to_all | solution.py:155
  865.0 4.8 fusion.99
  869.8 4.8 fusion.94
  878.5 5.4 subtract_bitcast_fusion
  (79 shorter events, 88.7 us)
Async XLA Ops:
  1.6 14.3 %copy-start.10 = (f32[1,32,256,128]{3,2,1,0:T(8,128)S(1)}, f32[1,32,256,128]{3,2,1,0:T(8,128)}, u32[]{:S(2)}) copy-start(f32[1,32,256,128]{3,2,1,0:T(8,128)} %param.7) | copy-start | bytes 12582916
  10.6 15.1 %copy-start = (f32[1,32,256,128]{3,2,1,0:T(8,128)}, f32[1,32,256,128]{3,2,1,0:T(8,128)S(1)}, u32[]{:S(2)}) copy-start(f32[1,32,256,128]{3,2,1,0:T(8,128)S(1)} %select_select_fusion) | copy-start | bytes 12582916
  10.7 10.6 %collective-permute-start = (f32[1,1,256,128]{3,2,1,0:T(8,128)S(1)}, f32[1,1,256,128]{3,2,1,0:T(8,128)S(1)}, u32[]{:S(2)}, u32[]{:S(2)}) collective-permute-start(f32[1,1,256,128]{3,2,1,0:T(8,128)S(1)} %get-tuple-element.15), channel_id=1, source_target_pairs={{4,0},{8,4},{12,8},{5,1},{9,5},{13,9},{6,2},{10,6},{14,10},{7,3},{... | collective-permute-start | bytes 393224 | tf_op jit(solution)/shard_map/ppermute | solution.py:25
  12.8 8.6 collective-permute-start.2
  16.0 9.7 %collective-permute-start.1 = (f32[1,1,256,128]{3,2,1,0:T(8,128)S(1)}, f32[1,1,256,128]{3,2,1,0:T(8,128)S(1)}, u32[]{:S(2)}, u32[]{:S(2)}) collective-permute-start(f32[1,1,256,128]{3,2,1,0:T(8,128)S(1)} %get-tuple-element.17), channel_id=1, source_target_pairs={{4,0},{8,4},{12,8},{5,1},{9,5},{13,9},{6,2},{10,6},{14,10},{7,3},{... | collective-permute-start | bytes 393224 | tf_op jit(solution)/shard_map/ppermute | solution.py:25
  18.1 7.6 collective-permute-start.3
  58.4 5.7 collective-permute-start.4
  60.5 6.0 collective-permute-start.5
  101.0 5.7 collective-permute-start.6
  103.0 5.7 collective-permute-start.7
  143.5 6.0 collective-permute-start.8
  145.4 5.7 collective-permute-start.9
  184.7 6.3 copy-start.8
  191.0 3.7 copy-start.9
  194.7 4.8 copy-start.4
  208.9 56.2 %all-to-all-start = ((f32[1,32,256,128]{3,1,0,2:T(8,128)}), f32[1,32,256,128]{3,1,0,2:T(8,128)}, u32[]{:S(2)}, u32[]{:S(2)}) async-start(f32[1,32,256,128]{3,1,0,2:T(8,128)} %copy.48), calls=%async_computation | async-start | bytes 8388608 | tf_op jit(solution)/shard_map/all_to_all | solution.py:125
  218.6 7.5 copy-start.5
  265.0 53.3 %all-to-all-start.2 = ((f32[1,32,256,128]{3,1,0,2:T(8,128)}), f32[1,32,256,128]{3,1,0,2:T(8,128)}, u32[]{:S(2)}, u32[]{:S(2)}) async-start(f32[1,32,256,128]{3,1,0,2:T(8,128)} %copy.52), calls=%async_computation.2 | async-start | bytes 8388608 | tf_op jit(solution)/shard_map/all_to_all | solution.py:132
  318.3 95.0 %all-to-all-start.1 = ((f32[4,32,64,128]{3,0,1,2:T(4,128)}), f32[4,32,64,128]{3,0,1,2:T(4,128)}, u32[]{:S(2)}, u32[]{:S(2)}) async-start(f32[4,32,64,128]{3,0,1,2:T(4,128)} %bitcast.158), calls=%async_computation.1 | async-start | bytes 8388608 | tf_op jit(solution)/shard_map/all_to_all | solution.py:124
  413.3 8.6 copy-start.14
  413.3 8.6 copy-start.15
  413.3 97.1 %all-to-all-start.3 = ((f32[4,32,64,128]{3,0,1,2:T(4,128)}), f32[4,32,64,128]{3,0,1,2:T(4,128)}, u32[]{:S(2)}, u32[]{:S(2)}) async-start(f32[4,32,64,128]{3,0,1,2:T(4,128)} %bitcast.156), calls=%async_computation.3 | async-start | bytes 8388608 | tf_op jit(solution)/shard_map/all_to_all | solution.py:131
  425.1 2.0 copy-start.6
  513.1 4.1 copy-start.12
  517.2 5.8 copy-start.7
  546.3 4.1 copy-start.1
  546.3 4.1 copy-start.3
  559.1 98.3 %all-to-all-start.4 = ((f32[4,128,16,128]{3,2,0,1:T(8,128)}), f32[4,128,16,128]{3,2,0,1:T(8,128)}, u32[]{:S(2)}, u32[]{:S(2)}) async-start(f32[4,128,16,128]{3,2,0,1:T(8,128)} %copy.60), calls=%async_computation.4 | async-start | bytes 8388608 | tf_op jit(solution)/shard_map/all_to_all | solution.py:149
  568.6 6.1 copy-start.2
  657.4 97.7 %all-to-all-start.6 = ((f32[4,128,16,128]{3,2,0,1:T(8,128)}), f32[4,128,16,128]{3,2,0,1:T(8,128)}, u32[]{:S(2)}, u32[]{:S(2)}) async-start(f32[4,128,16,128]{3,2,0,1:T(8,128)} %copy.66), calls=%async_computation.6 | async-start | bytes 8388608 | tf_op jit(solution)/shard_map/all_to_all | solution.py:156
  755.0 54.4 %all-to-all-start.5 = ((f32[4,32,64,128]{3,2,1,0:T(8,128)}), f32[4,32,64,128]{3,2,1,0:T(8,128)}, u32[]{:S(2)}, u32[]{:S(2)}) async-start(f32[4,32,64,128]{3,2,1,0:T(8,128)} %bitcast.159), calls=%async_computation.5 | async-start | bytes 8388608 | tf_op jit(solution)/shard_map/all_to_all | solution.py:148
  809.4 53.1 %all-to-all-start.7 = ((f32[4,32,64,128]{3,2,1,0:T(8,128)}), f32[4,32,64,128]{3,2,1,0:T(8,128)}, u32[]{:S(2)}, u32[]{:S(2)}) async-start(f32[4,32,64,128]{3,2,1,0:T(8,128)} %bitcast.157), calls=%async_computation.7 | async-start | bytes 8388608 | tf_op jit(solution)/shard_map/all_to_all | solution.py:155
  869.8 4.8 copy-start.11
  874.6 3.9 copy-start.13
where the time goes:
time: 899 us; the launch traced here: 884 us
  waiting for transfers between devices  463 us (52%)
  other arithmetic  154 us (17%)
  matrix products  105 us (12%)
  starting transfers between devices  90.7 us (10%)
  local copies, waits for them, and re-layouts  71.1 us (8%)
    dot_general x20, matrix products, multiply_along(): jnp.einsum(FORMS[axis_dim], values, matrix, precision=lax.Precision.HIGHEST)  105 us
    all_to_all x1, waiting for transfers between devices, local(): lax.all_to_all(cross_imag, 'slab', split_axis=1, concat_axis=2, tiled=True)  84 us
    all_to_all x1, waiting for transfers between devices, local(): lax.all_to_all(lax.all_to_all(real_part, 'pair', split_axis=2, concat_axi...  81.2 us
    all_to_all x1, waiting for transfers between devices, local(): lax.all_to_all(lax.all_to_all(imag_part, 'pair', split_axis=2, concat_axi...  77.5 us
    add x3, other arithmetic, local(): volume = volume + STEP_SIZE * change  76 us
    all_to_all x1, waiting for transfers between devices, local(): lax.all_to_all(cross_real, 'slab', split_axis=1, concat_axis=2, tiled=True)  74.2 us
    all_to_all x1, waiting for transfers between devices, local(): lax.all_to_all(lax.all_to_all(cross_real, 'slab', split_axis=1, concat_ax...  41.5 us
    all_to_all x1, waiting for transfers between devices, local(): lax.all_to_all(imag_part, 'pair', split_axis=2, concat_axis=0, tiled=True)  38.2 us
  transfers between devices with their start and end apart: 18, of which 14 were waited for; matrix products, arithmetic and copies ran while one was open for 10% of the time, Pallas kernels for 0%

commit v1 on v0

v1 whole, which is shorter than its diff:
```python
import functools
import math

import jax
import jax.numpy as jnp
import ml_dtypes
import numpy as np
from jax import lax
from jax.experimental import pallas as pl
from jax.experimental.pallas import tpu as pltpu
from jax.sharding import PartitionSpec as P

STEPS = 4
STEP_SIZE = 1.0 / 6.0
FLOOR_VALUE = 0.01
AXES = ("slab", "pair")
PAD = 8
VMEM_BYTES = 60 * 1024 * 1024
BF = jnp.bfloat16
F32 = jnp.float32


def split_table(table):
    high = table.astype(ml_dtypes.bfloat16)
    low = (table - high.astype(np.float64)).astype(ml_dtypes.bfloat16)
    return high, low


def trig(rows, columns, length):
    angles = (np.asarray(rows)[:, None] * np.asarray(columns)[None, :] % length) * (2.0 * math.pi / length)
    factor = 1.0 / math.sqrt(length)
    return np.cos(angles) * factor, np.sin(angles) * factor


def left_table(table):
    high, low = split_table(table)
    return np.concatenate([high, high, low], axis=1)


def right_table(table):
    high, low = split_table(table)
    top = np.concatenate([high, low], axis=1)
    return np.concatenate([top, np.concatenate([high, np.zeros_like(low)], axis=1)], axis=0)


def half_forward(length):
    half = length // 2
    cosine, sine = trig(np.arange(length), np.arange(half + 1), length)
    return np.concatenate([cosine[:, :half], cosine[:, half:], -sine[:, 1:half]], axis=1)


def half_inverse(length):
    half = length // 2
    cosine, sine = trig(np.arange(half + 1), np.arange(length), length)
    return np.concatenate(
        [cosine[:1], 2 * cosine[1:half], cosine[half:], -2 * sine[1:half]], axis=0
    )


def first_column_masks(rows, length, lanes):
    half = lanes // 2
    lower = (rows > 0) & (rows < length // 2)
    upper = rows > length // 2
    sign = np.where(np.arange(lanes) < half, 1.0, -1.0)
    take_cosine = np.ones((rows.size, lanes))
    take_sine = np.ones((rows.size, lanes)) * sign
    take_sine[lower, 0] = 0
    take_cosine[lower, half] = 0
    take_cosine[upper, 0] = 0
    take_sine[upper, half] = 0
    weight = np.ones((rows.size, lanes))
    weight[lower, 0] = 2
    weight[lower, half] = 0
    weight[upper, 0] = 0
    weight[upper, half] = 2
    return take_cosine.astype(np.float32), take_sine.astype(np.float32), weight.astype(np.float32)


def split(values):
    high = values.astype(BF)
    return high, (values - high.astype(F32)).astype(BF)


def dot(a, b):
    return jnp.dot(a, b, preferred_element_type=F32)


def along_lanes(values, table):
    high, low = split(values)
    both = dot(jnp.concatenate([high, low], axis=1), table)
    lanes = values.shape[1]
    return both[:, :lanes] + both[:, lanes:]


def forward_kernel(steps, chunks, depth, *refs):
    if steps:
        occ, cls, below, above, edge, conductance = refs[:6]
        refs = refs[6:]
    else:
        occ = refs[0]
        refs = refs[1:]
    table_y, table_x, take_cosine, take_sine = refs[:4]
    outs = refs[4 : 4 + chunks]
    scratch = refs[4 + chunks :]
    length, lanes = occ.shape[1:]
    rows = length // chunks
    if steps:
        first, second, centre, along_x, along_y, along_z = scratch
        total = depth + 2 * steps
        lane = lax.broadcasted_iota(jnp.int32, (length, lanes), 1)
        zeros = jnp.zeros((PAD, lanes), F32)
        inside = pl.ds(PAD, length)
        kappa = second

        def fill(z, ids, field):
            value = jnp.zeros((length, lanes), F32)
            for index in range(conductance.shape[0]):
                value = jnp.where(ids == index, conductance[index] * (0.5 * STEP_SIZE), value)
            kappa[z, inside, :] = value
            first[z, inside, :] = field

        def clear(z, carry):
            for ref in (first, second, along_x):
                ref[z, pl.ds(0, PAD), :] = zeros
                ref[z, pl.ds(PAD + length, PAD), :] = zeros
            return carry

        lax.fori_loop(0, total, clear, 0)

        def own(z, carry):
            fill(z + steps, cls[z], occ[z])
            return carry

        lax.fori_loop(0, depth, own, 0)

        def outer(z, carry):
            for ref, start, flag in ((below, 0, 0), (above, steps + depth, 1)):
                fill(start + z, ref[steps + z].astype(jnp.int32), ref[z])

                @pl.when(edge[flag] == 0)
                def _():
                    kappa[start + z, inside, :] = jnp.zeros((length, lanes), F32)

            return carry

        lax.fori_loop(0, steps, outer, 0)

        block = 64

        def coefficients(z, carry):
            for x in range(0, length, block):
                here = kappa[z, pl.ds(PAD + x, block), :]
                x_next = kappa[z, pl.ds(PAD + x + 1, block), :]
                x_back = kappa[z, pl.ds(PAD + x - 1, block), :]
                z_next = kappa[z + 1, pl.ds(PAD + x, block), :]
                z_back = kappa[z - 1, pl.ds(PAD + x, block), :]
                at = lane[x : x + block]
                y_next = jnp.where(at < lanes - 1, pltpu.roll(here, lanes - 1, 1), 0.0)
                y_back = jnp.where(at > 0, pltpu.roll(here, 1, 1), 0.0)
                along_x[z, pl.ds(PAD + x, block), :] = here + x_next
                along_y[z, pl.ds(x, block), :] = jnp.where(at < lanes - 1, here + y_next, 0.0)
                along_z[z, pl.ds(x, block), :] = here + z_next
                around = (x_next + x_back) + (y_next + y_back) + (z_next + z_back)
                centre[z, pl.ds(x, block), :] = 1.0 - (6.0 * here + around)
            return carry

        lax.fori_loop(1, total - 1, coefficients, 0)

        def first_faces(x, carry):
            along_z[0, pl.ds(x * PAD, PAD), :] = (
                kappa[0, pl.ds(PAD + x * PAD, PAD), :] + kappa[1, pl.ds(PAD + x * PAD, PAD), :]
            )
            return carry

        lax.fori_loop(0, length // PAD, first_faces, 0)

        old, new = first, second
        for step in range(1, steps + 1):

            def advance(z, carry):
                scale = jnp.where(
                    ((z < steps) & (edge[0] == 0)) | ((z >= steps + depth) & (edge[1] == 0)), 0.0, 1.0
                )
                for x in range(0, length, block):
                    own_rows = pl.ds(x, block)
                    padded_rows = pl.ds(PAD + x, block)
                    here = old[z, padded_rows, :]
                    face_y = along_y[z, own_rows, :]
                    value = centre[z, own_rows, :] * here
                    value += face_y * pltpu.roll(here, lanes - 1, 1)
                    value += pltpu.roll(face_y * here, 1, 1)
                    value += along_x[z, padded_rows, :] * old[z, pl.ds(PAD + x + 1, block), :]
                    back = pl.ds(PAD + x - 1, block)
                    value += along_x[z, back, :] * old[z, back, :]
                    value += along_z[z, own_rows, :] * old[z + 1, padded_rows, :]
                    value += along_z[z - 1, own_rows, :] * old[z - 1, padded_rows, :]
                    new[z, padded_rows, :] = value * scale
                return carry

            lax.fori_loop(step, total - step, advance, 0)
            old, new = new, old
        plane = lambda z: old[z + steps, pl.ds(PAD, length), :]
    else:
        plane = lambda z: occ[z]

    width = 2

    def transform(group, carry):
        sides = []
        for k in range(width):
            sides.append(along_lanes(plane(group * width + k), table_y[...]))
        high, low = split(jnp.concatenate(sides, axis=1))
        both = dot(table_x[...], jnp.concatenate([high, low, high], axis=0))
        for k in range(width):
            part = both[:, k * lanes : (k + 1) * lanes]
            turned = pltpu.roll(part[length:], lanes // 2, 1)
            value = take_cosine[...] * part[:length] + take_sine[...] * turned
            for chunk in range(chunks):
                outs[chunk][pl.ds(group * width + k, rows, stride=depth), :] = value[
                    chunk * rows : (chunk + 1) * rows
                ]
        return carry

    lax.fori_loop(0, depth // width, transform, 0)


def cross_kernel(length_x, start, damping, matches, spectra, table_f, table_i, out, held, weight):
    slabs, submaps, _, depth, lanes = spectra.shape
    length_z = slabs * depth
    half = lanes // 2
    lane = lax.broadcasted_iota(jnp.int32, (length_z, lanes), 1)
    sign = jnp.where(lane < half, 1.0, -1.0)
    first = (lane == 0) | (lane == half)
    row = start[0] + pl.program_id(0)
    special = (row == 0) | (row == length_x // 2)
    upper = row > length_x // 2

    def signed(count, length):
        return jnp.where(count < length // 2, count, count - length).astype(F32) / length

    @pl.when(pl.program_id(0) == 0)
    def _():
        along = signed(lax.broadcasted_iota(jnp.int32, (length_z, lanes), 0), length_z)
        for s in range(submaps):
            weight[s] = jnp.exp(-damping[s] * (along * along))

    at_x = signed(row, length_x)
    lane_row = lax.broadcasted_iota(jnp.int32, (8, lanes), 1)
    count_y = jnp.where(lane_row < half, lane_row, lane_row - half)
    nyquist = ((lane_row == 0) & upper) | ((lane_row == half) & (special | upper))
    at_y = jnp.where(nyquist, -0.5, signed(count_y, lanes))
    radius = at_x * at_x + at_y * at_y

    for s in range(submaps):
        column = jnp.concatenate([spectra[i, s, 0] for i in range(slabs)], axis=0)
        high, low = split(column)
        both = dot(table_f[...], jnp.concatenate([high, low, high], axis=0))
        cosine, sine = both[:length_z], both[length_z:]
        value = cosine + sign * pltpu.roll(sine, half, 1)
        square = value * value
        held[0, s] = value
        held[1, s] = square + pltpu.roll(square, half, 1)
        held[2, s] = cosine
        held[3, s] = sine

    for s in range(submaps):
        partner = matches[s]
        own, far = held[0, s], held[0, partner]
        damp = weight[s] * jnp.tile(jnp.exp(-damping[s] * radius), (length_z // 8, 1))
        scale = damp * lax.rsqrt(held[1, s] * held[1, partner] + FLOOR_VALUE**2)
        same = own * far
        mixed = own * pltpu.roll(far, half, 1)
        real = same + pltpu.roll(same, half, 1)
        imag = mixed - pltpu.roll(mixed, half, 1)
        imag = jnp.where(lane < half, -imag, imag)
        x_here = jnp.where(lane < half, real, imag) * scale
        x_turn = jnp.where(lane < half, -imag, real) * scale
        held[4, s] = jnp.where(first & upper, x_turn, x_here)
        held[5, s] = jnp.where(first & upper, -x_here, x_turn)

        @pl.when(special)
        def _():
            own_r, own_i = held[2, s], -held[3, s]
            far_r, far_i = held[2, partner], -held[3, partner]
            size = (own_r * own_r + own_i * own_i) * (far_r * far_r + far_i * far_i)
            scale = damp * lax.rsqrt(size + FLOOR_VALUE**2)
            held[4, s] = jnp.where(first, (own_r * far_r + own_i * far_i) * scale, held[4, s])
            held[5, s] = jnp.where(first, (own_r * far_i - own_i * far_r) * scale, held[5, s])

        high, low = split(jnp.concatenate([held[4, s], held[5, s]], axis=0))
        back = dot(table_i[...], jnp.concatenate([high, low, high], axis=0))
        for i in range(slabs):
            out[i, s, 0] = back[i * depth : (i + 1) * depth]


def inverse_kernel(depth, rows, *refs):
    columns, weights, table_x, table_y = refs[:4]
    before = refs[4] if len(refs) > 5 else None
    out = refs[-1]
    width, length, lanes = out.shape
    half = lanes // 2
    lane = lax.broadcasted_iota(jnp.int32, (rows, lanes), 1)
    sign = jnp.where(lane < half, -1.0, 1.0)
    group = pl.program_id(0)
    sides = []
    for k in range(width):
        value = columns[pl.ds(group * width + k, rows, stride=depth), :]
        turned = pltpu.roll(value, half, 1) * sign
        sides.append(jnp.concatenate([value * weights[...], turned * weights[...]], axis=0))
    high, low = split(jnp.concatenate(sides, axis=1))
    both = dot(table_x[...], jnp.concatenate([high, low, high], axis=0))
    for k in range(width):
        value = along_lanes(both[:, k * lanes : (k + 1) * lanes], table_y[...])
        if before is not None:
            value += before[k]
        out[k] = value


def params():
    return pltpu.CompilerParams(vmem_limit_bytes=VMEM_BYTES)


def whole_spec():
    return pl.BlockSpec(memory_space=pltpu.VMEM)


def scalar_spec():
    return pl.BlockSpec(memory_space=pltpu.SMEM)


def forward(volume, halo, chunks, tables):
    depth, length, lanes = volume.shape
    steps = STEPS if halo is not None else 0
    outs = [jax.ShapeDtypeStruct((length // chunks * depth, lanes), F32)] * chunks
    specs = [whole_spec()]
    operands = [volume]
    scratch = []
    if steps:
        operands += list(halo)
        specs += [whole_spec()] * 3 + [scalar_spec()] * 2
        total = depth + 2 * steps
        padded = pltpu.VMEM((total, length + 2 * PAD, lanes), F32)
        plain = pltpu.VMEM((total, length, lanes), F32)
        scratch = [padded, padded, plain, padded, plain, plain]
    return pl.pallas_call(
        functools.partial(forward_kernel, steps, chunks, depth),
        out_shape=outs,
        in_specs=specs + [whole_spec()] * len(tables),
        out_specs=[whole_spec()] * chunks,
        scratch_shapes=scratch,
        compiler_params=params(),
        name="forward",
    )(*operands, *tables)


def middle(spectra, start, damping, matches, length_x, tables):
    slabs, submaps, rows, depth, lanes = spectra.shape
    length_z = slabs * depth
    block = pl.BlockSpec((slabs, submaps, 1, depth, lanes), lambda r: (0, 0, r, 0, 0))
    return pl.pallas_call(
        functools.partial(cross_kernel, length_x),
        out_shape=jax.ShapeDtypeStruct(spectra.shape, F32),
        grid=(rows,),
        in_specs=[scalar_spec()] * 3 + [block] + [whole_spec()] * 2,
        out_specs=block,
        scratch_shapes=[
            pltpu.VMEM((6, submaps, length_z, lanes), F32),
            pltpu.VMEM((submaps, length_z, lanes), F32),
        ],
        compiler_params=params(),
        cost_estimate=pl.CostEstimate(
            flops=6 * 2 * spectra.size * length_z * 2,
            bytes_accessed=spectra.size * 8,
            transcendentals=spectra.size,
        ),
        name="middle",
    )(start, damping, matches, spectra, *tables)


def inverse(columns, before, depth, length, tables):
    total, lanes = columns.shape
    rows = total // depth
    width = 2
    block = pl.BlockSpec((width, length, lanes), lambda g: (g, 0, 0))
    extra = [] if before is None else [before]
    return pl.pallas_call(
        functools.partial(inverse_kernel, depth, rows),
        out_shape=jax.ShapeDtypeStruct((depth, length, lanes), F32),
        grid=(depth // width,),
        in_specs=[whole_spec()] * 4 + [block] * len(extra),
        out_specs=block,
        compiler_params=params(),
        cost_estimate=pl.CostEstimate(
            flops=6 * 2 * depth * length * lanes * rows,
            bytes_accessed=columns.size * 4 + depth * length * lanes * 4 * (1 + len(extra)),
            transcendentals=0,
        ),
        name="inverse",
    )(columns, *tables, *extra)


def ends(size):
    up = [(i, i + 1) for i in range(size - 1)]
    return up, [(j, i) for i, j in up]


def diffuse_plain(field, classes, conductance):
    up, down = ends(lax.axis_size("slab"))

    def widened(volume):
        before = lax.ppermute(volume[-1:], "slab", up)
        after = lax.ppermute(volume[:1], "slab", down)
        return jnp.pad(jnp.concatenate([before, volume, after], axis=0), ((0, 0), (1, 1), (1, 1)))

    def around(volume):
        wide = widened(volume)
        core = slice(1, -1)
        for low in (slice(2, None), slice(None, -2)):
            yield wide[low, core, core]
            yield wide[core, low, core]
            yield wide[core, core, low]

    kappa = conductance[classes]
    others = list(around(kappa))
    for _ in range(STEPS):
        change = jnp.zeros_like(field)
        for near, beside in zip(around(field), others):
            change = change + 0.5 * (kappa + beside) * (near - field)
        field = field + STEP_SIZE * change
    return field


def local(occupancy, classes, conductance, damping, matches):
    slabs, pairs = lax.axis_size("slab"), lax.axis_size("pair")
    devices = slabs * pairs
    occ, cls = occupancy[0], classes[0]
    depth, length, lanes = occ.shape
    each = length // devices
    chunks = 2 if each % 2 == 0 else 1
    rows = each // chunks
    length_z = depth * slabs

    kx = np.arange(length)
    cos_x, sin_x = trig(kx, kx, length)
    take_cosine, take_sine, weights = first_column_masks(kx, length, lanes)
    table_y = right_table(half_forward(lanes))
    table_x = left_table_stack(cos_x, sin_x)
    forward_tables = (table_y, table_x, take_cosine, take_sine)
    kz = np.arange(length_z)
    cos_z, sin_z = trig(kz, kz, length_z)
    middle_tables = (left_table_stack(cos_z, sin_z), left_table(np.concatenate([cos_z, sin_z], axis=1)))
    table_back = right_table(half_inverse(lanes))

    if depth >= STEPS:
        up, down = ends(slabs)
        pack = lambda low, high: jnp.concatenate([occ[low:high], cls[low:high].astype(F32)], axis=0)
        below = lax.ppermute(pack(depth - STEPS, depth), "slab", up)
        above = lax.ppermute(pack(0, STEPS), "slab", down)
        at = lax.axis_index("slab")
        edge = jnp.stack([at > 0, at < slabs - 1]).astype(jnp.int32)
        parts = forward(occ, (cls, below, above, edge, conductance), chunks, forward_tables)
    else:
        parts = forward(diffuse_plain(occ, cls, conductance), None, chunks, forward_tables)

    me = lax.axis_index(AXES)
    straight = depth % 8 == 0
    result = None
    backs = []
    for chunk in range(chunks):
        part = parts[chunk].reshape(devices, rows, depth, lanes)
        part = lax.all_to_all(part, AXES, 0, 0, tiled=True)
        part = part.reshape(slabs, pairs, rows, depth, lanes)
        if not straight:
            part = part.transpose(1, 2, 0, 3, 4).reshape(1, pairs, rows, length_z, lanes)
        start = (chunk * (length // chunks) + me * rows).astype(jnp.int32).reshape(1)
        part = middle(part, start, damping, matches, length, middle_tables)
        if not straight:
            part = part.reshape(pairs, rows, slabs, depth, lanes).transpose(2, 0, 1, 3, 4)
        part = part.reshape(devices, rows, depth, lanes)
        backs.append(part)
    for chunk in range(chunks):
        part = lax.all_to_all(backs[chunk], AXES, 0, 0, tiled=True)
        inside = slice(chunk * (length // chunks), (chunk + 1) * (length // chunks))
        table = left_table(np.concatenate([cos_x[:, inside], sin_x[:, inside]], axis=1))
        result = inverse(
            part.reshape(-1, lanes), result, depth, length, (weights[inside], table, table_back)
        )
    return result[None]


def left_table_stack(cosine, sine):
    return np.concatenate([left_table(cosine), left_table(sine)], axis=0)


def solution(mesh):
    in_specs = (
        P(("groups", "pair"), "slab", None, None),
        P(("groups", "pair"), "slab", None, None),
        P(),
        P("groups"),
        P("groups"),
    )
    out_specs = P(("groups", "pair"), "slab", None, None)
    return jax.shard_map(local, mesh=mesh, in_specs=in_specs, out_specs=out_specs, check_vma=False)
```

time: 899 us -> 317 us (0.35); the launches traced: 884 us -> 317 us
  waiting for transfers between devices: 463 us -> 123 us
  other arithmetic: 154 us -> 2.95 us
  Pallas kernels: 0 us -> 111 us
  matrix products: 105 us -> 0 us
  starting transfers between devices: 90.7 us -> 19.9 us
  local copies, waits for them, and re-layouts: 71.1 us -> 4.89 us
  blocking collectives: 0 us -> 54 us
    all_to_all x8 -> x3, waiting for transfers between devices: 456 us -> 100 us  [the longest x2 67.3 us: local(): part = lax.all_to_all(backs[chunk], AXES, 0, 0, tiled=True)]
    pallas_call x0 -> x5, Pallas kernels: none -> 111 us  [the longest x1 53.5 us: forward(): pl.pallas_call(functools.partial(forward_kernel, steps, chunks, depth), o...]
    dot_general x20 -> x0, matrix products: 105 us -> none  [multiply_along(): jnp.einsum(FORMS[axis_dim], values, matrix, precision=lax.Precision.HIGHEST)]
    add x5 -> x0, other arithmetic: 76.5 us -> none  [the longest x3 76 us: local(): volume = volume + STEP_SIZE * change]
    all_to_all x0 -> x1, blocking collectives: none -> 54 us  [local(): part = lax.all_to_all(part, AXES, 0, 0, tiled=True)]
    all_to_all x8 -> x3, starting transfers between devices: 63.8 us -> 14.6 us  [the longest x2 9.56 us: local(): part = lax.all_to_all(backs[chunk], AXES, 0, 0, tiled=True)]
    all_to_all x8 -> x0, local copies, waits for them, and re-layouts: 36.6 us -> none  [the longest x1 8.18 us: local(): lax.all_to_all(real_part, 'pair', split_axis=2, concat_axis=0, tiled=True)]
    concatenate x5 -> x2, other arithmetic: 35.7 us -> 1.11 us  [local(): jnp.concatenate([occ[low:high], cls[low:high].astype(F32)], axis=0)]
  transfers between devices with their start and end apart: 18 -> 5, of which waited for: 14 -> 5; matrix products, arithmetic and copies ran while one was open for 10% -> 1% of each run, Pallas kernels for 0% -> 13%
where the time goes in v1:
time: 317 us
  waiting for transfers between devices  123 us (39%)
  Pallas kernels  111 us (35%)
  blocking collectives  54 us (17%)
  starting transfers between devices  19.9 us (6%)
  local copies, waits for them, and re-layouts  4.89 us (2%)
    all_to_all x2, waiting for transfers between devices, local(): part = lax.all_to_all(backs[chunk], AXES, 0, 0, tiled=True)  67.3 us
    all_to_all x1, blocking collectives, local(): part = lax.all_to_all(part, AXES, 0, 0, tiled=True)  54 us
    pallas_call x1, Pallas kernels, forward(): pl.pallas_call(functools.partial(forward_kernel, steps, chunks, depth), o...  53.5 us
    all_to_all x1, waiting for transfers between devices, local(): part = lax.all_to_all(part, AXES, 0, 0, tiled=True)  32.9 us
    pallas_call x2, Pallas kernels, middle(): pl.pallas_call(functools.partial(cross_kernel, length_x), out_shape=jax.S...  29 us
    pallas_call x2, Pallas kernels, inverse(): pl.pallas_call(functools.partial(inverse_kernel, depth, rows), out_shape=...  28.9 us
    ppermute x1, waiting for transfers between devices, local(): below = lax.ppermute(pack(depth - STEPS, depth), 'slab', up)  19 us
    all_to_all x2, starting transfers between devices, local(): part = lax.all_to_all(backs[chunk], AXES, 0, 0, tiled=True)  9.56 us
  transfers between devices with their start and end apart: 5, of which 5 were waited for; matrix products, arithmetic and copies ran while one was open for 1% of the time, Pallas kernels for 13%

profile of v1, /device:TPU:11, one launch (start us, length us, event | category | flops | bytes accessed | tf_op | source)
XLA Modules:
  0.0 316.7 jit_solution(10865122302180607209)
XLA Ops:
  0.0 1.3 slice_bitcast_fusion
  1.3 1.3 convert_bitcast_fusion
  2.6 0.1 pad_maximum_fusion
  2.6 3.2 %collective-permute-start = (f32[8,256,128]{2,1,0:T(8,128)S(1)}, f32[8,256,128]{2,1,0:T(8,128)S(1)}, u32[]{:S(2)}, u32[]{:S(2)}) collective-permute-start(f32[8,256,128]{2,1,0:T(8,128)S(1)} %pad_maximum_fusion), channel_id=1, source_target_pairs={{0,4},{4,8},{8,12},{1,5},{5,9},{9,13},{2,6},{6,10},{10,14},{3,7},{... | collective-permute-start | bytes 3145736 | tf_op jit(solution)/shard_map/ppermute | solution.py:457
  5.9 1.0 pad_maximum_fusion.1
  6.9 2.1 collective-permute-start.1
  9.0 0.6 add_convert_fusion.refs_4_
  9.6 19.0 %collective-permute-done.refs_2_ = f32[8,256,128]{2,1,0:T(8,128)S(1)} collective-permute-done((f32[8,256,128]{2,1,0:T(8,128)S(1)}, f32[8,256,128]{2,1,0:T(8,128)S(1)}, u32[]{:S(2)}, u32[]{:S(2)}) %collective-permute-start) | collective-permute-done | bytes 1048608 | tf_op jit(solution)/shard_map/ppermute | solution.py:457
  28.6 0.0 copy-start.2
  28.6 4.2 %collective-permute-done.1.refs_3_ = f32[8,256,128]{2,1,0:T(8,128)S(1)} collective-permute-done((f32[8,256,128]{2,1,0:T(8,128)}, f32[8,256,128]{2,1,0:T(8,128)S(1)}, u32[]{:S(2)}, u32[]{:S(2)}) %collective-permute-start.1) | collective-permute-done | bytes 1048608 | tf_op jit(solution)/shard_map/ppermute | solution.py:458
  32.8 0.0 copy-start.3
  32.8 0.0 copy-done.2
  32.8 1.0 copy-done.3
  33.7 53.5 %forward.1 = (f32[4096,128]{1,0:T(8,128)}, f32[4096,128]{1,0:T(8,128)}) custom-call(f32[32,256,128]{2,1,0:T(8,128)} %bitcast.24, s32[32,256,128]{2,1,0:T(8,128)} %bitcast.25, f32[8,256,128]{2,1,0:T(8,128)} %copy-done.2, f32[8,256,128]{2,1,0:T(8,128)} %copy-done.3, s32[2]{0:T(128)} %add_convert_fusion.refs_4_, f32[8]{0:T(128)} %refs_5_.1, ...), custom_call_target="tpu_custom_call" | custom-call | tf_op jit(solution)/shard_map/forward/pallas_call | solution.py:345
  87.3 54.0 %all_to_all.20 = f32[16,8,32,128]{3,2,1,0:T(8,128)} all-to-all(f32[16,8,32,128]{3,2,1,0:T(8,128)} %bitcast.31), channel_id=1, replica_groups=mesh['groups'=2,'slab'=4,'pair'=4] {'slab','pair'}, dimensions={0} | all-to-all | bytes 4194304 | tf_op jit(solution)/shard_map/all_to_all | solution.py:471
  141.3 5.0 %all-to-all-start = ((f32[16,8,32,128]{3,2,1,0:T(8,128)}), f32[16,8,32,128]{3,2,1,0:T(8,128)S(1)}, u32[]{:S(2)}, u32[]{:S(2)}) async-start(f32[16,8,32,128]{3,2,1,0:T(8,128)} %bitcast.27), calls=%async_computation | async-start | bytes 4194304 | tf_op jit(solution)/shard_map/all_to_all | solution.py:471
  146.3 14.5 %middle.3 = f32[4,4,8,32,128]{4,3,2,1,0:T(8,128)} custom-call(s32[1]{0:T(128)} %bitcast.13.start, f32[4]{0:T(128)} %damping.3, s32[4]{0:T(128)} %matches.3, f32[4,4,8,32,128]{4,3,2,1,0:T(8,128)} %bitcast.28, bf16[256,384]{1,0:T(8,128)(2,1)} %constant.43.clone.table_f, bf16[128,768]{1,0:T(8,128)(2,1)} %constant.44.clone.table_i), custom_call_target="tpu_custom_call" | custom-call | flops 1610612736 | bytes 4194304 | tf_op jit(solution)/shard_map/middle/pallas_call | solution.py:360
  160.8 32.9 %all-to-all-done = f32[16,8,32,128]{3,2,1,0:T(8,128)S(1)} async-done(((f32[16,8,32,128]{3,2,1,0:T(8,128)}), f32[16,8,32,128]{3,2,1,0:T(8,128)S(1)}, u32[]{:S(2)}, u32[]{:S(2)}) %all-to-all-start) | async-done | bytes 2097184 | tf_op jit(solution)/shard_map/all_to_all | solution.py:471
  193.7 0.0 copy-start.1
  193.7 1.3 copy-done.1
  195.1 4.8 %all-to-all-start.3 = ((f32[16,8,32,128]{3,2,1,0:T(8,128)}), f32[16,8,32,128]{3,2,1,0:T(8,128)S(1)}, u32[]{:S(2)}, u32[]{:S(2)}) async-start(f32[16,8,32,128]{3,2,1,0:T(8,128)} %bitcast.29), calls=%async_computation.3 | async-start | bytes 4194304 | tf_op jit(solution)/shard_map/all_to_all | solution.py:482
  199.8 14.5 %middle.2 = f32[4,4,8,32,128]{4,3,2,1,0:T(8,128)} custom-call(s32[1]{0:T(128)} %bitcast.start, f32[4]{0:T(128)} %damping.3, s32[4]{0:T(128)} %matches.3, f32[4,4,8,32,128]{4,3,2,1,0:T(8,128)} %bitcast.26, bf16[256,384]{1,0:T(8,128)(2,1)} %constant.43.clone.table_f, bf16[128,768]{1,0:T(8,128)(2,1)} %constant.44.clone.table_i), custom_call_target="tpu_custom_call" | custom-call | flops 1610612736 | bytes 4194304 | tf_op jit(solution)/shard_map/middle/pallas_call | solution.py:360
  214.3 32.9 %all-to-all-done.3 = f32[16,8,32,128]{3,2,1,0:T(8,128)S(1)} async-done(((f32[16,8,32,128]{3,2,1,0:T(8,128)}), f32[16,8,32,128]{3,2,1,0:T(8,128)S(1)}, u32[]{:S(2)}, u32[]{:S(2)}) %all-to-all-start.3) | async-done | bytes 2097184 | tf_op jit(solution)/shard_map/all_to_all | solution.py:482
  247.3 0.0 copy-start
  247.3 1.3 copy-done
  248.6 4.8 %all-to-all-start.1 = ((f32[16,8,32,128]{3,2,1,0:T(8,128)}), f32[16,8,32,128]{3,2,1,0:T(8,128)}, u32[]{:S(2)}, u32[]{:S(2)}) async-start(f32[16,8,32,128]{3,2,1,0:T(8,128)} %bitcast.30), calls=%async_computation.1 | async-start | bytes 4194304 | tf_op jit(solution)/shard_map/all_to_all | solution.py:482
  253.4 13.1 %inverse.2.refs_4_ = f32[32,256,128]{2,1,0:T(8,128)} custom-call(f32[4096,128]{1,0:T(8,128)} %bitcast.23, f32[128,128]{1,0:T(8,128)} %constant.45.clone.refs_1_, bf16[256,768]{1,0:T(8,128)(2,1)} %constant.46.clone.refs_2_, bf16[256,256]{1,0:T(8,128)(2,1)} %constant.47.clone.refs_3_), custom_call_target="tpu_custom_call" | custom-call | flops 1610612736 | bytes 6291456 | tf_op jit(solution)/shard_map/inverse/pallas_call | solution.py:386
  266.5 34.4 %all-to-all-done.1 = f32[16,8,32,128]{3,2,1,0:T(8,128)} async-done(((f32[16,8,32,128]{3,2,1,0:T(8,128)}), f32[16,8,32,128]{3,2,1,0:T(8,128)}, u32[]{:S(2)}, u32[]{:S(2)}) %all-to-all-start.1) | async-done | bytes 2097184 | tf_op jit(solution)/shard_map/all_to_all | solution.py:482
  300.9 15.8 %inverse.3 = f32[32,256,128]{2,1,0:T(8,128)} custom-call(f32[4096,128]{1,0:T(8,128)} %bitcast.12.refs_0_, f32[128,128]{1,0:T(8,128)} %constant.48.clone.refs_1_, bf16[256,768]{1,0:T(8,128)(2,1)} %constant.49.clone.refs_2_, bf16[256,256]{1,0:T(8,128)(2,1)} %constant.47.clone.refs_3_, f32[32,256,128]{2,1,0:T(8,128)} %inverse.2.refs_4_), custom_call_target="tpu_custom_call" | custom-call | flops 1610612736 | bytes 10485760 | tf_op jit(solution)/shard_map/inverse/pallas_call | solution.py:386
Async XLA Ops:
  2.6 25.9 %collective-permute-start = (f32[8,256,128]{2,1,0:T(8,128)S(1)}, f32[8,256,128]{2,1,0:T(8,128)S(1)}, u32[]{:S(2)}, u32[]{:S(2)}) collective-permute-start(f32[8,256,128]{2,1,0:T(8,128)S(1)} %pad_maximum_fusion), channel_id=1, source_target_pairs={{0,4},{4,8},{8,12},{1,5},{5,9},{9,13},{2,6},{6,10},{10,14},{3,7},{... | collective-permute-start | bytes 3145736 | tf_op jit(solution)/shard_map/ppermute | solution.py:457
  6.9 25.9 %collective-permute-start.1 = (f32[8,256,128]{2,1,0:T(8,128)}, f32[8,256,128]{2,1,0:T(8,128)S(1)}, u32[]{:S(2)}, u32[]{:S(2)}) collective-permute-start(f32[8,256,128]{2,1,0:T(8,128)} %pad_maximum_fusion.1), channel_id=1, source_target_pairs={{4,0},{8,4},{12,8},{5,1},{9,5},{13,9},{6,2},{10,6},{14,10},{7,3},{... | collective-permute-start | bytes 3145736 | tf_op jit(solution)/shard_map/ppermute | solution.py:458
  28.6 4.2 %copy-start.2 = (f32[8,256,128]{2,1,0:T(8,128)}, f32[8,256,128]{2,1,0:T(8,128)S(1)}, u32[]{:S(2)}) copy-start(f32[8,256,128]{2,1,0:T(8,128)S(1)} %collective-permute-done.refs_2_) | copy-start | bytes 3145732
  32.8 1.0 copy-start.3
  141.3 52.4 %all-to-all-start = ((f32[16,8,32,128]{3,2,1,0:T(8,128)}), f32[16,8,32,128]{3,2,1,0:T(8,128)S(1)}, u32[]{:S(2)}, u32[]{:S(2)}) async-start(f32[16,8,32,128]{3,2,1,0:T(8,128)} %bitcast.27), calls=%async_computation | async-start | bytes 4194304 | tf_op jit(solution)/shard_map/all_to_all | solution.py:471
  193.7 1.3 copy-start.1
  195.1 52.2 %all-to-all-start.3 = ((f32[16,8,32,128]{3,2,1,0:T(8,128)}), f32[16,8,32,128]{3,2,1,0:T(8,128)S(1)}, u32[]{:S(2)}, u32[]{:S(2)}) async-start(f32[16,8,32,128]{3,2,1,0:T(8,128)} %bitcast.29), calls=%async_computation.3 | async-start | bytes 4194304 | tf_op jit(solution)/shard_map/all_to_all | solution.py:482
  247.3 1.3 copy-start
  248.6 52.3 %all-to-all-start.1 = ((f32[16,8,32,128]{3,2,1,0:T(8,128)}), f32[16,8,32,128]{3,2,1,0:T(8,128)}, u32[]{:S(2)}, u32[]{:S(2)}) async-start(f32[16,8,32,128]{3,2,1,0:T(8,128)} %bitcast.30), calls=%async_computation.1 | async-start | bytes 4194304 | tf_op jit(solution)/shard_map/all_to_all | solution.py:482

commit v2 on v1

--- a/solution.py
+++ b/solution.py
@@ -15,6 +15,8 @@
 FLOOR_VALUE = 0.01
 AXES = ("slab", "pair")
 PAD = 8
+BLOCK = 16
+PLANES = 2
 VMEM_BYTES = 60 * 1024 * 1024
 BF = jnp.bfloat16
 F32 = jnp.float32
@@ -92,136 +94,189 @@
     return both[:, :lanes] + both[:, lanes:]
 
 
-def forward_kernel(steps, chunks, depth, *refs):
-    if steps:
-        occ, cls, below, above, edge, conductance = refs[:6]
-        refs = refs[6:]
-    else:
-        occ = refs[0]
-        refs = refs[1:]
-    table_y, table_x, take_cosine, take_sine = refs[:4]
-    outs = refs[4 : 4 + chunks]
-    scratch = refs[4 + chunks :]
-    length, lanes = occ.shape[1:]
-    rows = length // chunks
-    if steps:
-        first, second, centre, along_x, along_y, along_z = scratch
-        total = depth + 2 * steps
-        lane = lax.broadcasted_iota(jnp.int32, (length, lanes), 1)
-        zeros = jnp.zeros((PAD, lanes), F32)
-        inside = pl.ds(PAD, length)
-        kappa = second
-
-        def fill(z, ids, field):
-            value = jnp.zeros((length, lanes), F32)
-            for index in range(conductance.shape[0]):
-                value = jnp.where(ids == index, conductance[index] * (0.5 * STEP_SIZE), value)
-            kappa[z, inside, :] = value
-            first[z, inside, :] = field
-
-        def clear(z, carry):
-            for ref in (first, second, along_x):
-                ref[z, pl.ds(0, PAD), :] = zeros
-                ref[z, pl.ds(PAD + length, PAD), :] = zeros
-            return carry
-
-        lax.fori_loop(0, total, clear, 0)
-
-        def own(z, carry):
-            fill(z + steps, cls[z], occ[z])
-            return carry
-
-        lax.fori_loop(0, depth, own, 0)
-
-        def outer(z, carry):
-            for ref, start, flag in ((below, 0, 0), (above, steps + depth, 1)):
-                fill(start + z, ref[steps + z].astype(jnp.int32), ref[z])
-
-                @pl.when(edge[flag] == 0)
-                def _():
-                    kappa[start + z, inside, :] = jnp.zeros((length, lanes), F32)
-
-            return carry
-
-        lax.fori_loop(0, steps, outer, 0)
-
-        block = 64
-
-        def coefficients(z, carry):
+def spread(first, kappa, along_x, length, lanes, total):
+    zeros = jnp.zeros((PAD, lanes), F32)
+
+    def clear(z, carry):
+        for ref in (first, kappa, along_x):
+            ref[z, pl.ds(0, PAD), :] = zeros
+            ref[z, pl.ds(PAD + length, PAD), :] = zeros
+        return carry
+
+    lax.fori_loop(0, total, clear, 0)
+
+
+def class_table(conductance, length, lanes):
+    at = lax.broadcasted_iota(jnp.int32, (PAD, lanes), 1)
+    entries = jnp.zeros((PAD, lanes), F32)
+    for index in range(conductance.shape[0]):
+        entries = jnp.where(at == index, conductance[index] * (0.5 * STEP_SIZE), entries)
+    return jnp.tile(entries, (length // PAD, 1))
+
+
+def face_weights(kappa, centre, along_x, along_y, along_z, total):
+    length, lanes = along_y.shape[1:]
+    block = BLOCK
+    at = lax.broadcasted_iota(jnp.int32, (block, lanes), 1)
+
+    def coefficients(z, carry):
+        for x in range(0, length, block):
+            rows = pl.ds(PAD + x, block)
+            here = kappa[z, rows, :]
+            x_next = kappa[z, pl.ds(PAD + x + 1, block), :]
+            x_back = kappa[z, pl.ds(PAD + x - 1, block), :]
+            z_next = kappa[z + 1, rows, :]
+            z_back = kappa[z - 1, rows, :]
+            y_next = jnp.where(at < lanes - 1, pltpu.roll(here, lanes - 1, 1), 0.0)
+            y_back = jnp.where(at > 0, pltpu.roll(here, 1, 1), 0.0)
+            along_x[z, rows, :] = here + x_next
+            along_y[z, pl.ds(x, block), :] = jnp.where(at < lanes - 1, here + y_next, 0.0)
+            along_z[z, pl.ds(x, block), :] = here + z_next
+            around = (x_next + x_back) + (y_next + y_back) + (z_next + z_back)
+            centre[z, pl.ds(x, block), :] = 1.0 - (6.0 * here + around)
+        return carry
+
+    lax.fori_loop(1, total - 1, coefficients, 0)
+    for x in range(0, length, block):
+        rows = pl.ds(PAD + x, block)
+        along_z[0, pl.ds(x, block), :] = kappa[0, rows, :] + kappa[1, rows, :]
+
+
+def advance_all(buffers, centre, along_x, along_y, along_z, total, steps, after_step):
+    length, lanes = along_y.shape[1:]
+    block = BLOCK
+    old, new = buffers
+    for step in range(1, steps + 1):
+
+        def advance(group, carry):
+            z0 = step + group * PLANES
             for x in range(0, length, block):
-                here = kappa[z, pl.ds(PAD + x, block), :]
-                x_next = kappa[z, pl.ds(PAD + x + 1, block), :]
-                x_back = kappa[z, pl.ds(PAD + x - 1, block), :]
-                z_next = kappa[z + 1, pl.ds(PAD + x, block), :]
-                z_back = kappa[z - 1, pl.ds(PAD + x, block), :]
-                at = lane[x : x + block]
-                y_next = jnp.where(at < lanes - 1, pltpu.roll(here, lanes - 1, 1), 0.0)
-                y_back = jnp.where(at > 0, pltpu.roll(here, 1, 1), 0.0)
-                along_x[z, pl.ds(PAD + x, block), :] = here + x_next
-                along_y[z, pl.ds(x, block), :] = jnp.where(at < lanes - 1, here + y_next, 0.0)
-                along_z[z, pl.ds(x, block), :] = here + z_next
-                around = (x_next + x_back) + (y_next + y_back) + (z_next + z_back)
-                centre[z, pl.ds(x, block), :] = 1.0 - (6.0 * here + around)
-            return carry
-
-        lax.fori_loop(1, total - 1, coefficients, 0)
-
-        def first_faces(x, carry):
-            along_z[0, pl.ds(x * PAD, PAD), :] = (
-                kappa[0, pl.ds(PAD + x * PAD, PAD), :] + kappa[1, pl.ds(PAD + x * PAD, PAD), :]
-            )
-            return carry
-
-        lax.fori_loop(0, length // PAD, first_faces, 0)
-
-        old, new = first, second
-        for step in range(1, steps + 1):
-
-            def advance(z, carry):
-                scale = jnp.where(
-                    ((z < steps) & (edge[0] == 0)) | ((z >= steps + depth) & (edge[1] == 0)), 0.0, 1.0
-                )
-                for x in range(0, length, block):
-                    own_rows = pl.ds(x, block)
-                    padded_rows = pl.ds(PAD + x, block)
-                    here = old[z, padded_rows, :]
+                own_rows = pl.ds(x, block)
+                padded_rows = pl.ds(PAD + x, block)
+                ahead = pl.ds(PAD + x + 1, block)
+                back = pl.ds(PAD + x - 1, block)
+                before = along_z[z0 - 1, own_rows, :] * old[z0 - 1, padded_rows, :]
+                here = old[z0, padded_rows, :]
+                for k in range(PLANES):
+                    z = z0 + k
+                    after = old[z + 1, padded_rows, :]
                     face_y = along_y[z, own_rows, :]
-                    value = centre[z, own_rows, :] * here
+                    face_z = along_z[z, own_rows, :]
+                    value = centre[z, own_rows, :] * here + before
+                    value += face_z * after
                     value += face_y * pltpu.roll(here, lanes - 1, 1)
                     value += pltpu.roll(face_y * here, 1, 1)
-                    value += along_x[z, padded_rows, :] * old[z, pl.ds(PAD + x + 1, block), :]
-                    back = pl.ds(PAD + x - 1, block)
+                    value += along_x[z, padded_rows, :] * old[z, ahead, :]
                     value += along_x[z, back, :] * old[z, back, :]
-                    value += along_z[z, own_rows, :] * old[z + 1, padded_rows, :]
-                    value += along_z[z - 1, own_rows, :] * old[z - 1, padded_rows, :]
-                    new[z, padded_rows, :] = value * scale
+                    new[z, padded_rows, :] = value
+                    before = face_z * here
+                    here = after
+            return carry
+
+        lax.fori_loop(0, (total - 2 * step) // PLANES, advance, 0)
+        after_step(new)
+        old, new = new, old
+    return old
+
+
+def inner_kernel(steps, conductance, occ, cls, out, first, second, centre, along_x, along_y, along_z, ids, sems, cls_sems):
+    total, length, lanes = occ.shape
+    inside = pl.ds(PAD, length)
+    pieces = cls_sems.shape[0]
+    size = total // pieces
+    loads = []
+    for k in range(pieces):
+        part = pl.ds(k * size, size)
+        loads.append(pltpu.make_async_copy(cls.at[part], ids.at[part], cls_sems.at[k]))
+        loads[-1].start()
+    field = pltpu.make_async_copy(occ, first.at[:, inside, :], sems.at[0])
+    field.start()
+    entries = class_table(conductance, length, lanes)
+    zeros = jnp.zeros((PAD, lanes), F32)
+
+    def clear(z, carry):
+        for ref in (first, second, along_x):
+            ref[z, pl.ds(0, PAD), :] = zeros
+            ref[z, pl.ds(PAD + length, PAD), :] = zeros
+        return carry
+
+    lax.fori_loop(0, total, clear, 0)
+    for k in range(pieces):
+        loads[k].wait()
+
+        def fill(z, carry):
+            second[z, inside, :] = jnp.take_along_axis(entries, ids[z], axis=1)
+            return carry
+
+        lax.fori_loop(k * size, (k + 1) * size, fill, 0)
+    face_weights(second, centre, along_x, along_y, along_z, total)
+    field.wait()
+    last = advance_all((first, second), centre, along_x, along_y, along_z, total, steps, lambda ref: None)
+    kept = pl.ds(steps, total - 2 * steps)
+    store = pltpu.make_async_copy(last.at[kept, inside, :], out.at[kept], sems.at[1])
+    store.start()
+    store.wait()
+
+
+def outer_kernel(steps, conductance, edge, occ, cls, below, above, _, out, first, second, centre, along_x, along_y, along_z):
+    total = 3 * steps
+    length, lanes = occ.shape[1:]
+    inside = pl.ds(PAD, length)
+    side = pl.program_id(0)
+    entries = class_table(conductance, length, lanes)
+    spread(first, second, along_x, length, lanes, total)
+
+    def own(z, carry):
+        at = z + jnp.where(side == 0, steps, 0)
+        second[at, inside, :] = jnp.take_along_axis(entries, cls[z], axis=1)
+        first[at, inside, :] = occ[z]
+        return carry
+
+    lax.fori_loop(0, 2 * steps, own, 0)
+    for at_side, ref, start in ((0, below, 0), (1, above, 2 * steps)):
+
+        @pl.when((side == at_side) & (edge[at_side] > 0))
+        def _():
+            def halo(z, carry):
+                ids = ref[steps + z].astype(jnp.int32)
+                second[start + z, inside, :] = jnp.take_along_axis(entries, ids, axis=1)
+                first[start + z, inside, :] = ref[z]
                 return carry
 
-            lax.fori_loop(step, total - step, advance, 0)
-            old, new = new, old
-        plane = lambda z: old[z + steps, pl.ds(PAD, length), :]
-    else:
-        plane = lambda z: occ[z]
-
-    width = 2
-
-    def transform(group, carry):
-        sides = []
-        for k in range(width):
-            sides.append(along_lanes(plane(group * width + k), table_y[...]))
+            lax.fori_loop(0, steps, halo, 0)
+
+    def clear_ghosts(ref):
+        for at_side, start in ((0, 0), (1, 2 * steps)):
+
+            @pl.when((side == at_side) & (edge[at_side] == 0))
+            def _():
+                def clear(z, carry):
+                    ref[start + z, inside, :] = jnp.zeros((length, lanes), F32)
+                    return carry
+
+                lax.fori_loop(0, steps, clear, 0)
+
+    clear_ghosts(first)
+    clear_ghosts(second)
+    face_weights(second, centre, along_x, along_y, along_z, total)
+    last = advance_all((first, second), centre, along_x, along_y, along_z, total, steps, clear_ghosts)
+    for k in range(steps):
+        out[k] = last[steps + k, inside, :]
+
+
+def spectrum_kernel(depth, volume, table_y, table_x, take_cosine, take_sine, out):
+    width, length, lanes = volume.shape
+    rows = take_cosine.shape[0]
+    group = pl.program_id(0)
+    for start in range(0, width, 2):
+        sides = [along_lanes(volume[start + k], table_y[...]) for k in range(2)]
         high, low = split(jnp.concatenate(sides, axis=1))
         both = dot(table_x[...], jnp.concatenate([high, low, high], axis=0))
-        for k in range(width):
+        for k in range(2):
             part = both[:, k * lanes : (k + 1) * lanes]
-            turned = pltpu.roll(part[length:], lanes // 2, 1)
-            value = take_cosine[...] * part[:length] + take_sine[...] * turned
-            for chunk in range(chunks):
-                outs[chunk][pl.ds(group * width + k, rows, stride=depth), :] = value[
-                    chunk * rows : (chunk + 1) * rows
-                ]
-        return carry
-
-    lax.fori_loop(0, depth // width, transform, 0)
+            turned = pltpu.roll(part[rows:], lanes // 2, 1)
+            value = take_cosine[...] * part[:rows] + take_sine[...] * turned
+            out[pl.ds(group * width + start + k, rows, stride=depth), :] = value
 
 
 def cross_kernel(length_x, start, damping, matches, spectra, table_f, table_i, out, held, weight):
@@ -328,29 +383,78 @@
     return pl.BlockSpec(memory_space=pltpu.SMEM)
 
 
-def forward(volume, halo, chunks, tables):
+def any_spec():
+    return pl.BlockSpec(memory_space=pl.ANY)
+
+
+def diffusion_scratch(total, length, lanes):
+    padded = pltpu.VMEM((total, length + 2 * PAD, lanes), F32)
+    plain = pltpu.VMEM((total, length, lanes), F32)
+    return [padded, padded, plain, padded, plain, plain]
+
+
+def diffuse_inner(occ, cls, conductance):
+    depth, length, lanes = occ.shape
+    return pl.pallas_call(
+        functools.partial(inner_kernel, STEPS),
+        out_shape=jax.ShapeDtypeStruct(occ.shape, F32),
+        in_specs=[scalar_spec(), any_spec(), any_spec()],
+        out_specs=any_spec(),
+        scratch_shapes=diffusion_scratch(depth, length, lanes)
+        + [
+            pltpu.VMEM(cls.shape, jnp.int32),
+            pltpu.SemaphoreType.DMA((2,)),
+            pltpu.SemaphoreType.DMA((4,)),
+        ],
+        compiler_params=params(),
+        cost_estimate=pl.CostEstimate(
+            flops=occ.size * 80, bytes_accessed=occ.size * 12, transcendentals=0
+        ),
+        name="inner",
+    )(conductance, occ, cls)
+
+
+def diffuse_outer(occ, cls, conductance, edge, below, above, inner):
+    depth, length, lanes = occ.shape
+    window = pl.BlockSpec((2 * STEPS, length, lanes), lambda s: (s * (depth // (2 * STEPS) - 1), 0, 0))
+    kept = pl.BlockSpec((STEPS, length, lanes), lambda s: (s * (depth // STEPS - 1), 0, 0))
+    return pl.pallas_call(
+        functools.partial(outer_kernel, STEPS),
+        out_shape=jax.ShapeDtypeStruct(occ.shape, F32),
+        grid=(2,),
+        in_specs=[scalar_spec(), scalar_spec(), window, window, whole_spec(), whole_spec(), any_spec()],
+        out_specs=kept,
+        scratch_shapes=diffusion_scratch(3 * STEPS, length, lanes),
+        input_output_aliases={6: 0},
+        compiler_params=params(),
+        cost_estimate=pl.CostEstimate(
+            flops=occ.size * 40, bytes_accessed=occ.size * 6, transcendentals=0
+        ),
+        name="outer",
+    )(conductance, edge, occ, cls, below, above, inner)
+
+
+def spectrum(volume, tables):
     depth, length, lanes = volume.shape
-    steps = STEPS if halo is not None else 0
-    outs = [jax.ShapeDtypeStruct((length // chunks * depth, lanes), F32)] * chunks
-    specs = [whole_spec()]
-    operands = [volume]
-    scratch = []
-    if steps:
-        operands += list(halo)
-        specs += [whole_spec()] * 3 + [scalar_spec()] * 2
-        total = depth + 2 * steps
-        padded = pltpu.VMEM((total, length + 2 * PAD, lanes), F32)
-        plain = pltpu.VMEM((total, length, lanes), F32)
-        scratch = [padded, padded, plain, padded, plain, plain]
+    table_y, table_x, take_cosine, take_sine = tables
+    rows = take_cosine.shape[0]
+    width = math.gcd(depth, 4)
+    block = pl.BlockSpec((width, length, lanes), lambda g: (g, 0, 0))
+    out = jax.ShapeDtypeStruct((rows * depth, lanes), F32)
     return pl.pallas_call(
-        functools.partial(forward_kernel, steps, chunks, depth),
-        out_shape=outs,
-        in_specs=specs + [whole_spec()] * len(tables),
-        out_specs=[whole_spec()] * chunks,
-        scratch_shapes=scratch,
+        functools.partial(spectrum_kernel, depth),
+        out_shape=out,
+        grid=(depth // width,),
+        in_specs=[block] + [whole_spec()] * 4,
+        out_specs=pl.BlockSpec(out.shape, lambda g: (0, 0)),
         compiler_params=params(),
-        name="forward",
-    )(*operands, *tables)
+        cost_estimate=pl.CostEstimate(
+            flops=6 * 2 * volume.size * (lanes + 2 * rows),
+            bytes_accessed=volume.size * 4 + rows * depth * lanes * 4,
+            transcendentals=0,
+        ),
+        name="spectrum",
+    )(volume, table_y, table_x, take_cosine, take_sine)
 
 
 def middle(spectra, start, damping, matches, length_x, tables):
@@ -444,30 +548,32 @@
     cos_x, sin_x = trig(kx, kx, length)
     take_cosine, take_sine, weights = first_column_masks(kx, length, lanes)
     table_y = right_table(half_forward(lanes))
-    table_x = left_table_stack(cos_x, sin_x)
-    forward_tables = (table_y, table_x, take_cosine, take_sine)
     kz = np.arange(length_z)
     cos_z, sin_z = trig(kz, kz, length_z)
     middle_tables = (left_table_stack(cos_z, sin_z), left_table(np.concatenate([cos_z, sin_z], axis=1)))
     table_back = right_table(half_inverse(lanes))
 
-    if depth >= STEPS:
+    if depth >= 4 * STEPS:
         up, down = ends(slabs)
         pack = lambda low, high: jnp.concatenate([occ[low:high], cls[low:high].astype(F32)], axis=0)
         below = lax.ppermute(pack(depth - STEPS, depth), "slab", up)
         above = lax.ppermute(pack(0, STEPS), "slab", down)
         at = lax.axis_index("slab")
         edge = jnp.stack([at > 0, at < slabs - 1]).astype(jnp.int32)
-        parts = forward(occ, (cls, below, above, edge, conductance), chunks, forward_tables)
+        inner = diffuse_inner(occ, cls, conductance)
+        volume = diffuse_outer(occ, cls, conductance, edge, below, above, inner)
     else:
-        parts = forward(diffuse_plain(occ, cls, conductance), None, chunks, forward_tables)
+        volume = diffuse_plain(occ, cls, conductance)
 
     me = lax.axis_index(AXES)
     straight = depth % 8 == 0
     result = None
     backs = []
     for chunk in range(chunks):
-        part = parts[chunk].reshape(devices, rows, depth, lanes)
+        inside = slice(chunk * (length // chunks), (chunk + 1) * (length // chunks))
+        table_x = left_table_stack(cos_x[inside], sin_x[inside])
+        part = spectrum(volume, (table_y, table_x, take_cosine[inside], take_sine[inside]))
+        part = part.reshape(devices, rows, depth, lanes)
         part = lax.all_to_all(part, AXES, 0, 0, tiled=True)
         part = part.reshape(slabs, pairs, rows, depth, lanes)
         if not straight:

time: 317 us -> 292 us (0.921)
  blocking collectives: 54 us -> 0 us
  waiting for transfers between devices: 123 us -> 137 us
  Pallas kernels: 111 us -> 118 us
  starting transfers between devices: 19.9 us -> 26.4 us
    all_to_all x1 -> x0, blocking collectives: 54 us -> none  [local(): part = lax.all_to_all(part, AXES, 0, 0, tiled=True)]
    all_to_all x1 -> x2, waiting for transfers between devices: 32.9 us -> 70 us  [local(): part = lax.all_to_all(part, AXES, 0, 0, tiled=True)]
    ppermute x1, waiting for transfers between devices: 19 us -> 0.01 us  [local(): below = lax.ppermute(pack(depth - STEPS, depth), 'slab', up)]
    pallas_call x1 -> x4, Pallas kernels: 53.5 us -> 60.4 us  [the longest x1 24 us: diffuse_inner(): pl.pallas_call(functools.partial(inner_kernel, STEPS), out_shape=jax.Shap...]
    all_to_all x1 -> x2, starting transfers between devices: 5.02 us -> 11.5 us  [local(): part = lax.all_to_all(part, AXES, 0, 0, tiled=True)]
    ppermute x1, waiting for transfers between devices: 4.17 us -> 0.01 us  [local(): above = lax.ppermute(pack(0, STEPS), 'slab', down)]
  transfers between devices with their start and end apart: 5 -> 6, of which waited for: 5 -> 4; matrix products, arithmetic and copies ran while one was open for 1% -> 1% of each run, Pallas kernels for 13% -> 26%
where the time goes in v2:
time: 292 us; the launch traced here: 291 us
  waiting for transfers between devices  137 us (47%)
  Pallas kernels  118 us (40%)
  starting transfers between devices  26.4 us (9%)
  local copies, waits for them, and re-layouts  5.87 us (2%)
  other arithmetic  3 us (1%)
    all_to_all x2, waiting for transfers between devices, local(): part = lax.all_to_all(part, AXES, 0, 0, tiled=True)  70 us
    all_to_all x2, waiting for transfers between devices, local(): part = lax.all_to_all(backs[chunk], AXES, 0, 0, tiled=True)  67.3 us
    pallas_call x2, Pallas kernels, middle(): pl.pallas_call(functools.partial(cross_kernel, length_x), out_shape=jax.S...  29 us
    pallas_call x2, Pallas kernels, inverse(): pl.pallas_call(functools.partial(inverse_kernel, depth, rows), out_shape=...  28.9 us
    pallas_call x1, Pallas kernels, diffuse_inner(): pl.pallas_call(functools.partial(inner_kernel, STEPS), out_shape=jax.Shap...  24 us
    pallas_call x2, Pallas kernels, spectrum(): pl.pallas_call(functools.partial(spectrum_kernel, depth), out_shape=out,...  20.6 us
    pallas_call x1, Pallas kernels, diffuse_outer(): pl.pallas_call(functools.partial(outer_kernel, STEPS), out_shape=jax.Shap...  15.8 us
    all_to_all x2, starting transfers between devices, local(): part = lax.all_to_all(part, AXES, 0, 0, tiled=True)  11.5 us
  transfers between devices with their start and end apart: 6, of which 4 were waited for; matrix products, arithmetic and copies ran while one was open for 1% of the time, Pallas kernels for 26%

profile of v2, /device:TPU:11, one launch (start us, length us, event | category | flops | bytes accessed | tf_op | source)
XLA Modules:
  0.0 291.0 jit_solution(6900162776113178613)
XLA Ops:
  0.0 1.3 slice_bitcast_fusion
  1.3 1.3 convert_bitcast_fusion
  2.6 0.1 pad_maximum_fusion
  2.6 3.2 %collective-permute-start = (f32[8,256,128]{2,1,0:T(8,128)S(1)}, f32[8,256,128]{2,1,0:T(8,128)S(1)}, u32[]{:S(2)}, u32[]{:S(2)}) collective-permute-start(f32[8,256,128]{2,1,0:T(8,128)S(1)} %pad_maximum_fusion), channel_id=1, source_target_pairs={{0,4},{4,8},{8,12},{1,5},{5,9},{9,13},{2,6},{6,10},{10,14},{3,7},{... | collective-permute-start | bytes 3145736 | tf_op jit(solution)/shard_map/ppermute | solution.py:559
  5.9 1.0 pad_maximum_fusion.1
  6.9 2.1 collective-permute-start.1
  9.1 24.0 %inner.1._ = f32[32,256,128]{2,1,0:T(8,128)} custom-call(f32[8]{0:T(128)} %conductance.3, f32[32,256,128]{2,1,0:T(8,128)} %bitcast.23, s32[32,256,128]{2,1,0:T(8,128)} %bitcast.25), custom_call_target="tpu_custom_call" | custom-call | flops 83886080 | bytes 12582912 | tf_op jit(solution)/shard_map/inner/pallas_call | solution.py:398
  33.1 0.6 add_convert_fusion.edge
  33.7 0.0 collective-permute-done.below
  33.7 0.0 copy-start.3
  33.7 0.0 collective-permute-done.1.above
  33.7 1.0 copy-done.3
  34.7 0.0 copy-start.4
  34.7 1.0 copy-done.4
  35.7 15.8 %outer.1.volume = f32[32,256,128]{2,1,0:T(8,128)} custom-call(f32[8]{0:T(128)} %conductance.3, s32[2]{0:T(128)} %add_convert_fusion.edge, f32[32,256,128]{2,1,0:T(8,128)} %bitcast.24, s32[32,256,128]{2,1,0:T(8,128)} %bitcast.26, f32[8,256,128]{2,1,0:T(8,128)} %copy-done.3, f32[8,256,128]{2,1,0:T(8,128)} %copy-done.4, ...), custom_call_target="tpu_custom_call", output_to_operand_aliasing={{}: (6, {})} | custom-call | flops 41943040 | bytes 6291456 | tf_op jit(solution)/shard_map/outer/pallas_call | solution.py:421
  51.4 10.3 %spectrum.3 = f32[4096,128]{1,0:T(8,128)} custom-call(f32[32,256,128]{2,1,0:T(8,128)} %outer.1.volume, bf16[256,256]{1,0:T(8,128)(2,1)} %constant.45.clone.table_y, bf16[256,768]{1,0:T(8,128)(2,1)} %constant.46.clone.table_x, f32[128,128]{1,0:T(8,128)} %constant.47.clone.take_cosine, f32[128,128]{1,0:T(8,128)} %constant.48.clone.take_sine), custom_call_target="tpu_custom_call" | custom-call | flops 4831838208 | bytes 6291456 | tf_op jit(solution)/shard_map/spectrum/pallas_call | solution.py:444
  61.7 6.7 %all-to-all-start.2 = ((f32[16,8,32,128]{3,2,1,0:T(8,128)}), f32[16,8,32,128]{3,2,1,0:T(8,128)S(1)}, u32[]{:S(2)}, u32[]{:S(2)}) async-start(f32[16,8,32,128]{3,2,1,0:T(8,128)} %bitcast.33), calls=%async_computation.2 | async-start | bytes 4194304 | tf_op jit(solution)/shard_map/all_to_all | solution.py:577
  68.4 10.3 %spectrum.2 = f32[4096,128]{1,0:T(8,128)} custom-call(f32[32,256,128]{2,1,0:T(8,128)} %outer.1.volume, bf16[256,256]{1,0:T(8,128)(2,1)} %constant.45.clone.table_y, bf16[256,768]{1,0:T(8,128)(2,1)} %constant.51.clone.table_x, f32[128,128]{1,0:T(8,128)} %constant.52.clone.take_cosine, f32[128,128]{1,0:T(8,128)} %constant.53.clone.take_sine), custom_call_target="tpu_custom_call" | custom-call | flops 4831838208 | bytes 6291456 | tf_op jit(solution)/shard_map/spectrum/pallas_call | solution.py:444
  78.7 37.1 %all-to-all-done.2 = f32[16,8,32,128]{3,2,1,0:T(8,128)S(1)} async-done(((f32[16,8,32,128]{3,2,1,0:T(8,128)}), f32[16,8,32,128]{3,2,1,0:T(8,128)S(1)}, u32[]{:S(2)}, u32[]{:S(2)}) %all-to-all-start.2) | async-done | bytes 2097184 | tf_op jit(solution)/shard_map/all_to_all | solution.py:577
  115.8 0.0 copy-start.2
  115.8 1.3 copy-done.2
  117.1 4.8 %all-to-all-start = ((f32[16,8,32,128]{3,2,1,0:T(8,128)}), f32[16,8,32,128]{3,2,1,0:T(8,128)S(1)}, u32[]{:S(2)}, u32[]{:S(2)}) async-start(f32[16,8,32,128]{3,2,1,0:T(8,128)} %bitcast.30), calls=%async_computation | async-start | bytes 4194304 | tf_op jit(solution)/shard_map/all_to_all | solution.py:577
  121.9 14.5 %middle.3 = f32[4,4,8,32,128]{4,3,2,1,0:T(8,128)} custom-call(s32[1]{0:T(128)} %bitcast.13.start, f32[4]{0:T(128)} %damping.3, s32[4]{0:T(128)} %matches.3, f32[4,4,8,32,128]{4,3,2,1,0:T(8,128)} %bitcast.29, bf16[256,384]{1,0:T(8,128)(2,1)} %constant.49.clone.table_f, bf16[128,768]{1,0:T(8,128)(2,1)} %constant.50.clone.table_i), custom_call_target="tpu_custom_call" | custom-call | flops 1610612736 | bytes 4194304 | tf_op jit(solution)/shard_map/middle/pallas_call | solution.py:464
  136.4 32.9 %all-to-all-done = f32[16,8,32,128]{3,2,1,0:T(8,128)S(1)} async-done(((f32[16,8,32,128]{3,2,1,0:T(8,128)}), f32[16,8,32,128]{3,2,1,0:T(8,128)S(1)}, u32[]{:S(2)}, u32[]{:S(2)}) %all-to-all-start) | async-done | bytes 2097184 | tf_op jit(solution)/shard_map/all_to_all | solution.py:577
  169.3 0.0 copy-start.1
  169.3 1.3 copy-done.1
  170.7 4.8 %all-to-all-start.3 = ((f32[16,8,32,128]{3,2,1,0:T(8,128)}), f32[16,8,32,128]{3,2,1,0:T(8,128)S(1)}, u32[]{:S(2)}, u32[]{:S(2)}) async-start(f32[16,8,32,128]{3,2,1,0:T(8,128)} %bitcast.31), calls=%async_computation.3 | async-start | bytes 4194304 | tf_op jit(solution)/shard_map/all_to_all | solution.py:588
  175.4 14.5 %middle.2 = f32[4,4,8,32,128]{4,3,2,1,0:T(8,128)} custom-call(s32[1]{0:T(128)} %bitcast.start, f32[4]{0:T(128)} %damping.3, s32[4]{0:T(128)} %matches.3, f32[4,4,8,32,128]{4,3,2,1,0:T(8,128)} %bitcast.28, bf16[256,384]{1,0:T(8,128)(2,1)} %constant.49.clone.table_f, bf16[128,768]{1,0:T(8,128)(2,1)} %constant.50.clone.table_i), custom_call_target="tpu_custom_call" | custom-call | flops 1610612736 | bytes 4194304 | tf_op jit(solution)/shard_map/middle/pallas_call | solution.py:464
  189.9 32.9 %all-to-all-done.3 = f32[16,8,32,128]{3,2,1,0:T(8,128)S(1)} async-done(((f32[16,8,32,128]{3,2,1,0:T(8,128)}), f32[16,8,32,128]{3,2,1,0:T(8,128)S(1)}, u32[]{:S(2)}, u32[]{:S(2)}) %all-to-all-start.3) | async-done | bytes 2097184 | tf_op jit(solution)/shard_map/all_to_all | solution.py:588
  222.9 0.0 copy-start
  222.9 4.8 %all-to-all-start.1 = ((f32[16,8,32,128]{3,2,1,0:T(8,128)}), f32[16,8,32,128]{3,2,1,0:T(8,128)}, u32[]{:S(2)}, u32[]{:S(2)}) async-start(f32[16,8,32,128]{3,2,1,0:T(8,128)} %bitcast.32), calls=%async_computation.1 | async-start | bytes 4194304 | tf_op jit(solution)/shard_map/all_to_all | solution.py:588
  227.6 0.0 copy-done
  227.6 13.1 %inverse.2.refs_4_ = f32[32,256,128]{2,1,0:T(8,128)} custom-call(f32[4096,128]{1,0:T(8,128)} %bitcast.27, f32[128,128]{1,0:T(8,128)} %constant.54.clone.refs_1_, bf16[256,768]{1,0:T(8,128)(2,1)} %constant.55.clone.refs_2_, bf16[256,256]{1,0:T(8,128)(2,1)} %constant.56.clone.refs_3_), custom_call_target="tpu_custom_call" | custom-call | flops 1610612736 | bytes 6291456 | tf_op jit(solution)/shard_map/inverse/pallas_call | solution.py:490
  240.8 34.4 %all-to-all-done.1 = f32[16,8,32,128]{3,2,1,0:T(8,128)} async-done(((f32[16,8,32,128]{3,2,1,0:T(8,128)}), f32[16,8,32,128]{3,2,1,0:T(8,128)}, u32[]{:S(2)}, u32[]{:S(2)}) %all-to-all-start.1) | async-done | bytes 2097184 | tf_op jit(solution)/shard_map/all_to_all | solution.py:588
  275.2 15.8 %inverse.3 = f32[32,256,128]{2,1,0:T(8,128)} custom-call(f32[4096,128]{1,0:T(8,128)} %bitcast.12.refs_0_, f32[128,128]{1,0:T(8,128)} %constant.57.clone.refs_1_, bf16[256,768]{1,0:T(8,128)(2,1)} %constant.58.clone.refs_2_, bf16[256,256]{1,0:T(8,128)(2,1)} %constant.56.clone.refs_3_, f32[32,256,128]{2,1,0:T(8,128)} %inverse.2.refs_4_), custom_call_target="tpu_custom_call" | custom-call | flops 1610612736 | bytes 10485760 | tf_op jit(solution)/shard_map/inverse/pallas_call | solution.py:490
Async XLA Ops:
  2.6 31.1 %collective-permute-start = (f32[8,256,128]{2,1,0:T(8,128)S(1)}, f32[8,256,128]{2,1,0:T(8,128)S(1)}, u32[]{:S(2)}, u32[]{:S(2)}) collective-permute-start(f32[8,256,128]{2,1,0:T(8,128)S(1)} %pad_maximum_fusion), channel_id=1, source_target_pairs={{0,4},{4,8},{8,12},{1,5},{5,9},{9,13},{2,6},{6,10},{10,14},{3,7},{... | collective-permute-start | bytes 3145736 | tf_op jit(solution)/shard_map/ppermute | solution.py:559
  6.9 26.8 %collective-permute-start.1 = (f32[8,256,128]{2,1,0:T(8,128)}, f32[8,256,128]{2,1,0:T(8,128)S(1)}, u32[]{:S(2)}, u32[]{:S(2)}) collective-permute-start(f32[8,256,128]{2,1,0:T(8,128)} %pad_maximum_fusion.1), channel_id=1, source_target_pairs={{4,0},{8,4},{12,8},{5,1},{9,5},{13,9},{6,2},{10,6},{14,10},{7,3},{... | collective-permute-start | bytes 3145736 | tf_op jit(solution)/shard_map/ppermute | solution.py:560
  33.7 1.0 copy-start.3
  34.7 1.0 copy-start.4
  61.7 54.1 %all-to-all-start.2 = ((f32[16,8,32,128]{3,2,1,0:T(8,128)}), f32[16,8,32,128]{3,2,1,0:T(8,128)S(1)}, u32[]{:S(2)}, u32[]{:S(2)}) async-start(f32[16,8,32,128]{3,2,1,0:T(8,128)} %bitcast.33), calls=%async_computation.2 | async-start | bytes 4194304 | tf_op jit(solution)/shard_map/all_to_all | solution.py:577
  115.8 1.3 copy-start.2
  117.1 52.2 %all-to-all-start = ((f32[16,8,32,128]{3,2,1,0:T(8,128)}), f32[16,8,32,128]{3,2,1,0:T(8,128)S(1)}, u32[]{:S(2)}, u32[]{:S(2)}) async-start(f32[16,8,32,128]{3,2,1,0:T(8,128)} %bitcast.30), calls=%async_computation | async-start | bytes 4194304 | tf_op jit(solution)/shard_map/all_to_all | solution.py:577
  169.3 1.3 copy-start.1
  170.7 52.2 %all-to-all-start.3 = ((f32[16,8,32,128]{3,2,1,0:T(8,128)}), f32[16,8,32,128]{3,2,1,0:T(8,128)S(1)}, u32[]{:S(2)}, u32[]{:S(2)}) async-start(f32[16,8,32,128]{3,2,1,0:T(8,128)} %bitcast.31), calls=%async_computation.3 | async-start | bytes 4194304 | tf_op jit(solution)/shard_map/all_to_all | solution.py:588
  222.9 4.8 %copy-start = (f32[16,8,32,128]{3,2,1,0:T(8,128)}, f32[16,8,32,128]{3,2,1,0:T(8,128)S(1)}, u32[]{:S(2)}) copy-start(f32[16,8,32,128]{3,2,1,0:T(8,128)S(1)} %all-to-all-done.3) | copy-start | bytes 6291460
  222.9 52.3 %all-to-all-start.1 = ((f32[16,8,32,128]{3,2,1,0:T(8,128)}), f32[16,8,32,128]{3,2,1,0:T(8,128)}, u32[]{:S(2)}, u32[]{:S(2)}) async-start(f32[16,8,32,128]{3,2,1,0:T(8,128)} %bitcast.32), calls=%async_computation.1 | async-start | bytes 4194304 | tf_op jit(solution)/shard_map/all_to_all | solution.py:588

commit v3 on v2

--- a/solution.py
+++ b/solution.py
@@ -10,6 +10,7 @@
 from jax.experimental.pallas import tpu as pltpu
 from jax.sharding import PartitionSpec as P
 
+
 STEPS = 4
 STEP_SIZE = 1.0 / 6.0
 FLOOR_VALUE = 0.01
@@ -18,6 +19,7 @@
 BLOCK = 16
 PLANES = 2
 VMEM_BYTES = 60 * 1024 * 1024
+MOST_TURNS = 16
 BF = jnp.bfloat16
 F32 = jnp.float32
 
@@ -264,8 +266,15 @@
         out[k] = last[steps + k, inside, :]
 
 
-def spectrum_kernel(depth, volume, table_y, table_x, take_cosine, take_sine, out):
-    width, length, lanes = volume.shape
+def turn(me, slot, count):
+    at = me + slot
+    return jnp.where(at < count, at, at - count)
+
+
+def spectrum_kernel(depth, me, volume, table_y, table_x, take_cosine, take_sine, *rest):
+    width, _, lanes = volume.shape
+    outs = rest if len(rest) == 1 else rest[:-1]
+    slots = len(outs)
     rows = take_cosine.shape[0]
     group = pl.program_id(0)
     for start in range(0, width, 2):
@@ -276,11 +285,43 @@
             part = both[:, k * lanes : (k + 1) * lanes]
             turned = pltpu.roll(part[rows:], lanes // 2, 1)
             value = take_cosine[...] * part[:rows] + take_sine[...] * turned
-            out[pl.ds(group * width + start + k, rows, stride=depth), :] = value
-
-
-def cross_kernel(length_x, start, damping, matches, spectra, table_f, table_i, out, held, weight):
-    slabs, submaps, _, depth, lanes = spectra.shape
+            z = group * width + start + k
+            if slots == 1:
+                outs[0][pl.ds(z, rows, stride=depth), :] = value
+                continue
+            held = rest[-1]
+            each = rows // slots
+            held[(start + k) % 2] = value
+            for slot in range(slots):
+                first = pl.multiple_of(turn(me[0], slot, slots) * each, each)
+                outs[slot][pl.ds(z, each, stride=depth), :] = held[(start + k) % 2, pl.ds(first, each), :]
+
+
+def cross_kernel(length_x, slots, start, me, damping, matches, *refs):
+    sources, refs = refs[:slots], refs[slots:]
+    table_f, table_i = refs[:2]
+    outs, refs = refs[2 : 2 + slots], refs[2 + slots :]
+    held, weight = refs[:2]
+    if slots == 1:
+        spectra, out = sources[0], outs[0]
+        slabs, submaps, _, depth, lanes = spectra.shape
+        piece = lambda i, s: spectra[i, s, 0]
+
+        def put(i, s, value):
+            out[i, s, 0] = value
+
+    else:
+        order = refs[2]
+        depth, lanes = sources[0].shape[1:]
+        submaps = weight.shape[0]
+        slabs = slots // submaps
+        for slot in range(slots):
+            order[turn(me[0], (slots - slot) % slots, slots)] = sources[slot][0]
+        piece = lambda i, s: order[i * submaps + s]
+
+        def put(i, s, value):
+            order[i * submaps + s] = value
+
     length_z = slabs * depth
     half = lanes // 2
     lane = lax.broadcasted_iota(jnp.int32, (length_z, lanes), 1)
@@ -307,7 +348,7 @@
     radius = at_x * at_x + at_y * at_y
 
     for s in range(submaps):
-        column = jnp.concatenate([spectra[i, s, 0] for i in range(slabs)], axis=0)
+        column = jnp.concatenate([piece(i, s) for i in range(slabs)], axis=0)
         high, low = split(column)
         both = dot(table_f[...], jnp.concatenate([high, low, high], axis=0))
         cosine, sine = both[:length_z], both[length_z:]
@@ -345,21 +386,35 @@
         high, low = split(jnp.concatenate([held[4, s], held[5, s]], axis=0))
         back = dot(table_i[...], jnp.concatenate([high, low, high], axis=0))
         for i in range(slabs):
-            out[i, s, 0] = back[i * depth : (i + 1) * depth]
-
-
-def inverse_kernel(depth, rows, *refs):
-    columns, weights, table_x, table_y = refs[:4]
-    before = refs[4] if len(refs) > 5 else None
-    out = refs[-1]
-    width, length, lanes = out.shape
+            put(i, s, back[i * depth : (i + 1) * depth])
+
+    if slots > 1:
+        for slot in range(slots):
+            outs[slot][0] = order[turn(me[0], slot, slots)]
+
+
+def inverse_kernel(depth, rows, slots, added, me, *refs):
+    columns, refs = refs[:slots], refs[slots:]
+    weights, table_x, table_y = refs[:3]
+    before = refs[3] if added else None
+    out = refs[3 + added]
+    each = rows // slots
+    width, _, lanes = out.shape
     half = lanes // 2
     lane = lax.broadcasted_iota(jnp.int32, (rows, lanes), 1)
     sign = jnp.where(lane < half, -1.0, 1.0)
     group = pl.program_id(0)
     sides = []
     for k in range(width):
-        value = columns[pl.ds(group * width + k, rows, stride=depth), :]
+        z = group * width + k
+        if slots == 1:
+            value = columns[0][pl.ds(z, rows, stride=depth), :]
+        else:
+            held = refs[-1]
+            for slot in range(slots):
+                first = pl.multiple_of(turn(me[0], (slots - slot) % slots, slots) * each, each)
+                held[k, pl.ds(first, each), :] = columns[slot][pl.ds(z, each, stride=depth), :]
+            value = held[k]
         turned = pltpu.roll(value, half, 1) * sign
         sides.append(jnp.concatenate([value * weights[...], turned * weights[...]], axis=0))
     high, low = split(jnp.concatenate(sides, axis=1))
@@ -434,19 +489,20 @@
     )(conductance, edge, occ, cls, below, above, inner)
 
 
-def spectrum(volume, tables):
+def spectrum(volume, me, slots, tables):
     depth, length, lanes = volume.shape
     table_y, table_x, take_cosine, take_sine = tables
     rows = take_cosine.shape[0]
     width = math.gcd(depth, 4)
     block = pl.BlockSpec((width, length, lanes), lambda g: (g, 0, 0))
-    out = jax.ShapeDtypeStruct((rows * depth, lanes), F32)
+    out = jax.ShapeDtypeStruct((rows // slots * depth, lanes), F32)
     return pl.pallas_call(
         functools.partial(spectrum_kernel, depth),
-        out_shape=out,
+        out_shape=[out] * slots,
         grid=(depth // width,),
-        in_specs=[block] + [whole_spec()] * 4,
-        out_specs=pl.BlockSpec(out.shape, lambda g: (0, 0)),
+        in_specs=[scalar_spec(), block] + [whole_spec()] * 4,
+        out_specs=[pl.BlockSpec(out.shape, lambda g: (0, 0))] * slots,
+        scratch_shapes=[pltpu.VMEM((2, rows, lanes), F32)] if slots > 1 else [],
         compiler_params=params(),
         cost_estimate=pl.CostEstimate(
             flops=6 * 2 * volume.size * (lanes + 2 * rows),
@@ -454,53 +510,60 @@
             transcendentals=0,
         ),
         name="spectrum",
-    )(volume, table_y, table_x, take_cosine, take_sine)
-
-
-def middle(spectra, start, damping, matches, length_x, tables):
-    slabs, submaps, rows, depth, lanes = spectra.shape
+    )(me, volume, table_y, table_x, take_cosine, take_sine)
+
+
+def middle(sources, dims, start, me, damping, matches, length_x, tables):
+    slabs, submaps, rows, depth, lanes = dims
     length_z = slabs * depth
-    block = pl.BlockSpec((slabs, submaps, 1, depth, lanes), lambda r: (0, 0, r, 0, 0))
+    slots = len(sources)
+    size = math.prod(dims)
+    scratch = [
+        pltpu.VMEM((6, submaps, length_z, lanes), F32),
+        pltpu.VMEM((submaps, length_z, lanes), F32),
+    ]
+    if slots == 1:
+        block = pl.BlockSpec((slabs, submaps, 1, depth, lanes), lambda r: (0, 0, r, 0, 0))
+    else:
+        block = pl.BlockSpec((1, depth, lanes), lambda r: (r, 0, 0))
+        scratch.append(pltpu.VMEM((slots, depth, lanes), F32))
     return pl.pallas_call(
-        functools.partial(cross_kernel, length_x),
-        out_shape=jax.ShapeDtypeStruct(spectra.shape, F32),
+        functools.partial(cross_kernel, length_x, slots),
+        out_shape=[jax.ShapeDtypeStruct(part.shape, F32) for part in sources],
         grid=(rows,),
-        in_specs=[scalar_spec()] * 3 + [block] + [whole_spec()] * 2,
-        out_specs=block,
-        scratch_shapes=[
-            pltpu.VMEM((6, submaps, length_z, lanes), F32),
-            pltpu.VMEM((submaps, length_z, lanes), F32),
-        ],
+        in_specs=[scalar_spec()] * 4 + [block] * slots + [whole_spec()] * 2,
+        out_specs=[block] * slots,
+        scratch_shapes=scratch,
         compiler_params=params(),
         cost_estimate=pl.CostEstimate(
-            flops=6 * 2 * spectra.size * length_z * 2,
-            bytes_accessed=spectra.size * 8,
-            transcendentals=spectra.size,
+            flops=6 * 2 * size * length_z * 2, bytes_accessed=size * 8, transcendentals=size
         ),
         name="middle",
-    )(start, damping, matches, spectra, *tables)
-
-
-def inverse(columns, before, depth, length, tables):
-    total, lanes = columns.shape
-    rows = total // depth
+    )(start, me, damping, matches, *sources, *tables)
+
+
+def inverse(columns, me, before, depth, length, tables):
+    slots = len(columns)
+    lanes = columns[0].shape[1]
+    rows = slots * columns[0].shape[0] // depth
     width = 2
     block = pl.BlockSpec((width, length, lanes), lambda g: (g, 0, 0))
     extra = [] if before is None else [before]
     return pl.pallas_call(
-        functools.partial(inverse_kernel, depth, rows),
+        functools.partial(inverse_kernel, depth, rows, slots, len(extra)),
         out_shape=jax.ShapeDtypeStruct((depth, length, lanes), F32),
         grid=(depth // width,),
-        in_specs=[whole_spec()] * 4 + [block] * len(extra),
+        in_specs=[scalar_spec()] + [whole_spec()] * (slots + 3) + [block] * len(extra),
         out_specs=block,
+        scratch_shapes=[pltpu.VMEM((width, rows, lanes), F32)] if slots > 1 else [],
         compiler_params=params(),
         cost_estimate=pl.CostEstimate(
             flops=6 * 2 * depth * length * lanes * rows,
-            bytes_accessed=columns.size * 4 + depth * length * lanes * 4 * (1 + len(extra)),
+            bytes_accessed=rows * depth * lanes * 4 + depth * length * lanes * 4 * (1 + len(extra)),
             transcendentals=0,
         ),
         name="inverse",
-    )(columns, *tables, *extra)
+    )(me, *columns, *tables, *extra)
 
 
 def ends(size):
@@ -565,32 +628,54 @@
     else:
         volume = diffuse_plain(occ, cls, conductance)
 
-    me = lax.axis_index(AXES)
+    me = lax.axis_index(AXES).astype(jnp.int32).reshape(1)
     straight = depth % 8 == 0
-    result = None
+    span = length // chunks
+
+    def turns(chunk):
+        return chunk % 2 == 1 and rows % 8 == 0 and devices <= MOST_TURNS
+
+    def exchange(parts):
+        if len(parts) == 1:
+            part = parts[0].reshape(devices, rows, depth, lanes)
+            return [lax.all_to_all(part, AXES, 0, 0, tiled=True)]
+        moved = [parts[0]]
+        for slot in range(1, devices):
+            pairs_of = [(i, (i + slot) % devices) for i in range(devices)]
+            moved.append(lax.ppermute(parts[slot], AXES, pairs_of))
+        return moved
+
+    dims = (slabs, pairs, rows, depth, lanes)
     backs = []
     for chunk in range(chunks):
-        inside = slice(chunk * (length // chunks), (chunk + 1) * (length // chunks))
+        inside = slice(chunk * span, (chunk + 1) * span)
         table_x = left_table_stack(cos_x[inside], sin_x[inside])
-        part = spectrum(volume, (table_y, table_x, take_cosine[inside], take_sine[inside]))
-        part = part.reshape(devices, rows, depth, lanes)
-        part = lax.all_to_all(part, AXES, 0, 0, tiled=True)
-        part = part.reshape(slabs, pairs, rows, depth, lanes)
+        slots = devices if turns(chunk) else 1
+        parts = spectrum(
+            volume, me, slots, (table_y, table_x, take_cosine[inside], take_sine[inside])
+        )
+        parts = exchange(parts)
+        start = chunk * span + me * rows
+        if slots > 1:
+            parts = [part.reshape(rows, depth, lanes) for part in parts]
+            parts = middle(parts, dims, start, me, damping, matches, length, middle_tables)
+            backs.append([part.reshape(rows * depth, lanes) for part in parts])
+            continue
+        part = parts[0].reshape(dims)
+        shape = dims
         if not straight:
-            part = part.transpose(1, 2, 0, 3, 4).reshape(1, pairs, rows, length_z, lanes)
-        start = (chunk * (length // chunks) + me * rows).astype(jnp.int32).reshape(1)
-        part = middle(part, start, damping, matches, length, middle_tables)
+            shape = (1, pairs, rows, length_z, lanes)
+            part = part.transpose(1, 2, 0, 3, 4).reshape(shape)
+        part = middle([part], shape, start, me, damping, matches, length, middle_tables)[0]
         if not straight:
             part = part.reshape(pairs, rows, slabs, depth, lanes).transpose(2, 0, 1, 3, 4)
-        part = part.reshape(devices, rows, depth, lanes)
-        backs.append(part)
+        backs.append([part])
+    result = None
     for chunk in range(chunks):
-        part = lax.all_to_all(backs[chunk], AXES, 0, 0, tiled=True)
-        inside = slice(chunk * (length // chunks), (chunk + 1) * (length // chunks))
+        parts = [part.reshape(-1, lanes) for part in exchange(backs[chunk])]
+        inside = slice(chunk * span, (chunk + 1) * span)
         table = left_table(np.concatenate([cos_x[:, inside], sin_x[:, inside]], axis=1))
-        result = inverse(
-            part.reshape(-1, lanes), result, depth, length, (weights[inside], table, table_back)
-        )
+        result = inverse(parts, me, result, depth, length, (weights[inside], table, table_back))
     return result[None]
 
 
@@ -607,4 +692,5 @@
         P("groups"),
     )
     out_specs = P(("groups", "pair"), "slab", None, None)
+
     return jax.shard_map(local, mesh=mesh, in_specs=in_specs, out_specs=out_specs, check_vma=False)

time: 292 us -> 330 us (1.13)
  the two profiles are of different devices: /device:TPU:11 before, /device:TPU:0 now
where the time goes in v3:
time: 330 us; the launch traced here: 329 us
  Pallas kernels  121 us (37%)
  waiting for transfers between devices  106 us (32%)
  starting transfers between devices  92.8 us (28%)
  local copies, waits for them, and re-layouts  6.35 us (2%)
    ppermute x30, starting transfers between devices, exchange(): moved.append(lax.ppermute(parts[slot], AXES, pairs_of))  68.5 us
    ppermute x30, waiting for transfers between devices, exchange(): moved.append(lax.ppermute(parts[slot], AXES, pairs_of))  64.3 us
    all_to_all x2, waiting for transfers between devices, exchange(): return [lax.all_to_all(part, AXES, 0, 0, tiled=True)]  41 us
    pallas_call x2, Pallas kernels, middle(): pl.pallas_call(functools.partial(cross_kernel, length_x, slots), out_shap...  30.4 us
    pallas_call x2, Pallas kernels, inverse(): pl.pallas_call(functools.partial(inverse_kernel, depth, rows, slots, len(...  29.6 us
    pallas_call x1, Pallas kernels, diffuse_inner(): pl.pallas_call(functools.partial(inner_kernel, STEPS), out_shape=jax.Shap...  24 us
    pallas_call x2, Pallas kernels, spectrum(): pl.pallas_call(functools.partial(spectrum_kernel, depth), out_shape=[out]...  21.4 us
    all_to_all x2, starting transfers between devices, exchange(): return [lax.all_to_all(part, AXES, 0, 0, tiled=True)]  18 us
  transfers between devices with their start and end apart: 34, of which 12 were waited for; matrix products, arithmetic and copies ran while one was open for 1% of the time, Pallas kernels for 19%

profile of v3, /device:TPU:0, one launch (start us, length us, event | category | flops | bytes accessed | tf_op | source)
XLA Modules:
  0.0 329.4 jit_solution(11088508281887358581)
XLA Ops:
  0.0 1.3 slice_bitcast_fusion
  1.3 1.3 convert_bitcast_fusion
  2.6 5.0 %collective-permute-start = (f32[8,256,128]{2,1,0:T(8,128)S(1)}, f32[8,256,128]{2,1,0:T(8,128)S(1)}, u32[]{:S(2)}, u32[]{:S(2)}) collective-permute-start(f32[8,256,128]{2,1,0:T(8,128)S(1)} %pad_maximum_fusion), channel_id=1, source_target_pairs={{0,4},{4,8},{8,12},{1,5},{5,9},{9,13},{2,6},{6,10},{10,14},{3,7},{... | collective-permute-start | bytes 3145736 | tf_op jit(solution)/shard_map/ppermute | solution.py:622
  7.7 1.1 pad_maximum_fusion.1
  8.8 1.3 collective-permute-start.1
  10.1 24.0 %inner.1._ = f32[32,256,128]{2,1,0:T(8,128)} custom-call(f32[8]{0:T(128)} %conductance.3, f32[32,256,128]{2,1,0:T(8,128)} %bitcast.50, s32[32,256,128]{2,1,0:T(8,128)} %bitcast.52), custom_call_target="tpu_custom_call" | custom-call | flops 83886080 | bytes 12582912 | tf_op jit(solution)/shard_map/inner/pallas_call | solution.py:453
  35.8 1.0 copy-done.3
  36.8 15.4 %outer.1.volume = f32[32,256,128]{2,1,0:T(8,128)} custom-call(f32[8]{0:T(128)} %conductance.3, s32[2]{0:T(128)} %add_convert_fusion.edge, f32[32,256,128]{2,1,0:T(8,128)} %bitcast.51, s32[32,256,128]{2,1,0:T(8,128)} %bitcast.53, f32[8,256,128]{2,1,0:T(8,128)} %copy-done.2, f32[8,256,128]{2,1,0:T(8,128)} %copy-done.3, ...), custom_call_target="tpu_custom_call", output_to_operand_aliasing={{}: (6, {})} | custom-call | flops 41943040 | bytes 6291456 | tf_op jit(solution)/shard_map/outer/pallas_call | solution.py:476
  52.2 10.3 %spectrum.3 = f32[4096,128]{1,0:T(8,128)} custom-call(s32[1]{0:T(128)} %bitcast.me, f32[32,256,128]{2,1,0:T(8,128)} %outer.1.volume, bf16[256,256]{1,0:T(8,128)(2,1)} %constant.45.clone.table_y, bf16[256,768]{1,0:T(8,128)(2,1)} %constant.46.clone.table_x, f32[128,128]{1,0:T(8,128)} %constant.47.clone.take_cosine, f32[128,128]{1,0:T(8,128)} %constant.48.clone.take_sine), custom_call_target="tpu_custom_call" | custom-call | flops 4831838208 | bytes 6291456 | tf_op jit(solution)/shard_map/spectrum/pallas_call | solution.py:499
  62.5 7.0 %all-to-all-start = ((f32[16,8,32,128]{3,2,1,0:T(8,128)}), f32[16,8,32,128]{3,2,1,0:T(8,128)S(1)}, u32[]{:S(2)}, u32[]{:S(2)}) async-start(f32[16,8,32,128]{3,2,1,0:T(8,128)} %bitcast.57), calls=%async_computation | async-start | bytes 4194304 | tf_op jit(solution)/shard_map/all_to_all | solution.py:641
  69.5 41.0 %all-to-all-done = f32[16,8,32,128]{3,2,1,0:T(8,128)S(1)} async-done(((f32[16,8,32,128]{3,2,1,0:T(8,128)}), f32[16,8,32,128]{3,2,1,0:T(8,128)S(1)}, u32[]{:S(2)}, u32[]{:S(2)}) %all-to-all-start) | async-done | bytes 2097184 | tf_op jit(solution)/shard_map/all_to_all | solution.py:641
  110.4 1.3 copy-done.1
  111.8 14.7 %middle.3 = f32[4,4,8,32,128]{4,3,2,1,0:T(8,128)} custom-call(s32[1]{0:T(128)S(6)} %mul.8.start, s32[1]{0:T(128)} %bitcast.me, f32[4]{0:T(128)} %damping.3, s32[4]{0:T(128)} %matches.3, f32[4,4,8,32,128]{4,3,2,1,0:T(8,128)} %bitcast.56, bf16[256,384]{1,0:T(8,128)(2,1)} %constant.49.clone.refs_16_.refs_1_, bf16[128,768]{1,0:T(8,128)(2,1)} %constant.50.clone.refs_17_.refs_2_), custom_call_target="tpu_custom_call" | custom-call | flops 1610612736 | bytes 4194304 | tf_op jit(solution)/shard_map/middle/pallas_call | solution.py:530
  126.4 11.0 %all-to-all-start.1 = ((f32[16,8,32,128]{3,2,1,0:T(8,128)}), f32[16,8,32,128]{3,2,1,0:T(8,128)S(1)}, u32[]{:S(2)}, u32[]{:S(2)}) async-start(f32[16,8,32,128]{3,2,1,0:T(8,128)} %bitcast.55), calls=%async_computation.1 | async-start | bytes 4194304 | tf_op jit(solution)/shard_map/all_to_all | solution.py:641
  137.5 11.1 %spectrum.2 = (f32[256,128]{1,0:T(8,128)}, f32[256,128]{1,0:T(8,128)}, f32[256,128]{1,0:T(8,128)}, f32[256,128]{1,0:T(8,128)}, f32[256,128]{1,0:T(8,128)}, /*ind...) custom-call(s32[1]{0:T(128)} %bitcast.me, ...), custom_call_target="tpu_custom_call" | custom-call | flops 4831838208 | bytes 6291456 | tf_op jit(solution)/shard_map/spectrum/pallas_call | solution.py:499
  148.9 1.6 collective-permute-start.3
  150.6 2.3 collective-permute-start.4
  152.8 1.5 collective-permute-start.5
  154.4 25.1 %collective-permute-done.2 = f32[256,128]{1,0:T(8,128)S(1)} collective-permute-done((f32[256,128]{1,0:T(8,128)}, f32[256,128]{1,0:T(8,128)S(1)}, u32[]{:S(2)}, u32[]{:S(2)}) %collective-permute-start.2) | collective-permute-done | bytes 131104 | tf_op jit(solution)/shard_map/ppermute | solution.py:645
  179.5 1.1 collective-permute-done.3
  180.7 14.5 %collective-permute-start.8 = (f32[256,128]{1,0:T(8,128)}, f32[256,128]{1,0:T(8,128)S(1)}, u32[]{:S(2)}, u32[]{:S(2)}) collective-permute-start(f32[256,128]{1,0:T(8,128)} %get-tuple-element.44), channel_id=1, source_target_pairs={{0,7},{1,8},{2,9},{3,10},{4,11},{5,12},{6,13},{7,14},{8,15},{9,0},... | collective-permute-start | bytes 393224 | tf_op jit(solution)/shard_map/ppermute | solution.py:645
  195.7 2.3 collective-permute-start.10
  198.0 12.9 %collective-permute-done.6 = f32[256,128]{1,0:T(8,128)S(1)} collective-permute-done((f32[256,128]{1,0:T(8,128)}, f32[256,128]{1,0:T(8,128)S(1)}, u32[]{:S(2)}, u32[]{:S(2)}) %collective-permute-start.6) | collective-permute-done | bytes 131104 | tf_op jit(solution)/shard_map/ppermute | solution.py:645
  210.8 1.1 collective-permute-done.7
  212.0 2.4 collective-permute-start.12
  214.4 8.4 %collective-permute-start.13 = (f32[256,128]{1,0:T(8,128)}, f32[256,128]{1,0:T(8,128)S(1)}, u32[]{:S(2)}, u32[]{:S(2)}) collective-permute-start(f32[256,128]{1,0:T(8,128)} %get-tuple-element.49), channel_id=1, source_target_pairs={{0,12},{1,13},{2,14},{3,15},{4,0},{5,1},{6,2},{7,3},{8,4},{9,5},{1... | collective-permute-start | bytes 393224 | tf_op jit(solution)/shard_map/ppermute | solution.py:645
  222.8 1.3 collective-permute-start.14
  224.1 3.4 %collective-permute-start.15 = (f32[256,128]{1,0:T(8,128)}, f32[256,128]{1,0:T(8,128)S(1)}, u32[]{:S(2)}, u32[]{:S(2)}) collective-permute-start(f32[256,128]{1,0:T(8,128)} %get-tuple-element.51), channel_id=1, source_target_pairs={{0,14},{1,15},{2,0},{3,1},{4,2},{5,3},{6,4},{7,5},{8,6},{9,7},{10,... | collective-permute-start | bytes 393224 | tf_op jit(solution)/shard_map/ppermute | solution.py:645
  227.5 3.1 collective-permute-start.16
  230.6 2.6 collective-permute-done.15
  233.1 1.0 collective-permute-done.16
  234.7 15.7 %middle.2 = (f32[8,32,128]{2,1,0:T(8,128)}, f32[8,32,128]{2,1,0:T(8,128)}, f32[8,32,128]{2,1,0:T(8,128)}, f32[8,32,128]{2,1,0:T(8,128)}, f32[8,32,128]{2,1,0:T(8...) custom-call(s32[1]{0:T(128)S(6)} %add.7.start, ...), custom_call_target="tpu_custom_call" | custom-call | flops 1610612736 | bytes 4194304 | tf_op jit(solution)/shard_map/middle/pallas_call | solution.py:530
  250.5 0.9 collective-permute-start.17
  251.4 1.2 collective-permute-start.18
  252.6 2.8 collective-permute-start.20
  255.3 1.0 collective-permute-start.21
  256.3 1.5 collective-permute-done.17.refs_1_
  257.8 2.9 collective-permute-done.18.refs_2_
  261.1 4.6 %collective-permute-start.25 = (f32[256,128]{1,0:T(8,128)}, f32[256,128]{1,0:T(8,128)S(1)}, u32[]{:S(2)}, u32[]{:S(2)}) collective-permute-start(f32[256,128]{1,0:T(8,128)} %bitcast.72), channel_id=1, source_target_pairs={{0,9},{1,10},{2,11},{3,12},{4,13},{5,14},{6,15},{7,0},{8,1},{9,2},... | collective-permute-start | bytes 393224 | tf_op jit(solution)/shard_map/ppermute | solution.py:645
  265.7 15.9 %collective-permute-done.21.refs_5_ = f32[256,128]{1,0:T(8,128)S(1)} collective-permute-done((f32[256,128]{1,0:T(8,128)}, f32[256,128]{1,0:T(8,128)S(1)}, u32[]{:S(2)}, u32[]{:S(2)}) %collective-permute-start.21) | collective-permute-done | bytes 131104 | tf_op jit(solution)/shard_map/ppermute | solution.py:645
  281.8 2.0 collective-permute-start.27
  283.8 2.9 collective-permute-start.28
  286.8 5.3 %collective-permute-start.29 = (f32[256,128]{1,0:T(8,128)}, f32[256,128]{1,0:T(8,128)}, u32[]{:S(2)}, u32[]{:S(2)}) collective-permute-start(f32[256,128]{1,0:T(8,128)} %bitcast.62), channel_id=1, source_target_pairs={{0,13},{1,14},{2,15},{3,0},{4,1},{5,2},{6,3},{7,4},{8,5},{9,6},{10... | collective-permute-start | bytes 393224 | tf_op jit(solution)/shard_map/ppermute | solution.py:645
  292.1 4.5 %collective-permute-start.30 = (f32[256,128]{1,0:T(8,128)}, f32[256,128]{1,0:T(8,128)}, u32[]{:S(2)}, u32[]{:S(2)}) collective-permute-start(f32[256,128]{1,0:T(8,128)} %bitcast.60), channel_id=1, source_target_pairs={{0,14},{1,15},{2,0},{3,1},{4,2},{5,3},{6,4},{7,5},{8,6},{9,7},{10,... | collective-permute-start | bytes 393224 | tf_op jit(solution)/shard_map/ppermute | solution.py:645
  296.6 1.2 collective-permute-start.31
  297.8 1.3 copy-done
  299.2 13.0 %inverse.2.refs_19_ = f32[32,256,128]{2,1,0:T(8,128)} custom-call(s32[1]{0:T(128)} %bitcast.me, f32[4096,128]{1,0:T(8,128)} %bitcast.54, f32[128,128]{1,0:T(8,128)} %constant.54.clone.refs_1_, bf16[256,768]{1,0:T(8,128)(2,1)} %constant.55.clone.refs_2_, bf16[256,256]{1,0:T(8,128)(2,1)} %constant.56.clone.refs_3_.refs_18_), custom_call_target="tpu_custom_call" | custom-call | flops 1610612736 | bytes 6291456 | tf_op jit(solution)/shard_map/inverse/pallas_call | solution.py:552
  312.8 16.5 %inverse.3 = f32[32,256,128]{2,1,0:T(8,128)} custom-call(s32[1]{0:T(128)} %bitcast.me, f32[256,128]{1,0:T(8,128)} %bitcast.58, f32[256,128]{1,0:T(8,128)} %copy-done.4, f32[256,128]{1,0:T(8,128)} %copy-done.5, f32[256,128]{1,0:T(8,128)} %copy-done.6, f32[256,128]{1,0:T(8,128)} %copy-done.7, f32[256,128]{1,0:T(8,128)} %copy-done.8, f32[256,128]{1,0:T(8,128)} %copy-done.9, ...), custom_call_target="tpu_custom_call" | custom-call | flops 1610612736 | bytes 10485760 | tf_op jit(solution)/shard_map/inverse/pallas_call | solution.py:552
  (93 shorter events, 4.5 us)
Async XLA Ops:
  2.6 32.1 %collective-permute-start = (f32[8,256,128]{2,1,0:T(8,128)S(1)}, f32[8,256,128]{2,1,0:T(8,128)S(1)}, u32[]{:S(2)}, u32[]{:S(2)}) collective-permute-start(f32[8,256,128]{2,1,0:T(8,128)S(1)} %pad_maximum_fusion), channel_id=1, source_target_pairs={{0,4},{4,8},{8,12},{1,5},{5,9},{9,13},{2,6},{6,10},{10,14},{3,7},{... | collective-permute-start | bytes 3145736 | tf_op jit(solution)/shard_map/ppermute | solution.py:622
  8.8 26.7 %collective-permute-start.1 = (f32[8,256,128]{2,1,0:T(8,128)}, f32[8,256,128]{2,1,0:T(8,128)S(1)}, u32[]{:S(2)}, u32[]{:S(2)}) collective-permute-start(f32[8,256,128]{2,1,0:T(8,128)} %pad_maximum_fusion.1), channel_id=1, source_target_pairs={{4,0},{8,4},{12,8},{5,1},{9,5},{13,9},{6,2},{10,6},{14,10},{7,3},{... | collective-permute-start | bytes 3145736 | tf_op jit(solution)/shard_map/ppermute | solution.py:623
  62.5 48.0 %all-to-all-start = ((f32[16,8,32,128]{3,2,1,0:T(8,128)}), f32[16,8,32,128]{3,2,1,0:T(8,128)S(1)}, u32[]{:S(2)}, u32[]{:S(2)}) async-start(f32[16,8,32,128]{3,2,1,0:T(8,128)} %bitcast.57), calls=%async_computation | async-start | bytes 4194304 | tf_op jit(solution)/shard_map/all_to_all | solution.py:641
  126.4 171.4 %all-to-all-start.1 = ((f32[16,8,32,128]{3,2,1,0:T(8,128)}), f32[16,8,32,128]{3,2,1,0:T(8,128)S(1)}, u32[]{:S(2)}, u32[]{:S(2)}) async-start(f32[16,8,32,128]{3,2,1,0:T(8,128)} %bitcast.55), calls=%async_computation.1 | async-start | bytes 4194304 | tf_op jit(solution)/shard_map/all_to_all | solution.py:641
  148.5 31.0 %collective-permute-start.2 = (f32[256,128]{1,0:T(8,128)}, f32[256,128]{1,0:T(8,128)S(1)}, u32[]{:S(2)}, u32[]{:S(2)}) collective-permute-start(f32[256,128]{1,0:T(8,128)} %get-tuple-element.38), channel_id=1, source_target_pairs={{0,1},{1,2},{2,3},{3,4},{4,5},{5,6},{6,7},{7,8},{8,9},{9,10},{10,1... | collective-permute-start | bytes 393224 | tf_op jit(solution)/shard_map/ppermute | solution.py:645
  148.9 31.7 %collective-permute-start.3 = (f32[256,128]{1,0:T(8,128)}, f32[256,128]{1,0:T(8,128)S(1)}, u32[]{:S(2)}, u32[]{:S(2)}) collective-permute-start(f32[256,128]{1,0:T(8,128)} %get-tuple-element.39), channel_id=1, source_target_pairs={{0,2},{1,3},{2,4},{3,5},{4,6},{5,7},{6,8},{7,9},{8,10},{9,11},{10,... | collective-permute-start | bytes 393224 | tf_op jit(solution)/shard_map/ppermute | solution.py:645
  150.6 44.6 %collective-permute-start.4 = (f32[256,128]{1,0:T(8,128)}, f32[256,128]{1,0:T(8,128)S(1)}, u32[]{:S(2)}, u32[]{:S(2)}) collective-permute-start(f32[256,128]{1,0:T(8,128)} %get-tuple-element.40), channel_id=1, source_target_pairs={{0,3},{1,4},{2,5},{3,6},{4,7},{5,8},{6,9},{7,10},{8,11},{9,12},{10... | collective-permute-start | bytes 393224 | tf_op jit(solution)/shard_map/ppermute | solution.py:645
  152.8 42.8 %collective-permute-start.5 = (f32[256,128]{1,0:T(8,128)}, f32[256,128]{1,0:T(8,128)S(1)}, u32[]{:S(2)}, u32[]{:S(2)}) collective-permute-start(f32[256,128]{1,0:T(8,128)} %get-tuple-element.41), channel_id=1, source_target_pairs={{0,4},{1,5},{2,6},{3,7},{4,8},{5,9},{6,10},{7,11},{8,12},{9,13},{1... | collective-permute-start | bytes 393224 | tf_op jit(solution)/shard_map/ppermute | solution.py:645
  154.3 56.5 %collective-permute-start.6 = (f32[256,128]{1,0:T(8,128)}, f32[256,128]{1,0:T(8,128)S(1)}, u32[]{:S(2)}, u32[]{:S(2)}) collective-permute-start(f32[256,128]{1,0:T(8,128)} %get-tuple-element.42), channel_id=1, source_target_pairs={{0,5},{1,6},{2,7},{3,8},{4,9},{5,10},{6,11},{7,12},{8,13},{9,14},{... | collective-permute-start | bytes 393224 | tf_op jit(solution)/shard_map/ppermute | solution.py:645
  179.5 54.6 %copy-start.15 = (f32[256,128]{1,0:T(8,128)}, f32[256,128]{1,0:T(8,128)S(1)}, u32[]{:S(2)}) copy-start(f32[256,128]{1,0:T(8,128)S(1)} %collective-permute-done.2) | copy-start | bytes 393220
  179.5 32.4 %collective-permute-start.7 = (f32[256,128]{1,0:T(8,128)}, f32[256,128]{1,0:T(8,128)S(1)}, u32[]{:S(2)}, u32[]{:S(2)}) collective-permute-start(f32[256,128]{1,0:T(8,128)} %get-tuple-element.43), channel_id=1, source_target_pairs={{0,6},{1,7},{2,8},{3,9},{4,10},{5,11},{6,12},{7,13},{8,14},{9,15},... | collective-permute-start | bytes 393224 | tf_op jit(solution)/shard_map/ppermute | solution.py:645
  180.7 53.4 %copy-start.16 = (f32[256,128]{1,0:T(8,128)}, f32[256,128]{1,0:T(8,128)S(1)}, u32[]{:S(2)}) copy-start(f32[256,128]{1,0:T(8,128)S(1)} %collective-permute-done.3) | copy-start | bytes 393220
  180.7 33.7 %collective-permute-start.8 = (f32[256,128]{1,0:T(8,128)}, f32[256,128]{1,0:T(8,128)S(1)}, u32[]{:S(2)}, u32[]{:S(2)}) collective-permute-start(f32[256,128]{1,0:T(8,128)} %get-tuple-element.44), channel_id=1, source_target_pairs={{0,7},{1,8},{2,9},{3,10},{4,11},{5,12},{6,13},{7,14},{8,15},{9,0},... | collective-permute-start | bytes 393224 | tf_op jit(solution)/shard_map/ppermute | solution.py:645
  195.2 38.9 %copy-start.17 = (f32[256,128]{1,0:T(8,128)}, f32[256,128]{1,0:T(8,128)S(1)}, u32[]{:S(2)}) copy-start(f32[256,128]{1,0:T(8,128)S(1)} %collective-permute-done.4) | copy-start | bytes 393220
  195.2 27.6 %collective-permute-start.9 = (f32[256,128]{1,0:T(8,128)}, f32[256,128]{1,0:T(8,128)S(1)}, u32[]{:S(2)}, u32[]{:S(2)}) collective-permute-start(f32[256,128]{1,0:T(8,128)} %get-tuple-element.45), channel_id=1, source_target_pairs={{0,8},{1,9},{2,10},{3,11},{4,12},{5,13},{6,14},{7,15},{8,0},{9,1},... | collective-permute-start | bytes 393224 | tf_op jit(solution)/shard_map/ppermute | solution.py:645
  195.7 38.4 %copy-start.18 = (f32[256,128]{1,0:T(8,128)}, f32[256,128]{1,0:T(8,128)S(1)}, u32[]{:S(2)}) copy-start(f32[256,128]{1,0:T(8,128)S(1)} %collective-permute-done.5) | copy-start | bytes 393220
  195.7 28.4 %collective-permute-start.10 = (f32[256,128]{1,0:T(8,128)}, f32[256,128]{1,0:T(8,128)S(1)}, u32[]{:S(2)}, u32[]{:S(2)}) collective-permute-start(f32[256,128]{1,0:T(8,128)} %get-tuple-element.46), channel_id=1, source_target_pairs={{0,9},{1,10},{2,11},{3,12},{4,13},{5,14},{6,15},{7,0},{8,1},{9,2},... | collective-permute-start | bytes 393224 | tf_op jit(solution)/shard_map/ppermute | solution.py:645
  210.8 23.3 %copy-start.19 = (f32[256,128]{1,0:T(8,128)}, f32[256,128]{1,0:T(8,128)S(1)}, u32[]{:S(2)}) copy-start(f32[256,128]{1,0:T(8,128)S(1)} %collective-permute-done.6) | copy-start | bytes 393220
  210.8 16.6 %collective-permute-start.11 = (f32[256,128]{1,0:T(8,128)}, f32[256,128]{1,0:T(8,128)S(1)}, u32[]{:S(2)}, u32[]{:S(2)}) collective-permute-start(f32[256,128]{1,0:T(8,128)} %get-tuple-element.47), channel_id=1, source_target_pairs={{0,10},{1,11},{2,12},{3,13},{4,14},{5,15},{6,0},{7,1},{8,2},{9,3},... | collective-permute-start | bytes 393224 | tf_op jit(solution)/shard_map/ppermute | solution.py:645
  212.0 22.1 %copy-start.20 = (f32[256,128]{1,0:T(8,128)}, f32[256,128]{1,0:T(8,128)S(1)}, u32[]{:S(2)}) copy-start(f32[256,128]{1,0:T(8,128)S(1)} %collective-permute-done.7) | copy-start | bytes 393220
  212.0 18.5 %collective-permute-start.12 = (f32[256,128]{1,0:T(8,128)}, f32[256,128]{1,0:T(8,128)S(1)}, u32[]{:S(2)}, u32[]{:S(2)}) collective-permute-start(f32[256,128]{1,0:T(8,128)} %get-tuple-element.48), channel_id=1, source_target_pairs={{0,11},{1,12},{2,13},{3,14},{4,15},{5,0},{6,1},{7,2},{8,3},{9,4},{... | collective-permute-start | bytes 393224 | tf_op jit(solution)/shard_map/ppermute | solution.py:645
  214.4 16.1 %collective-permute-start.13 = (f32[256,128]{1,0:T(8,128)}, f32[256,128]{1,0:T(8,128)S(1)}, u32[]{:S(2)}, u32[]{:S(2)}) collective-permute-start(f32[256,128]{1,0:T(8,128)} %get-tuple-element.49), channel_id=1, source_target_pairs={{0,12},{1,13},{2,14},{3,15},{4,0},{5,1},{6,2},{7,3},{8,4},{9,5},{1... | collective-permute-start | bytes 393224 | tf_op jit(solution)/shard_map/ppermute | solution.py:645
  222.8 7.7 %collective-permute-start.14 = (f32[256,128]{1,0:T(8,128)}, f32[256,128]{1,0:T(8,128)S(1)}, u32[]{:S(2)}, u32[]{:S(2)}) collective-permute-start(f32[256,128]{1,0:T(8,128)} %get-tuple-element.50), channel_id=1, source_target_pairs={{0,13},{1,14},{2,15},{3,0},{4,1},{5,2},{6,3},{7,4},{8,5},{9,6},{10... | collective-permute-start | bytes 393224 | tf_op jit(solution)/shard_map/ppermute | solution.py:645
  224.1 9.0 %collective-permute-start.15 = (f32[256,128]{1,0:T(8,128)}, f32[256,128]{1,0:T(8,128)S(1)}, u32[]{:S(2)}, u32[]{:S(2)}) collective-permute-start(f32[256,128]{1,0:T(8,128)} %get-tuple-element.51), channel_id=1, source_target_pairs={{0,14},{1,15},{2,0},{3,1},{4,2},{5,3},{6,4},{7,5},{8,6},{9,7},{10,... | collective-permute-start | bytes 393224 | tf_op jit(solution)/shard_map/ppermute | solution.py:645
  227.5 6.6 %collective-permute-start.16 = (f32[256,128]{1,0:T(8,128)}, f32[256,128]{1,0:T(8,128)S(1)}, u32[]{:S(2)}, u32[]{:S(2)}) collective-permute-start(f32[256,128]{1,0:T(8,128)} %get-tuple-element.52), channel_id=1, source_target_pairs={{0,15},{1,0},{2,1},{3,2},{4,3},{5,4},{6,5},{7,6},{8,7},{9,8},{10,9... | collective-permute-start | bytes 393224 | tf_op jit(solution)/shard_map/ppermute | solution.py:645
  250.5 7.4 %collective-permute-start.17 = (f32[256,128]{1,0:T(8,128)}, f32[256,128]{1,0:T(8,128)S(1)}, u32[]{:S(2)}, u32[]{:S(2)}) collective-permute-start(f32[256,128]{1,0:T(8,128)} %bitcast.88), channel_id=1, source_target_pairs={{0,1},{1,2},{2,3},{3,4},{4,5},{5,6},{6,7},{7,8},{8,9},{9,10},{10,1... | collective-permute-start | bytes 393224 | tf_op jit(solution)/shard_map/ppermute | solution.py:645
  251.4 9.3 %collective-permute-start.18 = (f32[256,128]{1,0:T(8,128)}, f32[256,128]{1,0:T(8,128)S(1)}, u32[]{:S(2)}, u32[]{:S(2)}) collective-permute-start(f32[256,128]{1,0:T(8,128)} %bitcast.86), channel_id=1, source_target_pairs={{0,2},{1,3},{2,4},{3,5},{4,6},{5,7},{6,8},{7,9},{8,10},{9,11},{10,... | collective-permute-start | bytes 393224 | tf_op jit(solution)/shard_map/ppermute | solution.py:645
  252.6 8.2 %collective-permute-start.19 = (f32[256,128]{1,0:T(8,128)}, f32[256,128]{1,0:T(8,128)S(1)}, u32[]{:S(2)}, u32[]{:S(2)}) collective-permute-start(f32[256,128]{1,0:T(8,128)} %bitcast.84), channel_id=1, source_target_pairs={{0,3},{1,4},{2,5},{3,6},{4,7},{5,8},{6,9},{7,10},{8,11},{9,12},{10... | collective-permute-start | bytes 393224 | tf_op jit(solution)/shard_map/ppermute | solution.py:645
  252.6 8.5 %collective-permute-start.20 = (f32[256,128]{1,0:T(8,128)}, f32[256,128]{1,0:T(8,128)S(1)}, u32[]{:S(2)}, u32[]{:S(2)}) collective-permute-start(f32[256,128]{1,0:T(8,128)} %bitcast.82), channel_id=1, source_target_pairs={{0,4},{1,5},{2,6},{3,7},{4,8},{5,9},{6,10},{7,11},{8,12},{9,13},{1... | collective-permute-start | bytes 393224 | tf_op jit(solution)/shard_map/ppermute | solution.py:645
  255.3 26.2 %collective-permute-start.21 = (f32[256,128]{1,0:T(8,128)}, f32[256,128]{1,0:T(8,128)S(1)}, u32[]{:S(2)}, u32[]{:S(2)}) collective-permute-start(f32[256,128]{1,0:T(8,128)} %bitcast.80), channel_id=1, source_target_pairs={{0,5},{1,6},{2,7},{3,8},{4,9},{5,10},{6,11},{7,12},{8,13},{9,14},{... | collective-permute-start | bytes 393224 | tf_op jit(solution)/shard_map/ppermute | solution.py:645
  257.8 54.4 %copy-start.4 = (f32[256,128]{1,0:T(8,128)}, f32[256,128]{1,0:T(8,128)S(1)}, u32[]{:S(2)}) copy-start(f32[256,128]{1,0:T(8,128)S(1)} %collective-permute-done.17.refs_1_) | copy-start | bytes 393220
  257.8 24.0 %collective-permute-start.22 = (f32[256,128]{1,0:T(8,128)}, f32[256,128]{1,0:T(8,128)S(1)}, u32[]{:S(2)}, u32[]{:S(2)}) collective-permute-start(f32[256,128]{1,0:T(8,128)} %bitcast.78), channel_id=1, source_target_pairs={{0,6},{1,7},{2,8},{3,9},{4,10},{5,11},{6,12},{7,13},{8,14},{9,15},... | collective-permute-start | bytes 393224 | tf_op jit(solution)/shard_map/ppermute | solution.py:645
  260.7 51.5 %copy-start.5 = (f32[256,128]{1,0:T(8,128)}, f32[256,128]{1,0:T(8,128)S(1)}, u32[]{:S(2)}) copy-start(f32[256,128]{1,0:T(8,128)S(1)} %collective-permute-done.18.refs_2_) | copy-start | bytes 393220
  260.7 23.1 %collective-permute-start.23 = (f32[256,128]{1,0:T(8,128)}, f32[256,128]{1,0:T(8,128)S(1)}, u32[]{:S(2)}, u32[]{:S(2)}) collective-permute-start(f32[256,128]{1,0:T(8,128)} %bitcast.76), channel_id=1, source_target_pairs={{0,7},{1,8},{2,9},{3,10},{4,11},{5,12},{6,13},{7,14},{8,15},{9,0},... | collective-permute-start | bytes 393224 | tf_op jit(solution)/shard_map/ppermute | solution.py:645
  260.7 51.5 %copy-start.6 = (f32[256,128]{1,0:T(8,128)}, f32[256,128]{1,0:T(8,128)S(1)}, u32[]{:S(2)}) copy-start(f32[256,128]{1,0:T(8,128)S(1)} %collective-permute-done.19.refs_3_) | copy-start | bytes 393220
  260.7 26.0 %collective-permute-start.24 = (f32[256,128]{1,0:T(8,128)}, f32[256,128]{1,0:T(8,128)S(1)}, u32[]{:S(2)}, u32[]{:S(2)}) collective-permute-start(f32[256,128]{1,0:T(8,128)} %bitcast.74), channel_id=1, source_target_pairs={{0,8},{1,9},{2,10},{3,11},{4,12},{5,13},{6,14},{7,15},{8,0},{9,1},... | collective-permute-start | bytes 393224 | tf_op jit(solution)/shard_map/ppermute | solution.py:645
  261.1 51.2 %copy-start.7 = (f32[256,128]{1,0:T(8,128)}, f32[256,128]{1,0:T(8,128)S(1)}, u32[]{:S(2)}) copy-start(f32[256,128]{1,0:T(8,128)S(1)} %collective-permute-done.20.refs_4_) | copy-start | bytes 393220
  261.1 31.0 %collective-permute-start.25 = (f32[256,128]{1,0:T(8,128)}, f32[256,128]{1,0:T(8,128)S(1)}, u32[]{:S(2)}, u32[]{:S(2)}) collective-permute-start(f32[256,128]{1,0:T(8,128)} %bitcast.72), channel_id=1, source_target_pairs={{0,9},{1,10},{2,11},{3,12},{4,13},{5,14},{6,15},{7,0},{8,1},{9,2},... | collective-permute-start | bytes 393224 | tf_op jit(solution)/shard_map/ppermute | solution.py:645
  281.6 30.7 %copy-start.8 = (f32[256,128]{1,0:T(8,128)}, f32[256,128]{1,0:T(8,128)S(1)}, u32[]{:S(2)}) copy-start(f32[256,128]{1,0:T(8,128)S(1)} %collective-permute-done.21.refs_5_) | copy-start | bytes 393220
  281.6 15.0 %collective-permute-start.26 = (f32[256,128]{1,0:T(8,128)}, f32[256,128]{1,0:T(8,128)S(1)}, u32[]{:S(2)}, u32[]{:S(2)}) collective-permute-start(f32[256,128]{1,0:T(8,128)} %bitcast.70), channel_id=1, source_target_pairs={{0,10},{1,11},{2,12},{3,13},{4,14},{5,15},{6,0},{7,1},{8,2},{9,3},... | collective-permute-start | bytes 393224 | tf_op jit(solution)/shard_map/ppermute | solution.py:645
  281.8 30.5 %copy-start.9 = (f32[256,128]{1,0:T(8,128)}, f32[256,128]{1,0:T(8,128)S(1)}, u32[]{:S(2)}) copy-start(f32[256,128]{1,0:T(8,128)S(1)} %collective-permute-done.22.refs_6_) | copy-start | bytes 393220
  281.8 30.4 %collective-permute-start.27 = (f32[256,128]{1,0:T(8,128)}, f32[256,128]{1,0:T(8,128)S(1)}, u32[]{:S(2)}, u32[]{:S(2)}) collective-permute-start(f32[256,128]{1,0:T(8,128)} %bitcast.66), channel_id=1, source_target_pairs={{0,11},{1,12},{2,13},{3,14},{4,15},{5,0},{6,1},{7,2},{8,3},{9,4},{... | collective-permute-start | bytes 393224 | tf_op jit(solution)/shard_map/ppermute | solution.py:645
  283.8 28.5 %copy-start.10 = (f32[256,128]{1,0:T(8,128)}, f32[256,128]{1,0:T(8,128)S(1)}, u32[]{:S(2)}) copy-start(f32[256,128]{1,0:T(8,128)S(1)} %collective-permute-done.23.refs_7_) | copy-start | bytes 393220
  283.8 28.4 %collective-permute-start.28 = (f32[256,128]{1,0:T(8,128)}, f32[256,128]{1,0:T(8,128)}, u32[]{:S(2)}, u32[]{:S(2)}) collective-permute-start(f32[256,128]{1,0:T(8,128)} %bitcast.64), channel_id=1, source_target_pairs={{0,12},{1,13},{2,14},{3,15},{4,0},{5,1},{6,2},{7,3},{8,4},{9,5},{1... | collective-permute-start | bytes 393224 | tf_op jit(solution)/shard_map/ppermute | solution.py:645
  286.8 25.5 %copy-start.11 = (f32[256,128]{1,0:T(8,128)}, f32[256,128]{1,0:T(8,128)S(1)}, u32[]{:S(2)}) copy-start(f32[256,128]{1,0:T(8,128)S(1)} %collective-permute-done.24.refs_8_) | copy-start | bytes 393220
  286.8 25.4 %collective-permute-start.29 = (f32[256,128]{1,0:T(8,128)}, f32[256,128]{1,0:T(8,128)}, u32[]{:S(2)}, u32[]{:S(2)}) collective-permute-start(f32[256,128]{1,0:T(8,128)} %bitcast.62), channel_id=1, source_target_pairs={{0,13},{1,14},{2,15},{3,0},{4,1},{5,2},{6,3},{7,4},{8,5},{9,6},{10... | collective-permute-start | bytes 393224 | tf_op jit(solution)/shard_map/ppermute | solution.py:645
  292.1 20.1 %collective-permute-start.30 = (f32[256,128]{1,0:T(8,128)}, f32[256,128]{1,0:T(8,128)}, u32[]{:S(2)}, u32[]{:S(2)}) collective-permute-start(f32[256,128]{1,0:T(8,128)} %bitcast.60), channel_id=1, source_target_pairs={{0,14},{1,15},{2,0},{3,1},{4,2},{5,3},{6,4},{7,5},{8,6},{9,7},{10,... | collective-permute-start | bytes 393224 | tf_op jit(solution)/shard_map/ppermute | solution.py:645
  296.6 15.6 %collective-permute-start.31 = (f32[256,128]{1,0:T(8,128)}, f32[256,128]{1,0:T(8,128)}, u32[]{:S(2)}, u32[]{:S(2)}) collective-permute-start(f32[256,128]{1,0:T(8,128)} %bitcast.59), channel_id=1, source_target_pairs={{0,15},{1,0},{2,1},{3,2},{4,3},{5,4},{6,5},{7,6},{8,7},{9,8},{10,9... | collective-permute-start | bytes 393224 | tf_op jit(solution)/shard_map/ppermute | solution.py:645
  (16 other events, 101.7 us)

commit v4 on v3

--- a/solution.py
+++ b/solution.py
@@ -17,6 +17,7 @@
 AXES = ("slab", "pair")
 PAD = 8
 BLOCK = 16
+WIDTH = 8
 PLANES = 2
 VMEM_BYTES = 60 * 1024 * 1024
 MOST_TURNS = 16
@@ -37,8 +38,17 @@
 
 
 def left_table(table):
-    high, low = split_table(table)
-    return np.concatenate([high, high, low], axis=1)
+    return np.concatenate(split_table(table), axis=1)
+
+
+def widen(table, wide):
+    depth = table.shape[1] // 2
+    wide[:, :depth] = table[:, :depth]
+    wide[:, depth:] = table[...]
+
+
+def wide_scratch(table):
+    return pltpu.VMEM((table.shape[0], table.shape[1] * 3 // 2), BF)
 
 
 def right_table(table):
@@ -271,159 +281,158 @@
     return jnp.where(at < count, at, at - count)
 
 
-def spectrum_kernel(depth, me, volume, table_y, table_x, take_cosine, take_sine, *rest):
+def spectrum_kernel(me, volume, table_y, table_x, take_cosine, take_sine, *rest):
+    wide, outs = rest[-1], rest[:-1] if len(rest) == 2 else rest[:-2]
     width, _, lanes = volume.shape
-    outs = rest if len(rest) == 1 else rest[:-1]
     slots = len(outs)
     rows = take_cosine.shape[0]
-    group = pl.program_id(0)
+
+    @pl.when(pl.program_id(0) == 0)
+    def _():
+        widen(table_x, wide)
+
     for start in range(0, width, 2):
         sides = [along_lanes(volume[start + k], table_y[...]) for k in range(2)]
         high, low = split(jnp.concatenate(sides, axis=1))
-        both = dot(table_x[...], jnp.concatenate([high, low, high], axis=0))
+        both = dot(wide[...], jnp.concatenate([high, low, high], axis=0))
         for k in range(2):
             part = both[:, k * lanes : (k + 1) * lanes]
             turned = pltpu.roll(part[rows:], lanes // 2, 1)
             value = take_cosine[...] * part[:rows] + take_sine[...] * turned
-            z = group * width + start + k
             if slots == 1:
-                outs[0][pl.ds(z, rows, stride=depth), :] = value
+                devices, _, each, _ = outs[0].shape
+                outs[0][:, start + k] = value.reshape(devices, each, lanes)
                 continue
-            held = rest[-1]
+            held = rest[-2]
             each = rows // slots
-            held[(start + k) % 2] = value
+            held[k] = value.reshape(slots, each, lanes)
             for slot in range(slots):
-                first = pl.multiple_of(turn(me[0], slot, slots) * each, each)
-                outs[slot][pl.ds(z, each, stride=depth), :] = held[(start + k) % 2, pl.ds(first, each), :]
-
-
-def cross_kernel(length_x, slots, start, me, damping, matches, *refs):
-    sources, refs = refs[:slots], refs[slots:]
-    table_f, table_i = refs[:2]
-    outs, refs = refs[2 : 2 + slots], refs[2 + slots :]
-    held, weight = refs[:2]
-    if slots == 1:
-        spectra, out = sources[0], outs[0]
-        slabs, submaps, _, depth, lanes = spectra.shape
-        piece = lambda i, s: spectra[i, s, 0]
-
-        def put(i, s, value):
-            out[i, s, 0] = value
-
-    else:
-        order = refs[2]
-        depth, lanes = sources[0].shape[1:]
-        submaps = weight.shape[0]
-        slabs = slots // submaps
-        for slot in range(slots):
-            order[turn(me[0], (slots - slot) % slots, slots)] = sources[slot][0]
-        piece = lambda i, s: order[i * submaps + s]
-
-        def put(i, s, value):
-            order[i * submaps + s] = value
-
+                outs[slot][start + k] = held[k, turn(me[0], slot, slots)]
+
+
+def cross_kernel(length_x, dims, start, me, damping, matches, *refs):
+    slabs, submaps, rows, depth, lanes = dims
+    slots = (len(refs) - 6) // 2 if len(refs) > 8 else 1
+    sources, (table_f, table_i) = refs[:slots], refs[slots : slots + 2]
+    outs, (held, weight, wide_f, wide_i) = refs[slots + 2 : 2 * slots + 2], refs[2 * slots + 2 : 2 * slots + 6]
+    each = depth * rows
+    source, out = (sources[0], outs[0]) if slots == 1 else (refs[-1], refs[-1])
     length_z = slabs * depth
     half = lanes // 2
     lane = lax.broadcasted_iota(jnp.int32, (length_z, lanes), 1)
     sign = jnp.where(lane < half, 1.0, -1.0)
     first = (lane == 0) | (lane == half)
-    row = start[0] + pl.program_id(0)
-    special = (row == 0) | (row == length_x // 2)
-    upper = row > length_x // 2
 
     def signed(count, length):
         return jnp.where(count < length // 2, count, count - length).astype(F32) / length
 
-    @pl.when(pl.program_id(0) == 0)
-    def _():
-        along = signed(lax.broadcasted_iota(jnp.int32, (length_z, lanes), 0), length_z)
-        for s in range(submaps):
-            weight[s] = jnp.exp(-damping[s] * (along * along))
-
-    at_x = signed(row, length_x)
-    lane_row = lax.broadcasted_iota(jnp.int32, (8, lanes), 1)
-    count_y = jnp.where(lane_row < half, lane_row, lane_row - half)
-    nyquist = ((lane_row == 0) & upper) | ((lane_row == half) & (special | upper))
-    at_y = jnp.where(nyquist, -0.5, signed(count_y, lanes))
-    radius = at_x * at_x + at_y * at_y
-
+    widen(table_f, wide_f)
+    widen(table_i, wide_i)
+    along = signed(lax.broadcasted_iota(jnp.int32, (length_z, lanes), 0), length_z)
     for s in range(submaps):
-        column = jnp.concatenate([piece(i, s) for i in range(slabs)], axis=0)
-        high, low = split(column)
-        both = dot(table_f[...], jnp.concatenate([high, low, high], axis=0))
-        cosine, sine = both[:length_z], both[length_z:]
-        value = cosine + sign * pltpu.roll(sine, half, 1)
-        square = value * value
-        held[0, s] = value
-        held[1, s] = square + pltpu.roll(square, half, 1)
-        held[2, s] = cosine
-        held[3, s] = sine
-
-    for s in range(submaps):
-        partner = matches[s]
-        own, far = held[0, s], held[0, partner]
-        damp = weight[s] * jnp.tile(jnp.exp(-damping[s] * radius), (length_z // 8, 1))
-        scale = damp * lax.rsqrt(held[1, s] * held[1, partner] + FLOOR_VALUE**2)
-        same = own * far
-        mixed = own * pltpu.roll(far, half, 1)
-        real = same + pltpu.roll(same, half, 1)
-        imag = mixed - pltpu.roll(mixed, half, 1)
-        imag = jnp.where(lane < half, -imag, imag)
-        x_here = jnp.where(lane < half, real, imag) * scale
-        x_turn = jnp.where(lane < half, -imag, real) * scale
-        held[4, s] = jnp.where(first & upper, x_turn, x_here)
-        held[5, s] = jnp.where(first & upper, -x_here, x_turn)
-
-        @pl.when(special)
-        def _():
-            own_r, own_i = held[2, s], -held[3, s]
-            far_r, far_i = held[2, partner], -held[3, partner]
-            size = (own_r * own_r + own_i * own_i) * (far_r * far_r + far_i * far_i)
-            scale = damp * lax.rsqrt(size + FLOOR_VALUE**2)
-            held[4, s] = jnp.where(first, (own_r * far_r + own_i * far_i) * scale, held[4, s])
-            held[5, s] = jnp.where(first, (own_r * far_i - own_i * far_r) * scale, held[5, s])
-
-        high, low = split(jnp.concatenate([held[4, s], held[5, s]], axis=0))
-        back = dot(table_i[...], jnp.concatenate([high, low, high], axis=0))
-        for i in range(slabs):
-            put(i, s, back[i * depth : (i + 1) * depth])
-
+        weight[s] = jnp.exp(-damping[s] * (along * along))
     if slots > 1:
         for slot in range(slots):
-            outs[slot][0] = order[turn(me[0], slot, slots)]
-
-
-def inverse_kernel(depth, rows, slots, added, me, *refs):
+            at = turn(me[0], (slots - slot) % slots, slots)
+            source[pl.ds(pl.multiple_of(at * each, each), each), :] = sources[slot][...]
+
+    def one_row(r, carry):
+        row = start[0] + r
+        special = (row == 0) | (row == length_x // 2)
+        upper = row > length_x // 2
+        at_x = signed(row, length_x)
+        lane_row = lax.broadcasted_iota(jnp.int32, (8, lanes), 1)
+        count_y = jnp.where(lane_row < half, lane_row, lane_row - half)
+        nyquist = ((lane_row == 0) & upper) | ((lane_row == half) & (special | upper))
+        at_y = jnp.where(nyquist, -0.5, signed(count_y, lanes))
+        radius = at_x * at_x + at_y * at_y
+
+        for s in range(submaps):
+            parts = [
+                source[pl.ds((i * submaps + s) * each + r, depth, stride=rows), :] for i in range(slabs)
+            ]
+            column = parts[0] if slabs == 1 else jnp.concatenate(parts, axis=0)
+            high, low = split(column)
+            both = dot(wide_f[...], jnp.concatenate([high, low, high], axis=0))
+            cosine, sine = both[:length_z], both[length_z:]
+            value = cosine + sign * pltpu.roll(sine, half, 1)
+            square = value * value
+            held[0, s] = value
+            held[1, s] = square + pltpu.roll(square, half, 1)
+            held[2, s] = cosine
+            held[3, s] = sine
+
+        for s in range(submaps):
+            partner = matches[s]
+            own, far = held[0, s], held[0, partner]
+            damp = weight[s] * jnp.tile(jnp.exp(-damping[s] * radius), (length_z // 8, 1))
+            scale = damp * lax.rsqrt(held[1, s] * held[1, partner] + FLOOR_VALUE**2)
+            same = own * far
+            mixed = own * pltpu.roll(far, half, 1)
+            real = same + pltpu.roll(same, half, 1)
+            imag = mixed - pltpu.roll(mixed, half, 1)
+            imag = jnp.where(lane < half, -imag, imag)
+            x_here = jnp.where(lane < half, real, imag) * scale
+            x_turn = jnp.where(lane < half, -imag, real) * scale
+            held[4, s] = jnp.where(first & upper, x_turn, x_here)
+            held[5, s] = jnp.where(first & upper, -x_here, x_turn)
+
+            @pl.when(special)
+            def _():
+                own_r, own_i = held[2, s], -held[3, s]
+                far_r, far_i = held[2, partner], -held[3, partner]
+                size = (own_r * own_r + own_i * own_i) * (far_r * far_r + far_i * far_i)
+                scale = damp * lax.rsqrt(size + FLOOR_VALUE**2)
+                held[4, s] = jnp.where(first, (own_r * far_r + own_i * far_i) * scale, held[4, s])
+                held[5, s] = jnp.where(first, (own_r * far_i - own_i * far_r) * scale, held[5, s])
+
+            high, low = split(jnp.concatenate([held[4, s], held[5, s]], axis=0))
+            back = dot(wide_i[...], jnp.concatenate([high, low, high], axis=0))
+            for i in range(slabs):
+                place = pl.ds((i * submaps + s) * each + r, depth, stride=rows)
+                out[place, :] = back[i * depth : (i + 1) * depth]
+        return carry
+
+    lax.fori_loop(0, rows, one_row, 0)
+    if slots > 1:
+        for slot in range(slots):
+            at = turn(me[0], slot, slots)
+            outs[slot][...] = out[pl.ds(pl.multiple_of(at * each, each), each), :]
+
+
+def inverse_kernel(rows, slots, added, me, *refs):
     columns, refs = refs[:slots], refs[slots:]
     weights, table_x, table_y = refs[:3]
     before = refs[3] if added else None
-    out = refs[3 + added]
-    each = rows // slots
+    out, wide = refs[3 + added], refs[4 + added]
+
+    @pl.when(pl.program_id(0) == 0)
+    def _():
+        widen(table_x, wide)
+
     width, _, lanes = out.shape
     half = lanes // 2
     lane = lax.broadcasted_iota(jnp.int32, (rows, lanes), 1)
     sign = jnp.where(lane < half, -1.0, 1.0)
-    group = pl.program_id(0)
-    sides = []
-    for k in range(width):
-        z = group * width + k
-        if slots == 1:
-            value = columns[0][pl.ds(z, rows, stride=depth), :]
-        else:
-            held = refs[-1]
-            for slot in range(slots):
-                first = pl.multiple_of(turn(me[0], (slots - slot) % slots, slots) * each, each)
-                held[k, pl.ds(first, each), :] = columns[slot][pl.ds(z, each, stride=depth), :]
-            value = held[k]
-        turned = pltpu.roll(value, half, 1) * sign
-        sides.append(jnp.concatenate([value * weights[...], turned * weights[...]], axis=0))
-    high, low = split(jnp.concatenate(sides, axis=1))
-    both = dot(table_x[...], jnp.concatenate([high, low, high], axis=0))
-    for k in range(width):
-        value = along_lanes(both[:, k * lanes : (k + 1) * lanes], table_y[...])
-        if before is not None:
-            value += before[k]
-        out[k] = value
+    for start in range(0, width, 2):
+        sides = []
+        for k in range(2):
+            if slots == 1:
+                value = columns[0][:, start + k].reshape(rows, lanes)
+            else:
+                held = refs[-1]
+                for slot in range(slots):
+                    held[k, turn(me[0], (slots - slot) % slots, slots)] = columns[slot][start + k]
+                value = held[k].reshape(rows, lanes)
+            turned = pltpu.roll(value, half, 1) * sign
+            sides.append(jnp.concatenate([value * weights[...], turned * weights[...]], axis=0))
+        high, low = split(jnp.concatenate(sides, axis=1))
+        both = dot(wide[...], jnp.concatenate([high, low, high], axis=0))
+        for k in range(2):
+            value = along_lanes(both[:, k * lanes : (k + 1) * lanes], table_y[...])
+            if before is not None:
+                value += before[start + k]
+            out[start + k] = value
 
 
 def params():
@@ -489,20 +498,27 @@
     )(conductance, edge, occ, cls, below, above, inner)
 
 
-def spectrum(volume, me, slots, tables):
+def spectrum(volume, me, devices, slots, tables):
     depth, length, lanes = volume.shape
     table_y, table_x, take_cosine, take_sine = tables
     rows = take_cosine.shape[0]
-    width = math.gcd(depth, 4)
+    each = rows // devices
+    width = math.gcd(depth, WIDTH)
     block = pl.BlockSpec((width, length, lanes), lambda g: (g, 0, 0))
-    out = jax.ShapeDtypeStruct((rows // slots * depth, lanes), F32)
+    if slots == 1:
+        out = jax.ShapeDtypeStruct((devices, depth, each, lanes), F32)
+        kept = pl.BlockSpec((devices, width, each, lanes), lambda g: (0, g, 0, 0))
+    else:
+        out = jax.ShapeDtypeStruct((depth, each, lanes), F32)
+        kept = pl.BlockSpec((width, each, lanes), lambda g: (g, 0, 0))
     return pl.pallas_call(
-        functools.partial(spectrum_kernel, depth),
+        spectrum_kernel,
         out_shape=[out] * slots,
         grid=(depth // width,),
         in_specs=[scalar_spec(), block] + [whole_spec()] * 4,
-        out_specs=[pl.BlockSpec(out.shape, lambda g: (0, 0))] * slots,
-        scratch_shapes=[pltpu.VMEM((2, rows, lanes), F32)] if slots > 1 else [],
+        out_specs=[kept] * slots,
+        scratch_shapes=([pltpu.VMEM((2, slots, each, lanes), F32)] if slots > 1 else [])
+        + [wide_scratch(table_x)],
         compiler_params=params(),
         cost_estimate=pl.CostEstimate(
             flops=6 * 2 * volume.size * (lanes + 2 * rows),
@@ -514,25 +530,23 @@
 
 
 def middle(sources, dims, start, me, damping, matches, length_x, tables):
-    slabs, submaps, rows, depth, lanes = dims
+    slabs, submaps, _, depth, lanes = dims
     length_z = slabs * depth
     slots = len(sources)
     size = math.prod(dims)
     scratch = [
         pltpu.VMEM((6, submaps, length_z, lanes), F32),
         pltpu.VMEM((submaps, length_z, lanes), F32),
+        wide_scratch(tables[0]),
+        wide_scratch(tables[1]),
     ]
-    if slots == 1:
-        block = pl.BlockSpec((slabs, submaps, 1, depth, lanes), lambda r: (0, 0, r, 0, 0))
-    else:
-        block = pl.BlockSpec((1, depth, lanes), lambda r: (r, 0, 0))
-        scratch.append(pltpu.VMEM((slots, depth, lanes), F32))
+    if slots > 1:
+        scratch.append(pltpu.VMEM((size // lanes, lanes), F32))
     return pl.pallas_call(
-        functools.partial(cross_kernel, length_x, slots),
+        functools.partial(cross_kernel, length_x, dims),
         out_shape=[jax.ShapeDtypeStruct(part.shape, F32) for part in sources],
-        grid=(rows,),
-        in_specs=[scalar_spec()] * 4 + [block] * slots + [whole_spec()] * 2,
-        out_specs=[block] * slots,
+        in_specs=[scalar_spec()] * 4 + [whole_spec()] * (slots + 2),
+        out_specs=[whole_spec()] * slots,
         scratch_shapes=scratch,
         compiler_params=params(),
         cost_estimate=pl.CostEstimate(
@@ -542,20 +556,26 @@
     )(start, me, damping, matches, *sources, *tables)
 
 
-def inverse(columns, me, before, depth, length, tables):
+def inverse(columns, me, before, length, tables):
     slots = len(columns)
-    lanes = columns[0].shape[1]
-    rows = slots * columns[0].shape[0] // depth
-    width = 2
+    depth, each, lanes = columns[0].shape[-3:]
+    weights = tables[0]
+    rows = weights.shape[0]
+    width = math.gcd(depth, WIDTH)
     block = pl.BlockSpec((width, length, lanes), lambda g: (g, 0, 0))
+    if slots == 1:
+        source = pl.BlockSpec((rows // each, width, each, lanes), lambda g: (0, g, 0, 0))
+    else:
+        source = pl.BlockSpec((width, each, lanes), lambda g: (g, 0, 0))
     extra = [] if before is None else [before]
     return pl.pallas_call(
-        functools.partial(inverse_kernel, depth, rows, slots, len(extra)),
+        functools.partial(inverse_kernel, rows, slots, len(extra)),
         out_shape=jax.ShapeDtypeStruct((depth, length, lanes), F32),
         grid=(depth // width,),
-        in_specs=[scalar_spec()] + [whole_spec()] * (slots + 3) + [block] * len(extra),
+        in_specs=[scalar_spec()] + [source] * slots + [whole_spec()] * 3 + [block] * len(extra),
         out_specs=block,
-        scratch_shapes=[pltpu.VMEM((width, rows, lanes), F32)] if slots > 1 else [],
+        scratch_shapes=[wide_scratch(tables[1])]
+        + ([pltpu.VMEM((2, slots, each, lanes), F32)] if slots > 1 else []),
         compiler_params=params(),
         cost_estimate=pl.CostEstimate(
             flops=6 * 2 * depth * length * lanes * rows,
@@ -637,8 +657,7 @@
 
     def exchange(parts):
         if len(parts) == 1:
-            part = parts[0].reshape(devices, rows, depth, lanes)
-            return [lax.all_to_all(part, AXES, 0, 0, tiled=True)]
+            return [lax.all_to_all(parts[0], AXES, 0, 0, tiled=True)]
         moved = [parts[0]]
         for slot in range(1, devices):
             pairs_of = [(i, (i + slot) % devices) for i in range(devices)]
@@ -651,31 +670,25 @@
         inside = slice(chunk * span, (chunk + 1) * span)
         table_x = left_table_stack(cos_x[inside], sin_x[inside])
         slots = devices if turns(chunk) else 1
-        parts = spectrum(
-            volume, me, slots, (table_y, table_x, take_cosine[inside], take_sine[inside])
-        )
+        tables = (table_y, table_x, take_cosine[inside], take_sine[inside])
+        parts = spectrum(volume, me, devices, slots, tables)
         parts = exchange(parts)
+        shapes, shape = [part.shape for part in parts], dims
+        if not straight:
+            parts = [parts[0].reshape(slabs, pairs, depth, rows, lanes).transpose(1, 0, 2, 3, 4)]
+            shape = (1, pairs, rows, length_z, lanes)
+        parts = [part.reshape(-1, lanes) for part in parts]
         start = chunk * span + me * rows
-        if slots > 1:
-            parts = [part.reshape(rows, depth, lanes) for part in parts]
-            parts = middle(parts, dims, start, me, damping, matches, length, middle_tables)
-            backs.append([part.reshape(rows * depth, lanes) for part in parts])
-            continue
-        part = parts[0].reshape(dims)
-        shape = dims
+        parts = middle(parts, shape, start, me, damping, matches, length, middle_tables)
         if not straight:
-            shape = (1, pairs, rows, length_z, lanes)
-            part = part.transpose(1, 2, 0, 3, 4).reshape(shape)
-        part = middle([part], shape, start, me, damping, matches, length, middle_tables)[0]
-        if not straight:
-            part = part.reshape(pairs, rows, slabs, depth, lanes).transpose(2, 0, 1, 3, 4)
-        backs.append([part])
+            parts = [parts[0].reshape(pairs, slabs, depth, rows, lanes).transpose(1, 0, 2, 3, 4)]
+        backs.append([part.reshape(like) for part, like in zip(parts, shapes)])
     result = None
     for chunk in range(chunks):
-        parts = [part.reshape(-1, lanes) for part in exchange(backs[chunk])]
+        parts = exchange(backs[chunk])
         inside = slice(chunk * span, (chunk + 1) * span)
         table = left_table(np.concatenate([cos_x[:, inside], sin_x[:, inside]], axis=1))
-        result = inverse(parts, me, result, depth, length, (weights[inside], table, table_back))
+        result = inverse(parts, me, result, length, (weights[inside], table, table_back))
     return result[None]
 
 

time: 330 us -> 318 us (0.964)
  the two profiles are of different devices: /device:TPU:0 before, /device:TPU:11 now
where the time goes in v4:
time: 318 us; the launch traced here: 312 us
  waiting for transfers between devices  151 us (47%)
  Pallas kernels  106 us (33%)
  starting transfers between devices  45.3 us (14%)
  local copies, waits for them, and re-layouts  7.04 us (2%)
    ppermute x30, waiting for transfers between devices, exchange(): moved.append(lax.ppermute(parts[slot], AXES, pairs_of))  103 us
    all_to_all x2, waiting for transfers between devices, exchange(): return [lax.all_to_all(parts[0], AXES, 0, 0, tiled=True)]  47.4 us
    pallas_call x2, Pallas kernels, middle(): pl.pallas_call(functools.partial(cross_kernel, length_x, dims), out_shape...  31.3 us
    ppermute x30, starting transfers between devices, exchange(): moved.append(lax.ppermute(parts[slot], AXES, pairs_of))  28.5 us
    pallas_call x1, Pallas kernels, diffuse_inner(): pl.pallas_call(functools.partial(inner_kernel, STEPS), out_shape=jax.Shap...  24 us
    pallas_call x2, Pallas kernels, inverse(): pl.pallas_call(functools.partial(inverse_kernel, rows, slots, len(extra))...  19.6 us
    pallas_call x1, Pallas kernels, diffuse_outer(): pl.pallas_call(functools.partial(outer_kernel, STEPS), out_shape=jax.Shap...  15.8 us
    pallas_call x2, Pallas kernels, spectrum(): pl.pallas_call(spectrum_kernel, out_shape=[out] * slots, grid=(depth // w...  15.1 us
  transfers between devices with their start and end apart: 34, of which 18 were waited for; matrix products, arithmetic and copies ran while one was open for 1% of the time, Pallas kernels for 18%

profile of v4, /device:TPU:11, one launch (start us, length us, event | category | flops | bytes accessed | tf_op | source)
XLA Modules:
  0.0 312.2 jit_solution(17785758242163257302)
XLA Ops:
  0.0 1.3 slice_bitcast_fusion
  1.3 1.3 convert_bitcast_fusion
  2.6 3.2 %collective-permute-start = (f32[8,256,128]{2,1,0:T(8,128)S(1)}, f32[8,256,128]{2,1,0:T(8,128)S(1)}, u32[]{:S(2)}, u32[]{:S(2)}) collective-permute-start(f32[8,256,128]{2,1,0:T(8,128)S(1)} %pad_maximum_fusion), channel_id=1, source_target_pairs={{0,4},{4,8},{8,12},{1,5},{5,9},{9,13},{2,6},{6,10},{10,14},{3,7},{... | collective-permute-start | bytes 3145736 | tf_op jit(solution)/shard_map/ppermute | solution.py:642
  5.9 1.1 pad_maximum_fusion.1
  7.0 2.1 collective-permute-start.1
  9.1 24.0 %inner.1._ = f32[32,256,128]{2,1,0:T(8,128)} custom-call(f32[8]{0:T(128)} %conductance.3, f32[32,256,128]{2,1,0:T(8,128)} %bitcast.48, s32[32,256,128]{2,1,0:T(8,128)} %bitcast.50), custom_call_target="tpu_custom_call" | custom-call | flops 83886080 | bytes 12582912 | tf_op jit(solution)/shard_map/inner/pallas_call | solution.py:462
  33.8 1.0 copy-done.2
  34.8 1.0 copy-done.3
  35.8 15.8 %outer.1.volume = f32[32,256,128]{2,1,0:T(8,128)} custom-call(f32[8]{0:T(128)} %conductance.3, s32[2]{0:T(128)} %add_convert_fusion.edge, f32[32,256,128]{2,1,0:T(8,128)} %bitcast.49, s32[32,256,128]{2,1,0:T(8,128)} %bitcast.51, f32[8,256,128]{2,1,0:T(8,128)} %copy-done.2, f32[8,256,128]{2,1,0:T(8,128)} %copy-done.3, ...), custom_call_target="tpu_custom_call", output_to_operand_aliasing={{}: (6, {})} | custom-call | flops 41943040 | bytes 6291456 | tf_op jit(solution)/shard_map/outer/pallas_call | solution.py:485
  51.6 7.4 %spectrum.3 = f32[16,32,8,128]{3,2,1,0:T(8,128)} custom-call(s32[1]{0:T(128)} %bitcast.me, f32[32,256,128]{2,1,0:T(8,128)} %outer.1.volume, bf16[256,256]{1,0:T(8,128)(2,1)} %constant.45.clone.table_y, bf16[256,512]{1,0:T(8,128)(2,1)} %constant.46.clone.table_x, f32[128,128]{1,0:T(8,128)} %constant.47.clone.take_cosine, f32[128,128]{1,0:T(8,128)} %constant.48.clone.take_sine), custom_call_target="tpu_custom_call" | custom-call | flops 4831838208 | bytes 6291456 | tf_op jit(solution)/shard_map/spectrum/pallas_call | solution.py:514
  59.0 6.7 %all-to-all-start = ((f32[16,32,8,128]{3,2,1,0:T(8,128)}), f32[16,32,8,128]{3,2,1,0:T(8,128)S(1)}, u32[]{:S(2)}, u32[]{:S(2)}) async-start(f32[16,32,8,128]{3,2,1,0:T(8,128)} %spectrum.3), calls=%async_computation | async-start | bytes 4194304 | tf_op jit(solution)/shard_map/all_to_all | solution.py:660
  65.6 47.4 %all-to-all-done = f32[16,32,8,128]{3,2,1,0:T(8,128)S(1)} async-done(((f32[16,32,8,128]{3,2,1,0:T(8,128)}), f32[16,32,8,128]{3,2,1,0:T(8,128)S(1)}, u32[]{:S(2)}, u32[]{:S(2)}) %all-to-all-start) | async-done | bytes 2097184 | tf_op jit(solution)/shard_map/all_to_all | solution.py:660
  113.1 1.3 copy-done.1
  114.4 15.5 %middle.3 = f32[4096,128]{1,0:T(8,128)} custom-call(s32[1]{0:T(128)S(6)} %mul.8.start, s32[1]{0:T(128)} %bitcast.me, f32[4]{0:T(128)} %damping.3, s32[4]{0:T(128)} %matches.3, f32[4096,128]{1,0:T(8,128)} %bitcast.53, bf16[256,256]{1,0:T(8,128)(2,1)} %constant.49.clone.refs_16_.refs_1_, bf16[128,512]{1,0:T(8,128)(2,1)} %constant.50.clone.refs_17_.refs_2_), custom_call_target="tpu_custom_call" | custom-call | flops 1610612736 | bytes 4194304 | tf_op jit(solution)/shard_map/middle/pallas_call | solution.py:545
  129.9 4.8 %all-to-all-start.1 = ((f32[16,32,8,128]{3,2,1,0:T(8,128)}), f32[16,32,8,128]{3,2,1,0:T(8,128)S(1)}, u32[]{:S(2)}, u32[]{:S(2)}) async-start(f32[16,32,8,128]{3,2,1,0:T(8,128)} %bitcast.52), calls=%async_computation.1 | async-start | bytes 4194304 | tf_op jit(solution)/shard_map/all_to_all | solution.py:660
  134.7 7.7 %spectrum.2 = (f32[32,8,128]{2,1,0:T(8,128)}, f32[32,8,128]{2,1,0:T(8,128)}, f32[32,8,128]{2,1,0:T(8,128)}, f32[32,8,128]{2,1,0:T(8,128)}, f32[32,8,128]{2,1,0:T...) custom-call(s32[1]{0:T(128)} %bitcast.me, ...), custom_call_target="tpu_custom_call" | custom-call | flops 4831838208 | bytes 6291456 | tf_op jit(solution)/shard_map/spectrum/pallas_call | solution.py:514
  142.4 1.5 collective-permute-start.2
  143.9 1.2 collective-permute-start.3
  146.3 2.9 collective-permute-start.6
  149.2 37.8 %collective-permute-done.2 = f32[32,8,128]{2,1,0:T(8,128)S(1)} collective-permute-done((f32[32,8,128]{2,1,0:T(8,128)}, f32[32,8,128]{2,1,0:T(8,128)S(1)}, u32[]{:S(2)}, u32[]{:S(2)}) %collective-permute-start.2) | collective-permute-done | bytes 131104 | tf_op jit(solution)/shard_map/ppermute | solution.py:664
  187.0 2.8 collective-permute-done.3
  189.8 2.8 collective-permute-done.4
  192.6 9.8 %collective-permute-done.5 = f32[32,8,128]{2,1,0:T(8,128)S(1)} collective-permute-done((f32[32,8,128]{2,1,0:T(8,128)}, f32[32,8,128]{2,1,0:T(8,128)S(1)}, u32[]{:S(2)}, u32[]{:S(2)}) %collective-permute-start.5) | collective-permute-done | bytes 131104 | tf_op jit(solution)/shard_map/ppermute | solution.py:664
  202.5 2.8 collective-permute-done.6
  205.3 9.8 %collective-permute-done.7 = f32[32,8,128]{2,1,0:T(8,128)S(1)} collective-permute-done((f32[32,8,128]{2,1,0:T(8,128)}, f32[32,8,128]{2,1,0:T(8,128)S(1)}, u32[]{:S(2)}, u32[]{:S(2)}) %collective-permute-start.7) | collective-permute-done | bytes 131104 | tf_op jit(solution)/shard_map/ppermute | solution.py:664
  215.1 2.8 collective-permute-done.8
  217.9 2.8 collective-permute-done.9
  220.7 3.1 collective-permute-start.15
  223.9 2.7 collective-permute-done.13
  226.5 0.9 collective-permute-done.14
  227.5 2.4 collective-permute-done.16
  230.6 15.8 %middle.2 = (f32[256,128]{1,0:T(8,128)}, f32[256,128]{1,0:T(8,128)}, f32[256,128]{1,0:T(8,128)}, f32[256,128]{1,0:T(8,128)}, f32[256,128]{1,0:T(8,128)}, /*index...) custom-call(s32[1]{0:T(128)S(6)} %add.7.start, ...), custom_call_target="tpu_custom_call" | custom-call | flops 1610612736 | bytes 4194304 | tf_op jit(solution)/shard_map/middle/pallas_call | solution.py:545
  246.4 3.3 %collective-permute-start.18 = (f32[32,8,128]{2,1,0:T(8,128)}, f32[32,8,128]{2,1,0:T(8,128)S(1)}, u32[]{:S(2)}, u32[]{:S(2)}) collective-permute-start(f32[32,8,128]{2,1,0:T(8,128)} %bitcast.82), channel_id=1, source_target_pairs={{0,2},{1,3},{2,4},{3,5},{4,6},{5,7},{6,8},{7,9},{8,10},{9,11},{10,... | collective-permute-start | bytes 393224 | tf_op jit(solution)/shard_map/ppermute | solution.py:664
  249.7 1.9 collective-permute-start.20
  251.6 0.9 collective-permute-start.21
  252.5 3.0 collective-permute-start.22
  256.2 1.8 collective-permute-start.24
  258.0 2.3 collective-permute-done.20.refs_4_
  260.3 1.4 collective-permute-done.21.refs_5_
  261.7 2.0 collective-permute-start.26
  263.7 14.9 %collective-permute-done.22.refs_6_ = f32[32,8,128]{2,1,0:T(8,128)S(1)} collective-permute-done((f32[32,8,128]{2,1,0:T(8,128)}, f32[32,8,128]{2,1,0:T(8,128)S(1)}, u32[]{:S(2)}, u32[]{:S(2)}) %collective-permute-start.22) | collective-permute-done | bytes 131104 | tf_op jit(solution)/shard_map/ppermute | solution.py:664
  278.6 2.8 collective-permute-start.27
  281.4 2.8 collective-permute-done.23.refs_7_
  284.2 4.2 %collective-permute-done.24.refs_8_ = f32[32,8,128]{2,1,0:T(8,128)S(1)} collective-permute-done((f32[32,8,128]{2,1,0:T(8,128)}, f32[32,8,128]{2,1,0:T(8,128)S(1)}, u32[]{:S(2)}, u32[]{:S(2)}) %collective-permute-start.24) | collective-permute-done | bytes 131104 | tf_op jit(solution)/shard_map/ppermute | solution.py:664
  288.4 1.7 collective-permute-start.30
  290.5 1.3 copy-done
  291.8 9.4 %inverse.2.refs_19_ = f32[32,256,128]{2,1,0:T(8,128)} custom-call(s32[1]{0:T(128)} %bitcast.me, f32[16,32,8,128]{3,2,1,0:T(8,128)} %copy-done, f32[128,128]{1,0:T(8,128)} %constant.54.clone.refs_1_, bf16[256,512]{1,0:T(8,128)(2,1)} %constant.55.clone.refs_2_, bf16[256,256]{1,0:T(8,128)(2,1)} %constant.56.clone.refs_3_.refs_18_), custom_call_target="tpu_custom_call" | custom-call | flops 1610612736 | bytes 6291456 | tf_op jit(solution)/shard_map/inverse/pallas_call | solution.py:571
  301.9 10.2 %inverse.3 = f32[32,256,128]{2,1,0:T(8,128)} custom-call(s32[1]{0:T(128)} %bitcast.me, f32[32,8,128]{2,1,0:T(8,128)} %bitcast.54, f32[32,8,128]{2,1,0:T(8,128)} %copy-done.4, f32[32,8,128]{2,1,0:T(8,128)} %copy-done.5, f32[32,8,128]{2,1,0:T(8,128)} %copy-done.6, f32[32,8,128]{2,1,0:T(8,128)} %copy-done.7, f32[32,8,128]{2,1,0:T(8,128)} %copy-done.8, ...), custom_call_target="tpu_custom_call" | custom-call | flops 1610612736 | bytes 10485760 | tf_op jit(solution)/shard_map/inverse/pallas_call | solution.py:571
  (93 shorter events, 4.2 us)
Async XLA Ops:
  2.6 31.2 %collective-permute-start = (f32[8,256,128]{2,1,0:T(8,128)S(1)}, f32[8,256,128]{2,1,0:T(8,128)S(1)}, u32[]{:S(2)}, u32[]{:S(2)}) collective-permute-start(f32[8,256,128]{2,1,0:T(8,128)S(1)} %pad_maximum_fusion), channel_id=1, source_target_pairs={{0,4},{4,8},{8,12},{1,5},{5,9},{9,13},{2,6},{6,10},{10,14},{3,7},{... | collective-permute-start | bytes 3145736 | tf_op jit(solution)/shard_map/ppermute | solution.py:642
  7.0 26.9 %collective-permute-start.1 = (f32[8,256,128]{2,1,0:T(8,128)}, f32[8,256,128]{2,1,0:T(8,128)S(1)}, u32[]{:S(2)}, u32[]{:S(2)}) collective-permute-start(f32[8,256,128]{2,1,0:T(8,128)} %pad_maximum_fusion.1), channel_id=1, source_target_pairs={{4,0},{8,4},{12,8},{5,1},{9,5},{13,9},{6,2},{10,6},{14,10},{7,3},{... | collective-permute-start | bytes 3145736 | tf_op jit(solution)/shard_map/ppermute | solution.py:643
  59.0 54.1 %all-to-all-start = ((f32[16,32,8,128]{3,2,1,0:T(8,128)}), f32[16,32,8,128]{3,2,1,0:T(8,128)S(1)}, u32[]{:S(2)}, u32[]{:S(2)}) async-start(f32[16,32,8,128]{3,2,1,0:T(8,128)} %spectrum.3), calls=%async_computation | async-start | bytes 4194304 | tf_op jit(solution)/shard_map/all_to_all | solution.py:660
  129.9 160.6 %all-to-all-start.1 = ((f32[16,32,8,128]{3,2,1,0:T(8,128)}), f32[16,32,8,128]{3,2,1,0:T(8,128)S(1)}, u32[]{:S(2)}, u32[]{:S(2)}) async-start(f32[16,32,8,128]{3,2,1,0:T(8,128)} %bitcast.52), calls=%async_computation.1 | async-start | bytes 4194304 | tf_op jit(solution)/shard_map/all_to_all | solution.py:660
  142.4 44.6 %collective-permute-start.2 = (f32[32,8,128]{2,1,0:T(8,128)}, f32[32,8,128]{2,1,0:T(8,128)S(1)}, u32[]{:S(2)}, u32[]{:S(2)}) collective-permute-start(f32[32,8,128]{2,1,0:T(8,128)} %get-tuple-element.38), channel_id=1, source_target_pairs={{0,1},{1,2},{2,3},{3,4},{4,5},{5,6},{6,7},{7,8},{8,9},{9,10},{10,1... | collective-permute-start | bytes 393224 | tf_op jit(solution)/shard_map/ppermute | solution.py:664
  143.9 45.9 %collective-permute-start.3 = (f32[32,8,128]{2,1,0:T(8,128)}, f32[32,8,128]{2,1,0:T(8,128)S(1)}, u32[]{:S(2)}, u32[]{:S(2)}) collective-permute-start(f32[32,8,128]{2,1,0:T(8,128)} %get-tuple-element.39), channel_id=1, source_target_pairs={{0,2},{1,3},{2,4},{3,5},{4,6},{5,7},{6,8},{7,9},{8,10},{9,11},{10,... | collective-permute-start | bytes 393224 | tf_op jit(solution)/shard_map/ppermute | solution.py:664
  145.1 47.5 %collective-permute-start.4 = (f32[32,8,128]{2,1,0:T(8,128)}, f32[32,8,128]{2,1,0:T(8,128)S(1)}, u32[]{:S(2)}, u32[]{:S(2)}) collective-permute-start(f32[32,8,128]{2,1,0:T(8,128)} %get-tuple-element.40), channel_id=1, source_target_pairs={{0,3},{1,4},{2,5},{3,6},{4,7},{5,8},{6,9},{7,10},{8,11},{9,12},{10... | collective-permute-start | bytes 393224 | tf_op jit(solution)/shard_map/ppermute | solution.py:664
  145.5 56.9 %collective-permute-start.5 = (f32[32,8,128]{2,1,0:T(8,128)}, f32[32,8,128]{2,1,0:T(8,128)S(1)}, u32[]{:S(2)}, u32[]{:S(2)}) collective-permute-start(f32[32,8,128]{2,1,0:T(8,128)} %get-tuple-element.41), channel_id=1, source_target_pairs={{0,4},{1,5},{2,6},{3,7},{4,8},{5,9},{6,10},{7,11},{8,12},{9,13},{1... | collective-permute-start | bytes 393224 | tf_op jit(solution)/shard_map/ppermute | solution.py:664
  146.3 59.0 %collective-permute-start.6 = (f32[32,8,128]{2,1,0:T(8,128)}, f32[32,8,128]{2,1,0:T(8,128)S(1)}, u32[]{:S(2)}, u32[]{:S(2)}) collective-permute-start(f32[32,8,128]{2,1,0:T(8,128)} %get-tuple-element.42), channel_id=1, source_target_pairs={{0,5},{1,6},{2,7},{3,8},{4,9},{5,10},{6,11},{7,12},{8,13},{9,14},{... | collective-permute-start | bytes 393224 | tf_op jit(solution)/shard_map/ppermute | solution.py:664
  187.0 42.9 %copy-start.15 = (f32[32,8,128]{2,1,0:T(8,128)}, f32[32,8,128]{2,1,0:T(8,128)S(1)}, u32[]{:S(2)}) copy-start(f32[32,8,128]{2,1,0:T(8,128)S(1)} %collective-permute-done.2) | copy-start | bytes 393220
  187.0 28.1 %collective-permute-start.7 = (f32[32,8,128]{2,1,0:T(8,128)}, f32[32,8,128]{2,1,0:T(8,128)S(1)}, u32[]{:S(2)}, u32[]{:S(2)}) collective-permute-start(f32[32,8,128]{2,1,0:T(8,128)} %get-tuple-element.43), channel_id=1, source_target_pairs={{0,6},{1,7},{2,8},{3,9},{4,10},{5,11},{6,12},{7,13},{8,14},{9,15},... | collective-permute-start | bytes 393224 | tf_op jit(solution)/shard_map/ppermute | solution.py:664
  189.8 40.1 %copy-start.16 = (f32[32,8,128]{2,1,0:T(8,128)}, f32[32,8,128]{2,1,0:T(8,128)S(1)}, u32[]{:S(2)}) copy-start(f32[32,8,128]{2,1,0:T(8,128)S(1)} %collective-permute-done.3) | copy-start | bytes 393220
  189.8 28.1 %collective-permute-start.8 = (f32[32,8,128]{2,1,0:T(8,128)}, f32[32,8,128]{2,1,0:T(8,128)S(1)}, u32[]{:S(2)}, u32[]{:S(2)}) collective-permute-start(f32[32,8,128]{2,1,0:T(8,128)} %get-tuple-element.44), channel_id=1, source_target_pairs={{0,7},{1,8},{2,9},{3,10},{4,11},{5,12},{6,13},{7,14},{8,15},{9,0},... | collective-permute-start | bytes 393224 | tf_op jit(solution)/shard_map/ppermute | solution.py:664
  192.6 37.3 %copy-start.17 = (f32[32,8,128]{2,1,0:T(8,128)}, f32[32,8,128]{2,1,0:T(8,128)S(1)}, u32[]{:S(2)}) copy-start(f32[32,8,128]{2,1,0:T(8,128)S(1)} %collective-permute-done.4) | copy-start | bytes 393220
  192.6 28.1 %collective-permute-start.9 = (f32[32,8,128]{2,1,0:T(8,128)}, f32[32,8,128]{2,1,0:T(8,128)S(1)}, u32[]{:S(2)}, u32[]{:S(2)}) collective-permute-start(f32[32,8,128]{2,1,0:T(8,128)} %get-tuple-element.45), channel_id=1, source_target_pairs={{0,8},{1,9},{2,10},{3,11},{4,12},{5,13},{6,14},{7,15},{8,0},{9,1},... | collective-permute-start | bytes 393224 | tf_op jit(solution)/shard_map/ppermute | solution.py:664
  202.5 27.5 %copy-start.18 = (f32[32,8,128]{2,1,0:T(8,128)}, f32[32,8,128]{2,1,0:T(8,128)S(1)}, u32[]{:S(2)}) copy-start(f32[32,8,128]{2,1,0:T(8,128)S(1)} %collective-permute-done.5) | copy-start | bytes 393220
  202.5 18.3 %collective-permute-start.10 = (f32[32,8,128]{2,1,0:T(8,128)}, f32[32,8,128]{2,1,0:T(8,128)S(1)}, u32[]{:S(2)}, u32[]{:S(2)}) collective-permute-start(f32[32,8,128]{2,1,0:T(8,128)} %get-tuple-element.46), channel_id=1, source_target_pairs={{0,9},{1,10},{2,11},{3,12},{4,13},{5,14},{6,15},{7,0},{8,1},{9,2},... | collective-permute-start | bytes 393224 | tf_op jit(solution)/shard_map/ppermute | solution.py:664
  205.3 24.7 %copy-start.19 = (f32[32,8,128]{2,1,0:T(8,128)}, f32[32,8,128]{2,1,0:T(8,128)S(1)}, u32[]{:S(2)}) copy-start(f32[32,8,128]{2,1,0:T(8,128)S(1)} %collective-permute-done.6) | copy-start | bytes 393220
  205.3 18.6 %collective-permute-start.11 = (f32[32,8,128]{2,1,0:T(8,128)}, f32[32,8,128]{2,1,0:T(8,128)S(1)}, u32[]{:S(2)}, u32[]{:S(2)}) collective-permute-start(f32[32,8,128]{2,1,0:T(8,128)} %get-tuple-element.47), channel_id=1, source_target_pairs={{0,10},{1,11},{2,12},{3,13},{4,14},{5,15},{6,0},{7,1},{8,2},{9,3},... | collective-permute-start | bytes 393224 | tf_op jit(solution)/shard_map/ppermute | solution.py:664
  215.1 14.9 %copy-start.20 = (f32[32,8,128]{2,1,0:T(8,128)}, f32[32,8,128]{2,1,0:T(8,128)S(1)}, u32[]{:S(2)}) copy-start(f32[32,8,128]{2,1,0:T(8,128)S(1)} %collective-permute-done.7) | copy-start | bytes 393220
  215.1 8.8 %collective-permute-start.12 = (f32[32,8,128]{2,1,0:T(8,128)}, f32[32,8,128]{2,1,0:T(8,128)S(1)}, u32[]{:S(2)}, u32[]{:S(2)}) collective-permute-start(f32[32,8,128]{2,1,0:T(8,128)} %get-tuple-element.48), channel_id=1, source_target_pairs={{0,11},{1,12},{2,13},{3,14},{4,15},{5,0},{6,1},{7,2},{8,3},{9,4},{... | collective-permute-start | bytes 393224 | tf_op jit(solution)/shard_map/ppermute | solution.py:664
  217.9 8.6 %collective-permute-start.13 = (f32[32,8,128]{2,1,0:T(8,128)}, f32[32,8,128]{2,1,0:T(8,128)S(1)}, u32[]{:S(2)}, u32[]{:S(2)}) collective-permute-start(f32[32,8,128]{2,1,0:T(8,128)} %get-tuple-element.49), channel_id=1, source_target_pairs={{0,12},{1,13},{2,14},{3,15},{4,0},{5,1},{6,2},{7,3},{8,4},{9,5},{1... | collective-permute-start | bytes 393224 | tf_op jit(solution)/shard_map/ppermute | solution.py:664
  220.7 6.7 %collective-permute-start.14 = (f32[32,8,128]{2,1,0:T(8,128)}, f32[32,8,128]{2,1,0:T(8,128)S(1)}, u32[]{:S(2)}, u32[]{:S(2)}) collective-permute-start(f32[32,8,128]{2,1,0:T(8,128)} %get-tuple-element.50), channel_id=1, source_target_pairs={{0,13},{1,14},{2,15},{3,0},{4,1},{5,2},{6,3},{7,4},{8,5},{9,6},{10... | collective-permute-start | bytes 393224 | tf_op jit(solution)/shard_map/ppermute | solution.py:664
  220.7 6.7 %collective-permute-start.15 = (f32[32,8,128]{2,1,0:T(8,128)}, f32[32,8,128]{2,1,0:T(8,128)S(1)}, u32[]{:S(2)}, u32[]{:S(2)}) collective-permute-start(f32[32,8,128]{2,1,0:T(8,128)} %get-tuple-element.51), channel_id=1, source_target_pairs={{0,14},{1,15},{2,0},{3,1},{4,2},{5,3},{6,4},{7,5},{8,6},{9,7},{10,... | collective-permute-start | bytes 393224 | tf_op jit(solution)/shard_map/ppermute | solution.py:664
  223.8 6.1 %collective-permute-start.16 = (f32[32,8,128]{2,1,0:T(8,128)}, f32[32,8,128]{2,1,0:T(8,128)S(1)}, u32[]{:S(2)}, u32[]{:S(2)}) collective-permute-start(f32[32,8,128]{2,1,0:T(8,128)} %get-tuple-element.52), channel_id=1, source_target_pairs={{0,15},{1,0},{2,1},{3,2},{4,3},{5,4},{6,5},{7,6},{8,7},{9,8},{10,9... | collective-permute-start | bytes 393224 | tf_op jit(solution)/shard_map/ppermute | solution.py:664
  246.3 6.2 %collective-permute-start.17 = (f32[32,8,128]{2,1,0:T(8,128)}, f32[32,8,128]{2,1,0:T(8,128)S(1)}, u32[]{:S(2)}, u32[]{:S(2)}) collective-permute-start(f32[32,8,128]{2,1,0:T(8,128)} %bitcast.84), channel_id=1, source_target_pairs={{0,1},{1,2},{2,3},{3,4},{4,5},{5,6},{6,7},{7,8},{8,9},{9,10},{10,1... | collective-permute-start | bytes 393224 | tf_op jit(solution)/shard_map/ppermute | solution.py:664
  246.4 9.1 %collective-permute-start.18 = (f32[32,8,128]{2,1,0:T(8,128)}, f32[32,8,128]{2,1,0:T(8,128)S(1)}, u32[]{:S(2)}, u32[]{:S(2)}) collective-permute-start(f32[32,8,128]{2,1,0:T(8,128)} %bitcast.82), channel_id=1, source_target_pairs={{0,2},{1,3},{2,4},{3,5},{4,6},{5,7},{6,8},{7,9},{8,10},{9,11},{10,... | collective-permute-start | bytes 393224 | tf_op jit(solution)/shard_map/ppermute | solution.py:664
  249.7 6.5 %collective-permute-start.19 = (f32[32,8,128]{2,1,0:T(8,128)}, f32[32,8,128]{2,1,0:T(8,128)S(1)}, u32[]{:S(2)}, u32[]{:S(2)}) collective-permute-start(f32[32,8,128]{2,1,0:T(8,128)} %bitcast.80), channel_id=1, source_target_pairs={{0,3},{1,4},{2,5},{3,6},{4,7},{5,8},{6,9},{7,10},{8,11},{9,12},{10... | collective-permute-start | bytes 393224 | tf_op jit(solution)/shard_map/ppermute | solution.py:664
  249.7 10.6 %collective-permute-start.20 = (f32[32,8,128]{2,1,0:T(8,128)}, f32[32,8,128]{2,1,0:T(8,128)S(1)}, u32[]{:S(2)}, u32[]{:S(2)}) collective-permute-start(f32[32,8,128]{2,1,0:T(8,128)} %bitcast.78), channel_id=1, source_target_pairs={{0,4},{1,5},{2,6},{3,7},{4,8},{5,9},{6,10},{7,11},{8,12},{9,13},{1... | collective-permute-start | bytes 393224 | tf_op jit(solution)/shard_map/ppermute | solution.py:664
  251.6 10.1 %collective-permute-start.21 = (f32[32,8,128]{2,1,0:T(8,128)}, f32[32,8,128]{2,1,0:T(8,128)S(1)}, u32[]{:S(2)}, u32[]{:S(2)}) collective-permute-start(f32[32,8,128]{2,1,0:T(8,128)} %bitcast.76), channel_id=1, source_target_pairs={{0,5},{1,6},{2,7},{3,8},{4,9},{5,10},{6,11},{7,12},{8,13},{9,14},{... | collective-permute-start | bytes 393224 | tf_op jit(solution)/shard_map/ppermute | solution.py:664
  252.5 48.8 %copy-start.4 = (f32[32,8,128]{2,1,0:T(8,128)}, f32[32,8,128]{2,1,0:T(8,128)S(1)}, u32[]{:S(2)}) copy-start(f32[32,8,128]{2,1,0:T(8,128)S(1)} %collective-permute-done.17.refs_1_) | copy-start | bytes 393220
  252.5 26.1 %collective-permute-start.22 = (f32[32,8,128]{2,1,0:T(8,128)}, f32[32,8,128]{2,1,0:T(8,128)S(1)}, u32[]{:S(2)}, u32[]{:S(2)}) collective-permute-start(f32[32,8,128]{2,1,0:T(8,128)} %bitcast.74), channel_id=1, source_target_pairs={{0,6},{1,7},{2,8},{3,9},{4,10},{5,11},{6,12},{7,13},{8,14},{9,15},... | collective-permute-start | bytes 393224 | tf_op jit(solution)/shard_map/ppermute | solution.py:664
  255.5 45.8 %copy-start.5 = (f32[32,8,128]{2,1,0:T(8,128)}, f32[32,8,128]{2,1,0:T(8,128)S(1)}, u32[]{:S(2)}) copy-start(f32[32,8,128]{2,1,0:T(8,128)S(1)} %collective-permute-done.18.refs_2_) | copy-start | bytes 393220
  255.5 28.7 %collective-permute-start.23 = (f32[32,8,128]{2,1,0:T(8,128)}, f32[32,8,128]{2,1,0:T(8,128)S(1)}, u32[]{:S(2)}, u32[]{:S(2)}) collective-permute-start(f32[32,8,128]{2,1,0:T(8,128)} %bitcast.72), channel_id=1, source_target_pairs={{0,7},{1,8},{2,9},{3,10},{4,11},{5,12},{6,13},{7,14},{8,15},{9,0},... | collective-permute-start | bytes 393224 | tf_op jit(solution)/shard_map/ppermute | solution.py:664
  256.2 45.1 %copy-start.6 = (f32[32,8,128]{2,1,0:T(8,128)}, f32[32,8,128]{2,1,0:T(8,128)S(1)}, u32[]{:S(2)}) copy-start(f32[32,8,128]{2,1,0:T(8,128)S(1)} %collective-permute-done.19.refs_3_) | copy-start | bytes 393220
  256.2 32.3 %collective-permute-start.24 = (f32[32,8,128]{2,1,0:T(8,128)}, f32[32,8,128]{2,1,0:T(8,128)S(1)}, u32[]{:S(2)}, u32[]{:S(2)}) collective-permute-start(f32[32,8,128]{2,1,0:T(8,128)} %bitcast.70), channel_id=1, source_target_pairs={{0,8},{1,9},{2,10},{3,11},{4,12},{5,13},{6,14},{7,15},{8,0},{9,1},... | collective-permute-start | bytes 393224 | tf_op jit(solution)/shard_map/ppermute | solution.py:664
  260.3 41.0 %copy-start.7 = (f32[32,8,128]{2,1,0:T(8,128)}, f32[32,8,128]{2,1,0:T(8,128)S(1)}, u32[]{:S(2)}) copy-start(f32[32,8,128]{2,1,0:T(8,128)S(1)} %collective-permute-done.20.refs_4_) | copy-start | bytes 393220
  260.3 28.2 %collective-permute-start.25 = (f32[32,8,128]{2,1,0:T(8,128)}, f32[32,8,128]{2,1,0:T(8,128)S(1)}, u32[]{:S(2)}, u32[]{:S(2)}) collective-permute-start(f32[32,8,128]{2,1,0:T(8,128)} %bitcast.68), channel_id=1, source_target_pairs={{0,9},{1,10},{2,11},{3,12},{4,13},{5,14},{6,15},{7,0},{8,1},{9,2},... | collective-permute-start | bytes 393224 | tf_op jit(solution)/shard_map/ppermute | solution.py:664
  261.7 39.6 %copy-start.8 = (f32[32,8,128]{2,1,0:T(8,128)}, f32[32,8,128]{2,1,0:T(8,128)S(1)}, u32[]{:S(2)}) copy-start(f32[32,8,128]{2,1,0:T(8,128)S(1)} %collective-permute-done.21.refs_5_) | copy-start | bytes 393220
  261.7 28.5 %collective-permute-start.26 = (f32[32,8,128]{2,1,0:T(8,128)}, f32[32,8,128]{2,1,0:T(8,128)S(1)}, u32[]{:S(2)}, u32[]{:S(2)}) collective-permute-start(f32[32,8,128]{2,1,0:T(8,128)} %bitcast.66), channel_id=1, source_target_pairs={{0,10},{1,11},{2,12},{3,13},{4,14},{5,15},{6,0},{7,1},{8,2},{9,3},... | collective-permute-start | bytes 393224 | tf_op jit(solution)/shard_map/ppermute | solution.py:664
  278.6 22.7 %copy-start.9 = (f32[32,8,128]{2,1,0:T(8,128)}, f32[32,8,128]{2,1,0:T(8,128)S(1)}, u32[]{:S(2)}) copy-start(f32[32,8,128]{2,1,0:T(8,128)S(1)} %collective-permute-done.22.refs_6_) | copy-start | bytes 393220
  278.6 22.6 %collective-permute-start.27 = (f32[32,8,128]{2,1,0:T(8,128)}, f32[32,8,128]{2,1,0:T(8,128)S(1)}, u32[]{:S(2)}, u32[]{:S(2)}) collective-permute-start(f32[32,8,128]{2,1,0:T(8,128)} %bitcast.62), channel_id=1, source_target_pairs={{0,11},{1,12},{2,13},{3,14},{4,15},{5,0},{6,1},{7,2},{8,3},{9,4},{... | collective-permute-start | bytes 393224 | tf_op jit(solution)/shard_map/ppermute | solution.py:664
  284.2 17.1 %copy-start.10 = (f32[32,8,128]{2,1,0:T(8,128)}, f32[32,8,128]{2,1,0:T(8,128)S(1)}, u32[]{:S(2)}) copy-start(f32[32,8,128]{2,1,0:T(8,128)S(1)} %collective-permute-done.23.refs_7_) | copy-start | bytes 393220
  284.2 17.0 %collective-permute-start.28 = (f32[32,8,128]{2,1,0:T(8,128)}, f32[32,8,128]{2,1,0:T(8,128)}, u32[]{:S(2)}, u32[]{:S(2)}) collective-permute-start(f32[32,8,128]{2,1,0:T(8,128)} %bitcast.60), channel_id=1, source_target_pairs={{0,12},{1,13},{2,14},{3,15},{4,0},{5,1},{6,2},{7,3},{8,4},{9,5},{1... | collective-permute-start | bytes 393224 | tf_op jit(solution)/shard_map/ppermute | solution.py:664
  288.4 12.8 %collective-permute-start.29 = (f32[32,8,128]{2,1,0:T(8,128)}, f32[32,8,128]{2,1,0:T(8,128)}, u32[]{:S(2)}, u32[]{:S(2)}) collective-permute-start(f32[32,8,128]{2,1,0:T(8,128)} %bitcast.58), channel_id=1, source_target_pairs={{0,13},{1,14},{2,15},{3,0},{4,1},{5,2},{6,3},{7,4},{8,5},{9,6},{10... | collective-permute-start | bytes 393224 | tf_op jit(solution)/shard_map/ppermute | solution.py:664
  288.4 12.9 %copy-start.12 = (f32[32,8,128]{2,1,0:T(8,128)}, f32[32,8,128]{2,1,0:T(8,128)S(1)}, u32[]{:S(2)}) copy-start(f32[32,8,128]{2,1,0:T(8,128)S(1)} %collective-permute-done.25.refs_9_) | copy-start | bytes 393220
  288.4 12.8 %collective-permute-start.30 = (f32[32,8,128]{2,1,0:T(8,128)}, f32[32,8,128]{2,1,0:T(8,128)}, u32[]{:S(2)}, u32[]{:S(2)}) collective-permute-start(f32[32,8,128]{2,1,0:T(8,128)} %bitcast.56), channel_id=1, source_target_pairs={{0,14},{1,15},{2,0},{3,1},{4,2},{5,3},{6,4},{7,5},{8,6},{9,7},{10,... | collective-permute-start | bytes 393224 | tf_op jit(solution)/shard_map/ppermute | solution.py:664
  290.2 11.1 %collective-permute-start.31 = (f32[32,8,128]{2,1,0:T(8,128)}, f32[32,8,128]{2,1,0:T(8,128)}, u32[]{:S(2)}, u32[]{:S(2)}) collective-permute-start(f32[32,8,128]{2,1,0:T(8,128)} %bitcast.55), channel_id=1, source_target_pairs={{0,15},{1,0},{2,1},{3,2},{4,3},{5,4},{6,5},{7,6},{8,7},{9,8},{10,9... | collective-permute-start | bytes 393224 | tf_op jit(solution)/shard_map/ppermute | solution.py:664
  (16 other events, 81.6 us)
